TPU v7x, 32 devices: a whole 2x2x4 slice. The times are simulated.
32 devices in a mesh: dp: 8 (over z, core), mp: 4 (over y, x).
Axes of the slice: x: 2, y: 2, z: 4, core: 2. Of those that a mesh axis runs over, the one named last changes fastest.
Arguments:
- tokens: bfloat16 [4, 4096, 768], P(None, ('dp', 'mp')), may hold values from -6 to 6
- first_values: bfloat16 [4, 4096, 384], P(None, ('dp', 'mp')), may hold values from -6 to 6
- out_cot: bfloat16 [4, 4096, 768], P(None, ('dp', 'mp')), may hold values from -6 to 6
- ln1_gain: bfloat16 [768], P(('dp', 'mp')), may hold values from 0.25 to 1.75
- ln1_bias: bfloat16 [768], P(('dp', 'mp')), may hold values from -3 to 3
- w_qkv: bfloat16 [768, 1920], P('dp', 'mp'), may hold values from -0.21875 to 0.21875
- q_bias: bfloat16 [768], P(('dp', 'mp')), may hold values from -3 to 3
- v_bias: bfloat16 [384], P(('dp', 'mp')), may hold values from -3 to 3
- w_out: bfloat16 [768, 768], P('dp', 'mp'), may hold values from -1.75 to 1.75
- out_bias: bfloat16 [768], P(('dp', 'mp')), may hold values from -3 to 3
- ln2_gain: bfloat16 [768], P(('dp', 'mp')), may hold values from 0.25 to 1.75
- ln2_bias: bfloat16 [768], P(('dp', 'mp')), may hold values from -3 to 3
- w_up: bfloat16 [768, 3072], P('dp', 'mp'), may hold values from -0.21875 to 0.21875
- up_bias: bfloat16 [3072], P(('dp', 'mp')), may hold values from -3 to 3
- w_down: bfloat16 [3072, 768], P('mp', 'dp'), may hold values from -0.109375 to 0.109375
- down_bias: bfloat16 [768], P(('dp', 'mp')), may hold values from -3 to 3
Outputs:
- layer_out: bfloat16 [4, 4096, 768], P(None, ('dp', 'mp'))
- input_grad: bfloat16 [4, 4096, 768], P(None, ('dp', 'mp'))
- first_grad: bfloat16 [4, 4096, 384], P(None, ('dp', 'mp'))
- ln1_gain_grad: float32 [768], P(('dp', 'mp'))
- ln1_bias_grad: float32 [768], P(('dp', 'mp'))
- qkv_grad: float32 [768, 1920], P('dp', 'mp')
- q_bias_grad: float32 [768], P(('dp', 'mp'))
- v_bias_grad: float32 [384], P(('dp', 'mp'))
- out_grad: float32 [768, 768], P('dp', 'mp')
- out_bias_grad: float32 [768], P(('dp', 'mp'))
- ln2_gain_grad: float32 [768], P(('dp', 'mp'))
- ln2_bias_grad: float32 [768], P(('dp', 'mp'))
- up_grad: float32 [768, 3072], P('dp', 'mp')
- up_bias_grad: float32 [3072], P(('dp', 'mp'))
- down_grad: float32 [3072, 768], P('mp', 'dp')
- down_bias_grad: float32 [768], P(('dp', 'mp'))
All inputs are finite; a program needn't handle non-finite values.
Results may differ from a plain program's by a relative error of at most 0.02.
Values may be sent and summed in bfloat16 or wider, within the bound.
A program may use at most 192 MiB of HBM per device.

v0:
```python
import jax
import jax.numpy as jnp
from jax import lax
from jax.sharding import PartitionSpec as P

D = 768
HEADS = 12
HEAD = 64
FF = 3072
MICRO = 4


EPS = 1e-05
BIG = 1e30
GELU_C = 0.7978845608028654
GELU_A = 0.044715


def layer_norm(inputs, gain_vec, shift_vec):
    average = jnp.mean(inputs, axis=-1, keepdims=True)
    centred = inputs - average
    variance = jnp.mean(centred * centred, axis=-1, keepdims=True)
    inv_std = lax.rsqrt(variance + EPS)
    scaled = centred * inv_std
    return (scaled * gain_vec + shift_vec, scaled, inv_std)


def norm_back(grad_out, scaled, inv_std, gain_vec):
    grad_scaled = grad_out * gain_vec
    first_term = jnp.mean(grad_scaled, axis=-1, keepdims=True)
    second_term = jnp.mean(grad_scaled * scaled, axis=-1, keepdims=True)
    grad_in = inv_std * (grad_scaled - first_term - scaled * second_term)
    return (grad_in, jnp.sum(grad_out * scaled, axis=0), jnp.sum(grad_out, axis=0))


def gelu_both(inputs):
    cubic_term = inputs + GELU_A * inputs * inputs * inputs
    tangent = jnp.tanh(GELU_C * cubic_term)
    gelu_out = 0.5 * inputs * (1.0 + tangent)
    gelu_slope = 0.5 * (1.0 + tangent) + 0.5 * inputs * (1.0 - tangent * tangent) * GELU_C * (
        1.0 + 3.0 * GELU_A * inputs * inputs
    )
    return (gelu_out, gelu_slope)


def split_heads(matrix):
    return matrix.reshape(matrix.shape[0], HEADS, HEAD)


def block_scores(query_heads, key_block, row_first, key_first):
    key_heads = split_heads(key_block)
    scores = jnp.einsum(
        "qhd,khd->hqk", query_heads, key_heads, preferred_element_type=jnp.float32
    ) * HEAD ** (-0.5)
    query_pos = row_first + jnp.arange(query_heads.shape[0], dtype=jnp.int32)
    key_pos = key_first + jnp.arange(key_block.shape[0], dtype=jnp.int32)
    allowed = key_pos[None, :] <= query_pos[:, None]
    return (jnp.where(allowed[None], scores, -BIG), allowed, key_heads)


def block_length():
    return 512


def fold_blocks(function, carried, key_block, value_block, key_first):
    row_count = key_block.shape[0]
    block_rows = block_length()
    if block_rows == row_count:
        return function(carried, key_block, value_block, key_first)
    key_parts = key_block.reshape(row_count // block_rows, block_rows, key_block.shape[1])
    value_parts = value_block.reshape(row_count // block_rows, block_rows, value_block.shape[1])
    offsets = key_first + jnp.arange(row_count // block_rows, dtype=jnp.int32) * block_rows

    def step_once(inner_state, element):
        return (function(inner_state, element[0], element[1], element[2]), None)

    result, ignored = lax.scan(step_once, carried, (key_parts, value_parts, offsets))
    return result


def map_blocks(function, key_block, value_block, key_first):
    row_count = key_block.shape[0]
    block_rows = block_length()
    if block_rows == row_count:
        return function(key_block, value_block, key_first)
    key_parts = key_block.reshape(row_count // block_rows, block_rows, key_block.shape[1])
    value_parts = value_block.reshape(row_count // block_rows, block_rows, value_block.shape[1])
    offsets = key_first + jnp.arange(row_count // block_rows, dtype=jnp.int32) * block_rows

    def apply_once(element):
        return function(element[0], element[1], element[2])

    outputs = lax.map(apply_once, (key_parts, value_parts, offsets))
    return outputs.reshape(row_count, outputs.shape[-1])


def attention_forward(queries, keys_low, values_low, row_first):
    query_heads = split_heads(queries)
    row_total = queries.shape[0]

    def online_step(fold_state, key_block, value_block, key_first):
        running_top, running_sum, running_acc = fold_state
        masked, allowed, ignored = block_scores(query_heads, key_block, row_first, key_first)
        new_top = jnp.maximum(running_top, jnp.max(masked, axis=-1))
        weights = jnp.exp(masked - new_top[:, :, None]) * allowed[None]
        shrink = jnp.exp(running_top - new_top)
        running_sum = running_sum * shrink + jnp.sum(weights, axis=-1)
        running_acc = running_acc * shrink[:, :, None] + jnp.einsum(
            "hqk,khd->hqd",
            weights.astype(jnp.bfloat16),
            split_heads(value_block),
            preferred_element_type=jnp.float32,
        )
        return (new_top, running_sum, running_acc)

    start_state = (
        jnp.full((HEADS, row_total), -BIG, jnp.float32),
        jnp.zeros((HEADS, row_total), jnp.float32),
        jnp.zeros((HEADS, row_total, HEAD), jnp.float32),
    )
    running_top, running_sum, running_acc = fold_blocks(
        online_step,
        start_state,
        lax.all_gather(keys_low, "mp", axis=0, tiled=True),
        lax.all_gather(values_low, "mp", axis=0, tiled=True),
        jnp.int32(0),
    )
    attended = (running_acc / running_sum[:, :, None]).transpose(1, 0, 2).reshape(row_total, D)
    return (attended, running_top + jnp.log(running_sum))


def attention_backward(queries, keys_low, values_low, grad_out, attended, log_total, row_first):
    query_heads = split_heads(queries)
    grad_heads = split_heads(grad_out)
    row_total = queries.shape[0]
    score_scale = HEAD ** (-0.5)
    row_delta = jnp.sum(grad_heads.astype(jnp.float32) * split_heads(attended), axis=-1).T
    keys_all, values_all = (
        lax.all_gather(keys_low, "mp", axis=0, tiled=True),
        lax.all_gather(values_low, "mp", axis=0, tiled=True),
    )

    def soft_grads(key_block, value_block, key_first):
        masked, allowed, key_heads = block_scores(query_heads, key_block, row_first, key_first)
        probabilities = jnp.exp(masked - log_total[:, :, None])
        grad_probs = jnp.einsum(
            "qhd,khd->hqk", grad_heads, split_heads(value_block), preferred_element_type=jnp.float32
        )
        grad_scores = (probabilities * (grad_probs - row_delta[:, :, None])).astype(jnp.bfloat16)
        return (probabilities, grad_scores, key_heads)

    def query_step(accum, key_block, value_block, key_first):
        probabilities, grad_scores, key_heads = soft_grads(key_block, value_block, key_first)
        return (
            accum
            + jnp.einsum("hqk,khd->qhd", grad_scores, key_heads, preferred_element_type=jnp.float32)
            * score_scale
        )

    grad_query = fold_blocks(
        query_step, jnp.zeros((row_total, HEADS, HEAD), jnp.float32), keys_all, values_all, 0
    )

    def key_step(key_block, value_block, key_first):
        probabilities, grad_scores, key_heads = soft_grads(key_block, value_block, key_first)
        grad_value = jnp.einsum(
            "hqk,qhd->khd",
            probabilities.astype(jnp.bfloat16),
            grad_heads,
            preferred_element_type=jnp.float32,
        )
        grad_key = (
            jnp.einsum("hqk,qhd->khd", grad_scores, query_heads, preferred_element_type=jnp.float32)
            * score_scale
        )
        return jnp.concatenate(
            [grad_key.reshape(key_block.shape[0], D), grad_value.reshape(key_block.shape[0], D)],
            axis=1,
        )

    key_block = keys_all
    value_block = values_all
    grad_kv = lax.psum_scatter(
        map_blocks(key_step, key_block, value_block, jnp.int32(0)).astype(jnp.bfloat16),
        "mp",
        scatter_dimension=0,
        tiled=True,
    ).astype(jnp.float32)
    return (grad_query.reshape(row_total, D), grad_kv)


def reduce_grads(local_grads):
    row_parts = (
        lax.psum_scatter(
            local_grads[0].astype(jnp.bfloat16), "dp", scatter_dimension=0, tiled=True
        ).astype(jnp.float32),
        lax.psum_scatter(
            local_grads[1].astype(jnp.bfloat16), "dp", scatter_dimension=0, tiled=True
        ).astype(jnp.float32),
        lax.psum_scatter(
            local_grads[2].astype(jnp.bfloat16), "dp", scatter_dimension=0, tiled=True
        ).astype(jnp.float32),
        lax.psum_scatter(
            local_grads[3].astype(jnp.bfloat16), "dp", scatter_dimension=0, tiled=True
        ).astype(jnp.float32),
        lax.psum_scatter(
            local_grads[4].astype(jnp.bfloat16), "dp", scatter_dimension=0, tiled=True
        ).astype(jnp.float32),
        lax.psum_scatter(
            local_grads[5].astype(jnp.bfloat16), "dp", scatter_dimension=0, tiled=True
        ).astype(jnp.float32),
        lax.psum_scatter(
            local_grads[6].astype(jnp.bfloat16), "dp", scatter_dimension=0, tiled=True
        ).astype(jnp.float32),
        lax.psum_scatter(
            local_grads[7].astype(jnp.bfloat16), "dp", scatter_dimension=0, tiled=True
        ).astype(jnp.float32),
        lax.psum_scatter(
            local_grads[8].astype(jnp.bfloat16), "dp", scatter_dimension=0, tiled=True
        ).astype(jnp.float32),
        lax.psum_scatter(
            local_grads[9].astype(jnp.bfloat16), "dp", scatter_dimension=0, tiled=True
        ).astype(jnp.float32),
        lax.psum_scatter(
            local_grads[10].astype(jnp.bfloat16), "dp", scatter_dimension=0, tiled=True
        ).astype(jnp.float32),
        lax.psum_scatter(
            local_grads[11].astype(jnp.bfloat16), "dp", scatter_dimension=1, tiled=True
        ).astype(jnp.float32),
        lax.psum_scatter(
            local_grads[12].astype(jnp.bfloat16), "dp", scatter_dimension=0, tiled=True
        ).astype(jnp.float32),
    )
    row_parts = tuple(row_parts)
    col_parts = tuple(
        (
            lax.psum_scatter(
                row_parts[0].astype(jnp.bfloat16), "mp", scatter_dimension=0, tiled=True
            ).astype(jnp.float32),
            lax.psum_scatter(
                row_parts[1].astype(jnp.bfloat16), "mp", scatter_dimension=0, tiled=True
            ).astype(jnp.float32),
            lax.psum_scatter(
                row_parts[2].astype(jnp.bfloat16), "mp", scatter_dimension=1, tiled=True
            ).astype(jnp.float32),
            lax.psum_scatter(
                row_parts[3].astype(jnp.bfloat16), "mp", scatter_dimension=0, tiled=True
            ).astype(jnp.float32),
            lax.psum_scatter(
                row_parts[4].astype(jnp.bfloat16), "mp", scatter_dimension=0, tiled=True
            ).astype(jnp.float32),
            lax.psum_scatter(
                row_parts[5].astype(jnp.bfloat16), "mp", scatter_dimension=1, tiled=True
            ).astype(jnp.float32),
            lax.psum_scatter(
                row_parts[6].astype(jnp.bfloat16), "mp", scatter_dimension=0, tiled=True
            ).astype(jnp.float32),
            lax.psum_scatter(
                row_parts[7].astype(jnp.bfloat16), "mp", scatter_dimension=0, tiled=True
            ).astype(jnp.float32),
            lax.psum_scatter(
                row_parts[8].astype(jnp.bfloat16), "mp", scatter_dimension=0, tiled=True
            ).astype(jnp.float32),
            lax.psum_scatter(
                row_parts[10].astype(jnp.bfloat16), "mp", scatter_dimension=0, tiled=True
            ).astype(jnp.float32),
            lax.psum_scatter(
                row_parts[12].astype(jnp.bfloat16), "mp", scatter_dimension=0, tiled=True
            ).astype(jnp.float32),
        )
    )
    return col_parts[:9] + (row_parts[9], col_parts[9], row_parts[11], col_parts[10])


def shards(
    tokens,
    first_values,
    out_cot,
    ln1_gain,
    ln1_bias,
    w_qkv,
    q_bias,
    v_bias,
    w_out,
    out_bias,
    ln2_gain,
    ln2_bias,
    w_up,
    up_bias,
    w_down,
    down_bias,
):
    near_blocks = tuple(
        (
            lax.all_gather(ln1_gain, "mp", axis=0, tiled=True),
            lax.all_gather(ln1_bias, "mp", axis=0, tiled=True),
            lax.all_gather(w_qkv, "mp", axis=1, tiled=True),
            lax.all_gather(q_bias, "mp", axis=0, tiled=True),
            lax.all_gather(v_bias, "mp", axis=0, tiled=True),
            lax.all_gather(w_out, "mp", axis=1, tiled=True),
            lax.all_gather(out_bias, "mp", axis=0, tiled=True),
            lax.all_gather(ln2_gain, "mp", axis=0, tiled=True),
            lax.all_gather(ln2_bias, "mp", axis=0, tiled=True),
            lax.all_gather(up_bias, "mp", axis=0, tiled=True),
            lax.all_gather(down_bias, "mp", axis=0, tiled=True),
        )
    )
    near_blocks = near_blocks[:9] + (w_up, near_blocks[9], w_down, near_blocks[10])
    params = tuple(
        (
            lax.all_gather(near_blocks[0], "dp", axis=0, tiled=True),
            lax.all_gather(near_blocks[1], "dp", axis=0, tiled=True),
            lax.all_gather(near_blocks[2], "dp", axis=0, tiled=True),
            lax.all_gather(near_blocks[3], "dp", axis=0, tiled=True),
            lax.all_gather(near_blocks[4], "dp", axis=0, tiled=True),
            lax.all_gather(near_blocks[5], "dp", axis=0, tiled=True),
            lax.all_gather(near_blocks[6], "dp", axis=0, tiled=True),
            lax.all_gather(near_blocks[7], "dp", axis=0, tiled=True),
            lax.all_gather(near_blocks[8], "dp", axis=0, tiled=True),
            lax.all_gather(near_blocks[9], "dp", axis=0, tiled=True),
            lax.all_gather(near_blocks[10], "dp", axis=0, tiled=True),
            lax.all_gather(near_blocks[11], "dp", axis=1, tiled=True),
            lax.all_gather(near_blocks[12], "dp", axis=0, tiled=True),
        )
    )
    gain_one = params[0].astype(jnp.float32)
    shift_one = params[1].astype(jnp.float32)
    qkv_full = params[2]
    query_shift = params[3].astype(jnp.float32)
    value_shift = params[4].astype(jnp.float32)
    out_full = params[5]
    out_shift = params[6].astype(jnp.float32)
    gain_two = params[7].astype(jnp.float32)
    shift_two = params[8].astype(jnp.float32)
    up_full = params[9]
    up_shift_all = params[10].astype(jnp.float32)
    down_full = params[11]
    down_shift = params[12].astype(jnp.float32)
    up_cols = up_full.shape[1]
    up_start = 0
    up_start = lax.axis_index("mp") * up_cols
    up_used = lax.dynamic_slice_in_dim(up_shift_all, up_start, up_cols, 0)
    row_total = tokens.shape[1]
    row_first = lax.axis_index("mp") * row_total
    fresh_cols = value_shift.shape[0]
    outputs = []
    grad_inputs = []
    grad_firsts = []
    summed = None
    for micro_index in range(MICRO):
        cot_low = out_cot[micro_index]
        inputs = tokens[micro_index].astype(jnp.float32)
        normed, scaled_one, inv_one = layer_norm(inputs, gain_one, shift_one)
        normed_low = normed.astype(jnp.bfloat16)
        mixed_proj = jnp.dot(normed_low, qkv_full, preferred_element_type=jnp.float32)
        queries = (mixed_proj[:, :D] + query_shift).astype(jnp.bfloat16)
        keys_low = mixed_proj[:, D : 2 * D].astype(jnp.bfloat16)
        values_low = jnp.concatenate(
            [
                (mixed_proj[:, 2 * D :] + value_shift).astype(jnp.bfloat16),
                first_values[micro_index],
            ],
            axis=1,
        )
        attended, log_total = attention_forward(queries, keys_low, values_low, row_first)
        attended_low = attended.astype(jnp.bfloat16)
        middle = inputs + (
            jnp.dot(attended_low, out_full, preferred_element_type=jnp.float32) + out_shift
        )
        normed_two, scaled_two, inv_two = layer_norm(middle, gain_two, shift_two)
        normed_two_low = normed_two.astype(jnp.bfloat16)
        cot_float = cot_low.astype(jnp.float32)
        row_piece = lax.all_gather(normed_two_low, "mp", axis=0, tiled=True)
        hidden = jnp.dot(row_piece, up_full, preferred_element_type=jnp.float32) + up_used
        gelu_out, gelu_slope = gelu_both(hidden)
        active_all = gelu_out.astype(jnp.bfloat16)
        down_part = lax.psum_scatter(
            jnp.dot(active_all, down_full, preferred_element_type=jnp.float32).astype(jnp.bfloat16),
            "mp",
            scatter_dimension=0,
            tiled=True,
        ).astype(jnp.float32)
        result = middle + (down_part + down_shift)
        back_row_piece = lax.all_gather(cot_low, "mp", axis=0, tiled=True)
        grad_active = jnp.einsum(
            "rd,fd->rf", back_row_piece, down_full, preferred_element_type=jnp.float32
        )
        back_gelu_out, back_gelu_slope = gelu_both(hidden)
        grad_hidden = (grad_active * back_gelu_slope).astype(jnp.bfloat16)
        grad_normed_two = lax.psum_scatter(
            jnp.einsum(
                "rf,df->rd", grad_hidden, up_full, preferred_element_type=jnp.float32
            ).astype(jnp.bfloat16),
            "mp",
            scatter_dimension=0,
            tiled=True,
        ).astype(jnp.float32)
        grad_down = jnp.einsum(
            "rf,rd->fd", active_all, back_row_piece, preferred_element_type=jnp.float32
        )
        grad_up = jnp.einsum(
            "rd,rf->df", row_piece, grad_hidden, preferred_element_type=jnp.float32
        )
        up_piece = jnp.sum(grad_hidden.astype(jnp.float32), axis=0)
        grad_up_shift = lax.dynamic_update_slice_in_dim(
            jnp.zeros((FF,), jnp.float32), up_piece, up_start, 0
        )
        grad_norm_two, grad_gain_two, grad_shift_two = norm_back(
            grad_normed_two, scaled_two, inv_two, gain_two
        )
        grad_middle = cot_float + grad_norm_two
        grad_branch = grad_middle.astype(jnp.bfloat16)
        grad_out_shift = jnp.sum(grad_branch.astype(jnp.float32), axis=0)
        grad_out_proj = jnp.einsum(
            "rd,re->de", attended_low, grad_branch, preferred_element_type=jnp.float32
        )
        grad_attended = jnp.einsum(
            "re,de->rd", grad_branch, out_full, preferred_element_type=jnp.float32
        ).astype(jnp.bfloat16)
        grad_query, grad_kv = attention_backward(
            queries, keys_low, values_low, grad_attended, attended, log_total, row_first
        )
        grad_query_low = grad_query.astype(jnp.bfloat16)
        grad_kv_low = grad_kv.astype(jnp.bfloat16)
        grad_mixed = jnp.concatenate([grad_query_low, grad_kv_low[:, : D + fresh_cols]], axis=1)
        grad_query_shift = jnp.sum(grad_query_low.astype(jnp.float32), axis=0)
        grad_value_shift = jnp.sum(grad_kv_low[:, D : D + fresh_cols].astype(jnp.float32), axis=0)
        grad_qkv = jnp.einsum(
            "rd,rc->dc", normed_low, grad_mixed, preferred_element_type=jnp.float32
        )
        grad_normed = jnp.einsum(
            "rc,dc->rd", grad_mixed, qkv_full, preferred_element_type=jnp.float32
        )
        grad_norm_one, grad_gain_one, grad_shift_one = norm_back(
            grad_normed, scaled_one, inv_one, gain_one
        )
        grad_input = grad_middle + grad_norm_one
        local_grads = (
            grad_gain_one,
            grad_shift_one,
            grad_qkv,
            grad_query_shift,
            grad_value_shift,
            grad_out_proj,
            grad_out_shift,
            grad_gain_two,
            grad_shift_two,
            grad_up,
            grad_up_shift,
            grad_down,
            jnp.sum(cot_float, axis=0),
        )
        result, grad_input, grad_first, local_grads = (
            result.astype(jnp.bfloat16),
            grad_input.astype(jnp.bfloat16),
            grad_kv_low[:, D + fresh_cols :],
            local_grads,
        )
        outputs.append(result)
        grad_inputs.append(grad_input)
        grad_firsts.append(grad_first)
        local_grads = reduce_grads(local_grads)
        summed = local_grads if summed is None else jax.tree.map(jnp.add, summed, local_grads)
    return (
        jnp.stack(outputs),
        jnp.stack(grad_inputs),
        jnp.stack(grad_firsts),
        summed[0],
        summed[1],
        summed[2],
        summed[3],
        summed[4],
        summed[5],
        summed[6],
        summed[7],
        summed[8],
        summed[9],
        summed[10],
        summed[11],
        summed[12],
    )


def solution(mesh):
    placed = (
        P(None, ("dp", "mp"), None),
        P(None, ("dp", "mp"), None),
        P(None, ("dp", "mp"), None),
        P(("dp", "mp")),
        P(("dp", "mp")),
        P("dp", "mp"),
        P(("dp", "mp")),
        P(("dp", "mp")),
        P("dp", "mp"),
        P(("dp", "mp")),
        P(("dp", "mp")),
        P(("dp", "mp")),
        P("dp", "mp"),
        P(("dp", "mp")),
        P("mp", "dp"),
        P(("dp", "mp")),
    )
    return jax.shard_map(
        shards,
        mesh=mesh,
        in_specs=placed,
        out_specs=(
            P(None, ("dp", "mp"), None),
            P(None, ("dp", "mp"), None),
            P(None, ("dp", "mp"), None),
            P(("dp", "mp")),
            P(("dp", "mp")),
            P("dp", "mp"),
            P(("dp", "mp")),
            P(("dp", "mp")),
            P("dp", "mp"),
            P(("dp", "mp")),
            P(("dp", "mp")),
            P(("dp", "mp")),
            P("dp", "mp"),
            P(("dp", "mp")),
            P("mp", "dp"),
            P(("dp", "mp")),
        ),
        check_vma=False,
    )
```

profile of v0, /device:TPU:1, one launch (start us, length us, event | category | flops | bytes accessed | tf_op | source)
XLA Modules:
  0.0 1544.9 jit_solution(5951854874780158373)
XLA Ops:
  7.2 9.2 all-gather.4
  42.2 28.1 %all-reduce.90 = (bf16[768]{0:T(1024)(128)(2,1)S(1)}, bf16[768]{0:T(1024)(128)(2,1)S(1)}, bf16[384]{0:T(512)(128)(2,1)S(1)}, bf16[768]{0:T(1024)(128)(2,1)S(1)},...) all-reduce(bf16[768]{0:T(1024)(128)(2,1)S(1)} %dynamic-update-slice, ...), channel_id=1, replica_groups=mesh['dp'=8,'mp'=4] {'dp'}, use_global_device_ids=true, to_apply=%add.3 | all-reduce | flops 4992 | bytes 19968
  71.2 16.7 %all-gather.5 = bf16[8,1,384]{2,1,0:T(2,128)(2,1)S(1)} all-gather(bf16[1,1,384]{2,1,0:T(2,128)(2,1)S(1)} %reshape.532), channel_id=1, replica_groups=mesh['dp'=8,'mp'=4] {'dp'}, dimensions={0}, use_global_device_ids=true | all-gather | bytes 6912 | tf_op jit(solution)/shard_map/all_gather | solution.py:321
  90.3 11.0 all-gather.2
  105.5 9.0 all_gather.158
  115.9 9.8 all_gather.159
  134.2 9.4 all_gather.160
  153.9 30.0 %reduce-scatter.69.cloned.1.call-done = bf16[128,768]{1,0:T(8,128)(2,1)} async-done(((bf16[512,768]{1,0:T(8,128)(2,1)}), bf16[128,768]{1,0:T(8,128)(2,1)}) %reduce-scatter.69.cloned.1.call-update) | async-done | bytes 196624 | tf_op jit(solution)/shard_map/reduce_scatter | solution.py:390
  196.7 15.9 %all-gather = bf16[1,512,768]{2,1,0:T(8,128)(2,1)} all-gather(bf16[1,128,768]{2,1,0:T(8,128)(2,1)S(1)} %copy-done.83), channel_id=2, replica_groups=mesh['dp'=8,'mp'=4] {'mp'}, dimensions={1}, use_global_device_ids=true | all-gather | bytes 983040 | tf_op jit(solution)/shard_map/all_gather | solution.py:384
  217.6 13.4 reduce-scatter.71.cloned.1.call-done
  240.3 9.9 all_gather.161
  252.5 10.2 all_gather.136
  269.7 11.2 all_gather.155
  295.1 9.6 all_gather.139
  308.0 9.1 all_gather.162
  320.4 10.6 all_gather.156
  360.7 9.9 all-gather.3
  386.2 10.1 all-gather.1
  396.4 10.6 all_gather.157
  416.4 21.8 %reduce-scatter.73.cloned.1.call-done = bf16[128,768]{1,0:T(8,128)(2,1)} async-done(((bf16[512,768]{1,0:T(8,128)(2,1)}), bf16[128,768]{1,0:T(8,128)(2,1)}) %reduce-scatter.73.cloned.1.call-update) | async-done | bytes 196624 | tf_op jit(solution)/shard_map/reduce_scatter | solution.py:390
  438.2 31.6 %reduce-scatter.65.cloned.1.call-done = bf16[128,768]{1,0:T(8,128)(2,1)} async-done(((bf16[512,768]{1,0:T(8,128)(2,1)}), bf16[128,768]{1,0:T(8,128)(2,1)}) %reduce-scatter.65.cloned.1.call-update) | async-done | bytes 196624 | tf_op jit(solution)/shard_map/reduce_scatter | solution.py:390
  584.0 17.1 %reduce-scatter.87.cloned.1.call-done = bf16[96,768]{1,0:T(8,128)(2,1)} async-done(((bf16[768,768]{1,0:T(8,128)(2,1)}), bf16[96,768]{1,0:T(8,128)(2,1)}) %reduce-scatter.87.cloned.1.call-update) | async-done | bytes 147472 | tf_op jit(solution)/shard_map/reduce_scatter | solution.py:209
  611.6 24.8 %reduce-scatter.63.cloned.1.call-done = bf16[128,1536]{1,0:T(8,128)(2,1)} async-done(((bf16[512,1536]{1,0:T(8,128)(2,1)}), bf16[128,1536]{1,0:T(8,128)(2,1)}) %reduce-scatter.63.cloned.1.call-update) | async-done | bytes 393232 | tf_op jit(solution)/shard_map/reduce_scatter | solution.py:183
  647.1 23.0 %reduce-scatter.75.cloned.1.call-done = bf16[128,1536]{1,0:T(8,128)(2,1)} async-done(((bf16[512,1536]{1,0:T(8,128)(2,1)}), bf16[128,1536]{1,0:T(8,128)(2,1)}) %reduce-scatter.75.cloned.1.call-update) | async-done | bytes 393232 | tf_op jit(solution)/shard_map/reduce_scatter | solution.py:183
  740.4 21.9 %reduce-scatter.105.cloned.1.call-done = bf16[768,96]{0,1:T(8,128)(2,1)} async-done(((bf16[768,768]{0,1:T(8,128)(2,1)}), bf16[768,96]{0,1:T(8,128)(2,1)}) %reduce-scatter.105.cloned.1.call-update) | async-done | bytes 147472 | tf_op jit(solution)/shard_map/reduce_scatter | solution.py:227
  762.3 33.2 %reduce-scatter.101.cloned.1.call-done = bf16[768,96]{0,1:T(8,128)(2,1)} async-done(((bf16[768,768]{0,1:T(8,128)(2,1)}), bf16[768,96]{0,1:T(8,128)(2,1)}) %reduce-scatter.101.cloned.1.call-update) | async-done | bytes 147472 | tf_op jit(solution)/shard_map/reduce_scatter | solution.py:227
  795.5 33.3 %reduce-scatter.107.cloned.1.call-done = bf16[768,96]{0,1:T(8,128)(2,1)} async-done(((bf16[768,768]{0,1:T(8,128)(2,1)}), bf16[768,96]{0,1:T(8,128)(2,1)}) %reduce-scatter.107.cloned.1.call-update) | async-done | bytes 147472 | tf_op jit(solution)/shard_map/reduce_scatter | solution.py:227
  828.8 33.3 %reduce-scatter.103.cloned.1.call-done = bf16[768,96]{0,1:T(8,128)(2,1)} async-done(((bf16[768,768]{0,1:T(8,128)(2,1)}), bf16[768,96]{0,1:T(8,128)(2,1)}) %reduce-scatter.103.cloned.1.call-update) | async-done | bytes 147472 | tf_op jit(solution)/shard_map/reduce_scatter | solution.py:227
  864.0 31.4 %reduce-scatter.97.cloned.1.call-done = bf16[96,768]{1,0:T(8,128)(2,1)} async-done(((bf16[768,768]{1,0:T(8,128)(2,1)}), bf16[96,768]{1,0:T(8,128)(2,1)}) %reduce-scatter.97.cloned.1.call-update) | async-done | bytes 147472 | tf_op jit(solution)/shard_map/reduce_scatter | solution.py:221
  895.4 33.3 %reduce-scatter.93.cloned.1.call-done = bf16[96,768]{1,0:T(8,128)(2,1)} async-done(((bf16[768,768]{1,0:T(8,128)(2,1)}), bf16[96,768]{1,0:T(8,128)(2,1)}) %reduce-scatter.93.cloned.1.call-update) | async-done | bytes 147472 | tf_op jit(solution)/shard_map/reduce_scatter | solution.py:221
  928.7 33.2 %reduce-scatter.99.cloned.1.call-done = bf16[96,768]{1,0:T(8,128)(2,1)} async-done(((bf16[768,768]{1,0:T(8,128)(2,1)}), bf16[96,768]{1,0:T(8,128)(2,1)}) %reduce-scatter.99.cloned.1.call-update) | async-done | bytes 147472 | tf_op jit(solution)/shard_map/reduce_scatter | solution.py:221
  961.9 33.3 %reduce-scatter.95.cloned.1.call-done = bf16[96,768]{1,0:T(8,128)(2,1)} async-done(((bf16[768,768]{1,0:T(8,128)(2,1)}), bf16[96,768]{1,0:T(8,128)(2,1)}) %reduce-scatter.95.cloned.1.call-update) | async-done | bytes 147472 | tf_op jit(solution)/shard_map/reduce_scatter | solution.py:221
  997.1 25.9 %reduce-scatter.123.cloned.1.call-done = bf16[192,96]{1,0:T(8,128)(2,1)} async-done(((bf16[768,96]{1,0:T(8,128)(2,1)}), bf16[192,96]{1,0:T(8,128)(2,1)}) %reduce-scatter.123.cloned.1.call-update) | async-done | bytes 36880
  1023.9 25.7 %reduce-scatter.117.cloned.1.call-done = bf16[192,96]{1,0:T(8,128)(2,1)} async-done(((bf16[768,96]{1,0:T(8,128)(2,1)}), bf16[192,96]{1,0:T(8,128)(2,1)}) %reduce-scatter.117.cloned.1.call-update) | async-done | bytes 36880
  1050.6 25.8 %reduce-scatter.119.cloned.1.call-done = bf16[192,96]{1,0:T(8,128)(2,1)} async-done(((bf16[768,96]{1,0:T(8,128)(2,1)}), bf16[192,96]{1,0:T(8,128)(2,1)}) %reduce-scatter.119.cloned.1.call-update) | async-done | bytes 36880
  1078.0 38.1 %reduce-scatter.81.cloned.1.call-done = bf16[96,1920]{1,0:T(8,128)(2,1)} async-done(((bf16[768,1920]{1,0:T(8,128)(2,1)}), bf16[96,1920]{1,0:T(8,128)(2,1)}) %reduce-scatter.81.cloned.1.call-update) | async-done | bytes 368656 | tf_op jit(solution)/shard_map/reduce_scatter | solution.py:200
  1118.2 38.5 %reduce-scatter.77.cloned.1.call-done = bf16[96,1920]{1,0:T(8,128)(2,1)} async-done(((bf16[768,1920]{1,0:T(8,128)(2,1)}), bf16[96,1920]{1,0:T(8,128)(2,1)}) %reduce-scatter.77.cloned.1.call-update) | async-done | bytes 368656 | tf_op jit(solution)/shard_map/reduce_scatter | solution.py:200
  1162.8 34.7 %reduce-scatter.83.cloned.1.call-done = bf16[96,1920]{1,0:T(8,128)(2,1)} async-done(((bf16[768,1920]{1,0:T(8,128)(2,1)}), bf16[96,1920]{1,0:T(8,128)(2,1)}) %reduce-scatter.83.cloned.1.call-update) | async-done | bytes 368656 | tf_op jit(solution)/shard_map/reduce_scatter | solution.py:200
  1200.4 65.0 %all-reduce.95.cloned.1.call-done = (bf16[768]{0:T(1024)(128)(2,1)}, bf16[768]{0:T(1024)(128)(2,1)}, bf16[768]{0:T(1024)(128)(2,1)}, bf16[768]{0:T(1024)(128)(2,...) async-done(((bf16[768]{0:T(1024)(128)(2,1)}, ...) | async-done | bytes 72208
  1292.9 13.8 all-reduce.91
  1314.0 23.6 %reduce-scatter.57.cloned.1.call-done = bf16[128,768]{1,0:T(8,128)(2,1)} async-done(((bf16[512,768]{1,0:T(8,128)(2,1)}), bf16[128,768]{1,0:T(8,128)(2,1)}) %reduce-scatter.57.cloned.1.call-update) | async-done | bytes 196624 | tf_op jit(solution)/shard_map/reduce_scatter | solution.py:377
  1337.6 29.8 %reduce-scatter.53.cloned.1.call-done = bf16[128,768]{1,0:T(8,128)(2,1)} async-done(((bf16[512,768]{1,0:T(8,128)(2,1)}), bf16[128,768]{1,0:T(8,128)(2,1)}) %reduce-scatter.53.cloned.1.call-update) | async-done | bytes 196624 | tf_op jit(solution)/shard_map/reduce_scatter | solution.py:377
  1367.4 29.1 %reduce-scatter.59.cloned.1.call-done = bf16[128,768]{1,0:T(8,128)(2,1)} async-done(((bf16[512,768]{1,0:T(8,128)(2,1)}), bf16[128,768]{1,0:T(8,128)(2,1)}) %reduce-scatter.59.cloned.1.call-update) | async-done | bytes 196624 | tf_op jit(solution)/shard_map/reduce_scatter | solution.py:377
  1396.5 29.1 %reduce-scatter.55.cloned.1.call-done = bf16[128,768]{1,0:T(8,128)(2,1)} async-done(((bf16[512,768]{1,0:T(8,128)(2,1)}), bf16[128,768]{1,0:T(8,128)(2,1)}) %reduce-scatter.55.cloned.1.call-update) | async-done | bytes 196624 | tf_op jit(solution)/shard_map/reduce_scatter | solution.py:377
  1428.1 25.3 %reduce-scatter.113.cloned.1.call-done = bf16[480,96]{1,0:T(8,128)(2,1)} async-done(((bf16[1920,96]{1,0:T(8,128)(2,1)}), bf16[480,96]{1,0:T(8,128)(2,1)}) %reduce-scatter.113.cloned.1.call-update) | async-done | bytes 92176
  1454.3 26.4 %reduce-scatter.109.cloned.1.call-done = bf16[480,96]{1,0:T(8,128)(2,1)} async-done(((bf16[1920,96]{1,0:T(8,128)(2,1)}), bf16[480,96]{1,0:T(8,128)(2,1)}) %reduce-scatter.109.cloned.1.call-update) | async-done | bytes 92176
  1481.8 26.8 %reduce-scatter.115.cloned.1.call-done = bf16[480,96]{1,0:T(8,128)(2,1)} async-done(((bf16[1920,96]{1,0:T(8,128)(2,1)}), bf16[480,96]{1,0:T(8,128)(2,1)}) %reduce-scatter.115.cloned.1.call-update) | async-done | bytes 92176
  1509.6 26.5 %reduce-scatter.111.cloned.1.call-done = bf16[480,96]{1,0:T(8,128)(2,1)} async-done(((bf16[1920,96]{1,0:T(8,128)(2,1)}), bf16[480,96]{1,0:T(8,128)(2,1)}) %reduce-scatter.111.cloned.1.call-update) | async-done | bytes 92176
  (802 shorter events, 421.0 us)
Async XLA Ops:
  7.2 94.3 %all-gather.11.cloned.1.call-start = ((), (), s32[]{:S(2)}) async-start(), calls=%async_computation.36 | async-start | bytes 3317760 | tf_op jit(solution)/shard_map/all_gather | solution.py:313
  18.1 113.9 %all-gather.13.cloned.1.call-start = ((), (), s32[]{:S(2)}) async-start(), calls=%async_computation.37 | async-start | bytes 1327104 | tf_op jit(solution)/shard_map/all_gather | solution.py:316
  24.9 118.8 %all-gather.15.cloned.1.call-start = ((), (), s32[]{:S(2)}) async-start(), calls=%async_computation.38 | async-start | bytes 1327104 | tf_op jit(solution)/shard_map/all_gather | solution.py:320
  25.6 121.7 %all-gather.17.cloned.1.call-start = ((), (), s32[]{:S(2)}) async-start(), calls=%async_computation.39 | async-start | bytes 1327104 | tf_op jit(solution)/shard_map/all_gather | solution.py:322
  26.2 157.7 %reduce-scatter.69.cloned.1.call-start = ((), (), s32[]{:S(2)}) async-start(), calls=%async_computation.48 | async-start | bytes 983040 | tf_op jit(solution)/shard_map/reduce_scatter | solution.py:390
  153.8 77.2 %reduce-scatter.71.cloned.1.call-start = ((), (), s32[]{:S(2)}) async-start(), calls=%async_computation.49 | async-start | bytes 1966080 | tf_op jit(solution)/shard_map/reduce_scatter | solution.py:183
  195.8 220.6 %reduce-scatter.61.cloned.1.call-start = ((), (), s32[]{:S(2)}) async-start(), calls=%async_computation.44 | async-start | bytes 983040 | tf_op jit(solution)/shard_map/reduce_scatter | solution.py:390
  360.6 77.6 %reduce-scatter.73.cloned.1.call-start = ((), (), s32[]{:S(2)}) async-start(), calls=%async_computation.50 | async-start | bytes 983040 | tf_op jit(solution)/shard_map/reduce_scatter | solution.py:390
  386.2 83.7 %reduce-scatter.65.cloned.1.call-start = ((), (), s32[]{:S(2)}) async-start(), calls=%async_computation.46 | async-start | bytes 983040 | tf_op jit(solution)/shard_map/reduce_scatter | solution.py:390
  413.7 136.5 %reduce-scatter.89.cloned.1.call-start = ((), (), s32[]{:S(2)}) async-start(), calls=%async_computation.58 | async-start | bytes 1327104 | tf_op jit(solution)/shard_map/reduce_scatter | solution.py:209
  416.4 164.0 %reduce-scatter.91.cloned.1.call-start = ((), (), s32[]{:S(2)}) async-start(), calls=%async_computation.59 | async-start | bytes 1327104 | tf_op jit(solution)/shard_map/reduce_scatter | solution.py:209
  477.7 104.5 %reduce-scatter.85.cloned.1.call-start = ((), (), s32[]{:S(2)}) async-start(), calls=%async_computation.56 | async-start | bytes 1327104 | tf_op jit(solution)/shard_map/reduce_scatter | solution.py:209
  483.3 117.8 %reduce-scatter.87.cloned.1.call-start = ((), (), s32[]{:S(2)}) async-start(), calls=%async_computation.57 | async-start | bytes 1327104 | tf_op jit(solution)/shard_map/reduce_scatter | solution.py:209
  486.0 150.4 %reduce-scatter.63.cloned.1.call-start = ((), (), s32[]{:S(2)}) async-start(), calls=%async_computation.45 | async-start | bytes 1966080 | tf_op jit(solution)/shard_map/reduce_scatter | solution.py:183
  507.2 163.0 %reduce-scatter.75.cloned.1.call-start = ((), (), s32[]{:S(2)}) async-start(), calls=%async_computation.51 | async-start | bytes 1966080 | tf_op jit(solution)/shard_map/reduce_scatter | solution.py:183
  528.6 175.4 %reduce-scatter.67.cloned.1.call-start = ((), (), s32[]{:S(2)}) async-start(), calls=%async_computation.47 | async-start | bytes 1966080 | tf_op jit(solution)/shard_map/reduce_scatter | solution.py:183
  550.2 188.3 %reduce-scatter.121.cloned.1.call-start = ((), (), s32[]{:S(2)}) async-start(), calls=%async_computation.74 | async-start | bytes 245760
  552.0 210.3 %reduce-scatter.105.cloned.1.call-start = ((), (), s32[]{:S(2)}) async-start(), calls=%async_computation.66 | async-start | bytes 1327104 | tf_op jit(solution)/shard_map/reduce_scatter | solution.py:227
  555.8 239.7 %reduce-scatter.101.cloned.1.call-start = ((), (), s32[]{:S(2)}) async-start(), calls=%async_computation.64 | async-start | bytes 1327104 | tf_op jit(solution)/shard_map/reduce_scatter | solution.py:227
  559.5 269.3 %reduce-scatter.107.cloned.1.call-start = ((), (), s32[]{:S(2)}) async-start(), calls=%async_computation.67 | async-start | bytes 1327104 | tf_op jit(solution)/shard_map/reduce_scatter | solution.py:227
  563.3 298.8 %reduce-scatter.103.cloned.1.call-start = ((), (), s32[]{:S(2)}) async-start(), calls=%async_computation.65 | async-start | bytes 1327104 | tf_op jit(solution)/shard_map/reduce_scatter | solution.py:227
  567.1 328.3 %reduce-scatter.97.cloned.1.call-start = ((), (), s32[]{:S(2)}) async-start(), calls=%async_computation.62 | async-start | bytes 1327104 | tf_op jit(solution)/shard_map/reduce_scatter | solution.py:221
  570.3 358.4 %reduce-scatter.93.cloned.1.call-start = ((), (), s32[]{:S(2)}) async-start(), calls=%async_computation.60 | async-start | bytes 1327104 | tf_op jit(solution)/shard_map/reduce_scatter | solution.py:221
  573.6 388.3 %reduce-scatter.99.cloned.1.call-start = ((), (), s32[]{:S(2)}) async-start(), calls=%async_computation.63 | async-start | bytes 1327104 | tf_op jit(solution)/shard_map/reduce_scatter | solution.py:221
  576.9 418.3 %reduce-scatter.95.cloned.1.call-start = ((), (), s32[]{:S(2)}) async-start(), calls=%async_computation.61 | async-start | bytes 1327104 | tf_op jit(solution)/shard_map/reduce_scatter | solution.py:221
  580.3 442.7 %reduce-scatter.123.cloned.1.call-start = ((), (), s32[]{:S(2)}) async-start(), calls=%async_computation.75 | async-start | bytes 245760
  582.1 467.5 %reduce-scatter.117.cloned.1.call-start = ((), (), s32[]{:S(2)}) async-start(), calls=%async_computation.72 | async-start | bytes 245760
  583.9 492.5 %reduce-scatter.119.cloned.1.call-start = ((), (), s32[]{:S(2)}) async-start(), calls=%async_computation.73 | async-start | bytes 245760
  602.8 513.2 %reduce-scatter.81.cloned.1.call-start = ((), (), s32[]{:S(2)}) async-start(), calls=%async_computation.54 | async-start | bytes 3317760 | tf_op jit(solution)/shard_map/reduce_scatter | solution.py:200
  606.7 550.0 %reduce-scatter.77.cloned.1.call-start = ((), (), s32[]{:S(2)}) async-start(), calls=%async_computation.52 | async-start | bytes 3317760 | tf_op jit(solution)/shard_map/reduce_scatter | solution.py:200
  641.8 555.8 %reduce-scatter.83.cloned.1.call-start = ((), (), s32[]{:S(2)}) async-start(), calls=%async_computation.55 | async-start | bytes 3317760 | tf_op jit(solution)/shard_map/reduce_scatter | solution.py:200
  675.6 589.8 %all-reduce.95.cloned.1.call-start = ((), (), s32[]{:S(2)}) async-start(), calls=%async_computation.76 | async-start | bytes 176128
  717.6 592.6 %reduce-scatter.79.cloned.1.call-start = ((), (), s32[]{:S(2)}) async-start(), calls=%async_computation.53 | async-start | bytes 3317760 | tf_op jit(solution)/shard_map/reduce_scatter | solution.py:200
  721.5 616.2 %reduce-scatter.57.cloned.1.call-start = ((), (), s32[]{:S(2)}) async-start(), calls=%async_computation.42 | async-start | bytes 983040 | tf_op jit(solution)/shard_map/reduce_scatter | solution.py:377
  725.2 642.2 %reduce-scatter.53.cloned.1.call-start = ((), (), s32[]{:S(2)}) async-start(), calls=%async_computation.40 | async-start | bytes 983040 | tf_op jit(solution)/shard_map/reduce_scatter | solution.py:377
  728.7 667.8 %reduce-scatter.59.cloned.1.call-start = ((), (), s32[]{:S(2)}) async-start(), calls=%async_computation.43 | async-start | bytes 983040 | tf_op jit(solution)/shard_map/reduce_scatter | solution.py:377
  730.9 694.8 %reduce-scatter.55.cloned.1.call-start = ((), (), s32[]{:S(2)}) async-start(), calls=%async_computation.41 | async-start | bytes 983040 | tf_op jit(solution)/shard_map/reduce_scatter | solution.py:377
  734.3 343.7 %copy-start.181 = (f32[128]{0:T(128)S(1)}, f32[128]{0:T(128)}, u32[]{:S(2)}) copy-start(f32[128]{0:T(128)} %get-tuple-element.23) | copy-start | bytes 1540
  734.3 719.0 %reduce-scatter.113.cloned.1.call-start = ((), (), s32[]{:S(2)}) async-start(), calls=%async_computation.70 | async-start | bytes 614400
  864.0 254.1 %copy-start.180 = (f32[128]{0:T(128)S(1)}, f32[128]{0:T(128)}, u32[]{:S(2)}) copy-start(f32[128]{0:T(128)} %get-tuple-element.24) | copy-start | bytes 1540
  864.0 254.2 %copy-start.179 = (f32[128]{0:T(128)S(1)}, f32[128]{0:T(128)}, u32[]{:S(2)}) copy-start(f32[128]{0:T(128)} %get-tuple-element.26) | copy-start | bytes 1540
  864.0 254.2 %copy-start.178 = (f32[128]{0:T(128)S(1)}, f32[128]{0:T(128)}, u32[]{:S(2)}) copy-start(f32[128]{0:T(128)} %get-tuple-element.48) | copy-start | bytes 1540
  864.0 254.2 %copy-start.177 = (f32[128]{0:T(128)S(1)}, f32[128]{0:T(128)}, u32[]{:S(2)}) copy-start(f32[128]{0:T(128)} %get-tuple-element.49) | copy-start | bytes 1540
  1118.1 362.7 %reduce-scatter.109.cloned.1.call-start = ((), (), s32[]{:S(2)}) async-start(), calls=%async_computation.68 | async-start | bytes 614400
  1158.8 349.8 %reduce-scatter.115.cloned.1.call-start = ((), (), s32[]{:S(2)}) async-start(), calls=%async_computation.71 | async-start | bytes 614400
  1199.5 226.2 %copy-start.22 = (f32[128,768]{1,0:T(8,128)S(1)}, f32[128,768]{1,0:T(8,128)}, u32[]{:S(2)}) copy-start(f32[128,768]{1,0:T(8,128)} %copy-done.21) | copy-start | bytes 1179652
  1199.5 226.2 %copy-start.25 = (f32[128,768]{1,0:T(8,128)S(1)}, f32[128,768]{1,0:T(8,128)}, u32[]{:S(2)}) copy-start(f32[128,768]{1,0:T(8,128)} %copy-done.23) | copy-start | bytes 1179652
  1199.5 336.6 %reduce-scatter.111.cloned.1.call-start = ((), (), s32[]{:S(2)}) async-start(), calls=%async_computation.69 | async-start | bytes 614400
  (184 other events, 2466.9 us)
Sparse Core Ops, SparseCore 0:
  18.2 38.8 all-gather.10
  59.4 21.6 all-gather.12
  82.7 22.4 all-gather.14
  106.7 22.2 all-gather.16
  153.9 29.8 reduce-scatter.68
  195.9 35.0 reduce-scatter.70
  360.7 42.1 reduce-scatter.60
  405.8 32.4 reduce-scatter.72
  441.1 28.6 reduce-scatter.64
  472.0 29.3 reduce-scatter.88
  503.7 30.9 reduce-scatter.90
  536.9 30.9 reduce-scatter.84
  570.1 30.9 reduce-scatter.86
  603.9 32.3 reduce-scatter.62
  639.2 30.9 reduce-scatter.74
  673.0 30.9 reduce-scatter.66
  706.6 23.5 reduce-scatter.120
  732.3 29.9 reduce-scatter.104
  764.6 30.8 reduce-scatter.100
  797.7 31.1 reduce-scatter.106
  831.1 30.9 reduce-scatter.102
  864.4 30.9 reduce-scatter.96
  897.7 30.9 reduce-scatter.92
  930.9 30.9 reduce-scatter.98
  964.2 30.9 reduce-scatter.94
  997.8 25.1 reduce-scatter.122
  1025.6 23.9 reduce-scatter.116
  1052.4 23.9 reduce-scatter.118
  1078.7 37.2 reduce-scatter.80
  1118.3 38.3 reduce-scatter.76
  1159.1 38.4 reduce-scatter.82
  1203.9 61.4 all-reduce.94
  1267.6 39.0 reduce-scatter.78
  1309.9 27.6 reduce-scatter.56
  1341.3 26.0 reduce-scatter.52
  1370.4 26.0 reduce-scatter.58
  1399.6 26.0 reduce-scatter.54
  1428.7 24.5 reduce-scatter.112
  1456.0 24.7 reduce-scatter.108
  1483.8 24.6 reduce-scatter.114
  1511.4 24.6 reduce-scatter.110
where the time goes:
time: 1560 us; the launch traced here: 1540 us
  waiting for transfers between devices  895 us (57%)
  blocking collectives  246 us (16%)
  matrix products  165 us (11%)
  local copies, waits for them, and re-layouts  140 us (9%)
  other arithmetic  71.1 us (5%)
  between operations  24.5 us (2%)
    unnamed x50, waiting for transfers between devices  249 us
    reduce_scatter x4, waiting for transfers between devices, reduce_grads(): lax.psum_scatter(local_grads[9].astype(jnp.bfloat16), 'dp', scatter_dimen...  131 us
    reduce_scatter x4, waiting for transfers between devices, reduce_grads(): lax.psum_scatter(local_grads[11].astype(jnp.bfloat16), 'dp', scatter_dime...  122 us
    reduce_scatter x4, waiting for transfers between devices, shards(): lax.psum_scatter(jnp.dot(active_all, down_full, preferred_element_type=jn...  112 us
    reduce_scatter x4, waiting for transfers between devices, reduce_grads(): lax.psum_scatter(local_grads[2].astype(jnp.bfloat16), 'dp', scatter_dimen...  111 us
    reduce_scatter x4, waiting for transfers between devices, shards(): lax.psum_scatter(jnp.einsum('rf,df->rd', grad_hidden, up_full, preferred_...  83.5 us
    unnamed x472, local copies, waits for them, and re-layouts  78.2 us
    reduce_scatter x4, waiting for transfers between devices, attention_backward(): lax.psum_scatter(map_blocks(key_step, key_block, value_block, jnp.int32(0...  69.6 us
  transfers between devices with their start and end apart: 41, of which 31 were waited for; matrix products, arithmetic and copies ran while one was open for 18% of the time, Pallas kernels for 0%

commit v1 on v0

v1 whole, which is shorter than its diff:
```python
import functools

import jax
import jax.numpy as jnp
from jax import lax
from jax.experimental import pallas as pl
from jax.experimental.pallas import tpu as pltpu
from jax.sharding import PartitionSpec as P

D = 768
HEADS = 12
HEAD = 64
FF = 3072
MICRO = 4
QKV = 1920
SEQ = 512
VFRESH = 384

EPS = 1e-05
BIG = 1e30
GELU_C = 0.7978845608028654
GELU_A = 0.044715
MESH = pl.DeviceIdType.MESH
ANY = pl.BlockSpec(memory_space=pl.ANY)


class Plan:
    def __init__(self, mesh):
        self.n_dp = mesh.shape["dp"]
        self.n_mp = mesh.shape["mp"]
        self.n_z = self.n_dp // 2
        self.rows = D // self.n_dp
        self.cols = FF // self.n_mp
        self.qkv = QKV // self.n_mp
        self.out = D // self.n_mp
        self.out_at = -(-self.qkv // 128) * 128
        self.unit = 3 * self.rows + 16
        self.small = self.n_dp * self.n_mp
        self.per_seq = SEQ * MICRO // SEQ
        self.n_seq = self.n_mp // MICRO
        assert self.out_at + self.out <= self.cols and self.rows % 16 == 0
        assert self.n_seq * MICRO == self.n_mp

    def ring_at(self, i):
        half = self.n_mp // 2
        return i + (i // half) * (self.n_mp - 1 + half - 2 * i)


def where_am_i():
    return lax.axis_index("dp"), lax.axis_index("mp")


def greet(plan, dp, i, z, c):
    barrier = pltpu.get_barrier_semaphore()
    partners = [(dp + 1 - 2 * c, i)]
    partners += [(((z + k) % plan.n_z) * 2 + c, i) for k in range(1, plan.n_z)]
    partners += [(dp, (i + k) % plan.n_mp) for k in range(1, plan.n_mp)]
    for partner in partners:
        pl.semaphore_signal(barrier, inc=1, device_id=partner, device_id_type=MESH)
    pl.semaphore_wait(barrier, len(partners))


def push(src, dst, send, recv, device):
    copy = pltpu.make_async_remote_copy(
        src_ref=src, dst_ref=dst, send_sem=send, recv_sem=recv, device_id=device, device_id_type=MESH
    )
    return copy


def gather_kernel(plan, pk, tok, fv, cot, g, x, f, y, own_sem, zs, zr, rs, rr, ss, sr, xs, xr):
    dp, i = where_am_i()
    c, z = dp % 2, dp // 2
    n_mp, n_z = plan.n_mp, plan.n_z
    sib = (dp + 1 - 2 * c, i)
    p = plan.ring_at(i)
    device_at = lambda pos: plan.ring_at((pos + n_mp) % n_mp)
    greet(plan, dp, i, z, c)

    pairs = ((tok, x), (fv, f), (cot, y))
    q = plan.per_seq
    for a, (src, dst) in enumerate(pairs):
        for m in range(MICRO):
            target = m * plan.n_seq + i // q
            place = i % q

            @pl.when(target != i)
            def _():
                push(src.at[m], dst.at[place], xs.at[a, m], xr.at[a, place], (dp, target)).start()

            @pl.when(target == i)
            def _():
                pltpu.make_async_copy(src.at[m], dst.at[place], xs.at[a, m]).start()

    mine = pltpu.make_async_copy(pk, g.at[i, dp], own_sem)
    mine.start()
    unit_dp = [((z + n_z - k) % n_z) * 2 + c for k in range(n_z)]

    def source(k, origin):
        return g.at[origin, unit_dp[k]]

    sends = []

    def to_sibling(k, h, src, origin):
        cp = push(src, g.at[origin, unit_dp[k]], ss.at[k, h], sr.at[k, h], sib)
        cp.start()
        sends.append(cp)

    def to_ring(k, h, src):
        sign = 1 if k % 2 == 0 else -1
        origin = device_at(p - sign * h)
        cp = push(src, g.at[origin, unit_dp[k]], rs.at[k, h], rr.at[k, h], (dp, device_at(p + sign)))
        cp.start()
        sends.append(cp)

    to_ring(0, 0, pk)
    for k in range(1, n_z):
        cp = push(pk, g.at[i, dp], zs.at[k - 1], zr.at[k - 1], (((z + k) % n_z) * 2 + c, i))
        cp.start()
        sends.append(cp)
    to_sibling(0, 0, pk, i)
    for k in range(1, n_z):
        here = source(k, i)
        push(here, here, zs.at[k - 1], zr.at[k - 1], sib).wait_recv()
        to_ring(k, 0, here)
        to_sibling(k, 0, here, i)
    for h in range(n_mp - 1):
        for k in range(n_z):
            sign = 1 if k % 2 == 0 else -1
            origin = device_at(p - sign * (h + 1))
            here = source(k, origin)
            push(here, here, rs.at[k, h], rr.at[k, h], sib).wait_recv()
            if h < n_mp - 2:
                to_ring(k, h + 1, here)
            to_sibling(k, h + 1, here, origin)
    sib_dp = [((z + n_z - k) % n_z) * 2 + 1 - c for k in range(n_z)]
    for h in range(n_mp):
        for k in range(n_z):
            sign = 1 if k % 2 == 0 else -1
            here = g.at[device_at(p - sign * h), sib_dp[k]]
            push(here, here, ss.at[k, h], sr.at[k, h], sib).wait_recv()
    for cp in sends:
        cp.wait_send()
    mine.wait()
    for a, (src, dst) in enumerate(pairs):
        for m in range(MICRO):
            target = m * plan.n_seq + i // q
            place = i % q

            @pl.when(target != i)
            def _():
                push(src.at[m], dst.at[place], xs.at[a, m], xr.at[a, place], (dp, target)).wait_send()

            @pl.when(target == i)
            def _():
                pltpu.make_async_copy(src.at[m], dst.at[place], xs.at[a, m]).wait()

        for place in range(q):
            origin = (i % plan.n_seq) * q + place

            @pl.when(origin != i)
            def _():
                push(dst.at[place], dst.at[place], xs.at[a, 0], xr.at[a, place], sib).wait_recv()


def gather(plan, packed, tok, fv, cot):
    n_mp, n_z = plan.n_mp, plan.n_z
    bf = jnp.bfloat16
    dma = pltpu.SemaphoreType.DMA
    return pl.pallas_call(
        functools.partial(gather_kernel, plan),
        name="gather",
        out_shape=(
            jax.ShapeDtypeStruct((n_mp, plan.n_dp, plan.unit, plan.cols), bf),
            jax.ShapeDtypeStruct(tok.shape, bf),
            jax.ShapeDtypeStruct(fv.shape, bf),
            jax.ShapeDtypeStruct(cot.shape, bf),
        ),
        in_specs=[ANY] * 4,
        out_specs=(ANY,) * 4,
        scratch_shapes=[
            dma,
            dma((n_z - 1,)),
            dma((n_z - 1,)),
            dma((n_z, n_mp - 1)),
            dma((n_z, n_mp - 1)),
            dma((n_z, n_mp)),
            dma((n_z, n_mp)),
            dma((3, MICRO)),
            dma((3, plan.per_seq)),
        ],
        compiler_params=pltpu.CompilerParams(collective_id=0, has_side_effects=True),
    )(packed, tok, fv, cot)


def reduce_kernel(
    plan, grads, o1, o2, o3, total, r1, r2, r3,
    own, other, ring, last, own_sem, ss, sr, rs, rr, zs, zr, xs, xr,
):
    dp, i = where_am_i()
    c, z = dp % 2, dp // 2
    n_mp, n_z, R = plan.n_mp, plan.n_z, plan.rows
    sib = (dp + 1 - 2 * c, i)
    p = plan.ring_at(i)
    device_at = lambda pos: plan.ring_at((pos + n_mp) % n_mp)
    f32, bf = jnp.float32, jnp.bfloat16
    greet(plan, dp, i, z, c)

    pairs = ((o1, r1), (o2, r2), (o3, r3))
    q = plan.per_seq
    micro, part = i // plan.n_seq, i % plan.n_seq
    place = i % q

    def back(start):
        for a, (src, dst) in enumerate(pairs):
            for s in range(q):
                owner = part * q + s
                far = push(src.at[s], dst.at[micro], xs.at[a, s], xr.at[a, micro], (dp, owner))
                near = pltpu.make_async_copy(src.at[s], dst.at[micro], xs.at[a, s])

                @pl.when(owner != i)
                def _():
                    far.start() if start else far.wait_send()

                @pl.when(owner == i)
                def _():
                    near.start() if start else near.wait()

    bounds = ((0, R), (R, 2 * R), (2 * R, plan.unit))
    tiles = [pl.ds(lo, hi - lo) for lo, hi in bounds]
    unit_dp = [((z + n_z - k) % n_z) * 2 + c for k in range(n_z)]
    sib_dp = [((z + n_z - k) % n_z) * 2 + 1 - c for k in range(n_z)]
    order = [k for k in range(n_z - 1, -1, -1)]
    sends = []
    for k in order:
        for t in range(n_mp):
            cp = push(grads.at[t, sib_dp[k]], other.at[t, k], ss.at[k, t], sr.at[k, t], sib)
            cp.start()
            sends.append(cp)
            pltpu.make_async_copy(grads.at[t, unit_dp[k]], own.at[t, k], own_sem.at[k, t]).start()
    back(True)

    def add(t, k, tile, extra):
        own[t, k, tile, :] = (own[t, k, tile, :].astype(f32) + extra.astype(f32)).astype(bf)

    def chunk(k, step):
        sign = 1 if k % 2 == 0 else -1
        return device_at(p - sign * (1 + step))

    def ring_send(k, piece, step):
        sign = 1 if k % 2 == 0 else -1
        tile = tiles[piece]
        cp = push(
            own.at[chunk(k, step), k, tile],
            ring.at[k, step, tile],
            rs.at[k, piece, step],
            rr.at[k, piece, step],
            (dp, device_at(p + sign)),
        )
        cp.start()
        sends.append(cp)

    for k0 in range(n_z - 2, -1, -2):
        ks = (k0, k0 + 1)
        for k in ks:
            for t in range(n_mp):
                pltpu.make_async_copy(grads.at[t, unit_dp[k]], own.at[t, k], own_sem.at[k, t]).wait()
                push(other.at[t, k], other.at[t, k], ss.at[k, t], sr.at[k, t], sib).wait_recv()
        for step in range(n_mp):
            for piece in range(3):
                for k in ks:
                    tile = tiles[piece]
                    t = chunk(k, step)
                    if step > 0:
                        got = ring.at[k, step - 1, tile]
                        push(got, got, rs.at[k, piece, step - 1], rr.at[k, piece, step - 1], sib).wait_recv()
                        own[t, k, tile, :] = (
                            own[t, k, tile, :].astype(f32)
                            + other[t, k, tile, :].astype(f32)
                            + ring[k, step - 1, tile, :].astype(f32)
                        ).astype(bf)
                    else:
                        add(t, k, tile, other[t, k, tile, :])
                    if step < n_mp - 1:
                        ring_send(k, piece, step)
                    elif k > 0:
                        cp = push(
                            own.at[i, k, tile],
                            last.at[k - 1, tile],
                            zs.at[k - 1, piece],
                            zr.at[k - 1, piece],
                            (unit_dp[k], i),
                        )
                        cp.start()
                        sends.append(cp)
    for piece in range(3):
        tile = tiles[piece]
        for k in range(1, n_z):
            got = last.at[k - 1, tile]
            push(got, got, zs.at[k - 1, piece], zr.at[k - 1, piece], sib).wait_recv()
        value = own[i, 0, tile, :].astype(f32)
        for k in range(1, n_z):
            value = value + last[k - 1, tile, :].astype(f32)
        total[tile, :] = value
    for cp in sends:
        cp.wait_send()
    back(False)
    for a, (src, dst) in enumerate(pairs):
        for m in range(MICRO):
            origin = m * plan.n_seq + i // q

            @pl.when(origin != i)
            def _():
                push(dst.at[m], dst.at[m], xs.at[a, 0], xr.at[a, m], sib).wait_recv()


def reduce(plan, grads, o1, o2, o3):
    n_mp, n_z = plan.n_mp, plan.n_z
    bf, f32 = jnp.bfloat16, jnp.float32
    dma = pltpu.SemaphoreType.DMA
    block = (plan.unit, plan.cols)
    return pl.pallas_call(
        functools.partial(reduce_kernel, plan),
        name="reduce",
        out_shape=(
            jax.ShapeDtypeStruct(block, f32),
            jax.ShapeDtypeStruct(o1.shape, bf),
            jax.ShapeDtypeStruct(o2.shape, bf),
            jax.ShapeDtypeStruct(o3.shape, bf),
        ),
        in_specs=[ANY] * 4,
        out_specs=(pl.BlockSpec(memory_space=pltpu.VMEM), ANY, ANY, ANY),
        scratch_shapes=[
            pltpu.VMEM((n_mp, n_z) + block, bf),
            pltpu.VMEM((n_mp, n_z) + block, bf),
            pltpu.VMEM((n_z, n_mp - 1) + block, bf),
            pltpu.VMEM((n_z - 1,) + block, bf),
            dma((n_z, n_mp)),
            dma((n_z, n_mp)),
            dma((n_z, n_mp)),
            dma((n_z, 3, n_mp - 1)),
            dma((n_z, 3, n_mp - 1)),
            dma((n_z - 1, 3)),
            dma((n_z - 1, 3)),
            dma((3, plan.per_seq)),
            dma((3, MICRO)),
        ],
        compiler_params=pltpu.CompilerParams(
            collective_id=1, has_side_effects=True, vmem_limit_bytes=56 << 20
        ),
    )(grads, o1, o2, o3)


def layer_norm(inputs, gain_vec, shift_vec):
    average = jnp.mean(inputs, axis=-1, keepdims=True)
    centred = inputs - average
    variance = jnp.mean(centred * centred, axis=-1, keepdims=True)
    inv_std = lax.rsqrt(variance + EPS)
    scaled = centred * inv_std
    return (scaled * gain_vec + shift_vec, scaled, inv_std)


def norm_back(grad_out, scaled, inv_std, gain_vec):
    grad_scaled = grad_out * gain_vec
    first_term = jnp.mean(grad_scaled, axis=-1, keepdims=True)
    second_term = jnp.mean(grad_scaled * scaled, axis=-1, keepdims=True)
    grad_in = inv_std * (grad_scaled - first_term - scaled * second_term)
    return (grad_in, jnp.sum(grad_out * scaled, axis=0), jnp.sum(grad_out, axis=0))


def gelu_both(inputs):
    cubic_term = inputs + GELU_A * inputs * inputs * inputs
    tangent = jnp.tanh(GELU_C * cubic_term)
    gelu_out = 0.5 * inputs * (1.0 + tangent)
    gelu_slope = 0.5 * (1.0 + tangent) + 0.5 * inputs * (1.0 - tangent * tangent) * GELU_C * (
        1.0 + 3.0 * GELU_A * inputs * inputs
    )
    return (gelu_out, gelu_slope)


def mm(eq, a, b):
    return jnp.einsum(eq, a, b, preferred_element_type=jnp.float32)


def layer(x_low, first, cot, weights, vectors):
    w_qkv, w_out, w_up, w_downt = weights
    g1, b1, qb, vb, ob, g2, b2, ub, db_ = vectors
    bf, f32 = jnp.bfloat16, jnp.float32
    rows = x_low.shape[0]
    x = x_low.astype(f32)
    normed, scaled_one, inv_one = layer_norm(x, g1, b1)
    hl = normed.astype(bf)
    mixed = mm("rd,dc->rc", hl, w_qkv)
    heads = lambda t: t.reshape(rows, HEADS, HEAD).transpose(1, 0, 2)
    q = heads((mixed[:, :D] + qb).astype(bf))
    k = heads(mixed[:, D : 2 * D].astype(bf))
    v = heads(jnp.concatenate([(mixed[:, 2 * D :] + vb).astype(bf), first], axis=1))
    scale = HEAD**-0.5
    s = mm("hqd,hkd->hqk", q, k) * scale
    at = jnp.arange(rows, dtype=jnp.int32)
    allowed = (at[None, :] <= at[:, None])[None]
    s = jnp.where(allowed, s, -BIG)
    top = jnp.max(s, axis=-1, keepdims=True)
    e = jnp.exp(s - top)
    prob = e / jnp.sum(e, axis=-1, keepdims=True)
    prob_low = prob.astype(bf)
    flat = lambda t: t.transpose(1, 0, 2).reshape(rows, D)
    ol = flat(mm("hqk,hkd->hqd", prob_low, v)).astype(bf)
    middle = x + (mm("rd,de->re", ol, w_out) + ob)
    n2, scaled_two, inv_two = layer_norm(middle, g2, b2)
    h2 = n2.astype(bf)
    u = mm("rd,df->rf", h2, w_up) + ub
    act, slope = gelu_both(u)
    act = act.astype(bf)
    out = (middle + (mm("rf,df->rd", act, w_downt) + db_)).astype(bf)
    dy = cot.astype(f32)
    g_downt = mm("rd,rf->df", cot, act)
    du = (mm("rd,df->rf", cot, w_downt) * slope).astype(bf)
    g_up = mm("rd,rf->df", h2, du)
    g_ub = jnp.sum(du.astype(f32), axis=0)
    dh2 = mm("rf,df->rd", du, w_up)
    dr, g_g2, g_b2 = norm_back(dh2, scaled_two, inv_two, g2)
    dmid = dy + dr
    dbr = dmid.astype(bf)
    g_ob = jnp.sum(dbr.astype(f32), axis=0)
    g_out = mm("rd,re->de", ol, dbr)
    do = heads(mm("re,de->rd", dbr, w_out).astype(bf))
    dp = mm("hqd,hkd->hqk", do, v)
    delta = jnp.sum(prob * dp, axis=-1, keepdims=True)
    ds = (prob * (dp - delta)).astype(bf)
    dq = flat(mm("hqk,hkd->hqd", ds, k) * scale).astype(bf)
    dk = flat(mm("hqk,hqd->hkd", ds, q) * scale).astype(bf)
    dv = flat(mm("hqk,hqd->hkd", prob_low, do)).astype(bf)
    dm = jnp.concatenate([dq, dk, dv[:, :VFRESH]], axis=1)
    g_qb = jnp.sum(dq.astype(f32), axis=0)
    g_vb = jnp.sum(dv[:, :VFRESH].astype(f32), axis=0)
    g_qkv = mm("rd,rc->dc", hl, dm)
    dh = mm("rc,dc->rd", dm, w_qkv)
    dr1, g_g1, g_b1 = norm_back(dh, scaled_one, inv_one, g1)
    dx = (dmid + dr1).astype(bf)
    grads = (g_qkv, g_out, g_up, g_downt)
    small = (g_g1, g_b1, g_qb, g_vb, g_ob, g_g2, g_b2, g_ub, jnp.sum(dy, axis=0))
    return out, dx, dv[:, VFRESH:], grads, small


def shards(
    plan, tokens, first_values, out_cot, ln1_gain, ln1_bias, w_qkv, q_bias, v_bias, w_out, out_bias,
    ln2_gain, ln2_bias, w_up, up_bias, w_down, down_bias,
):
    bf, f32 = jnp.bfloat16, jnp.float32
    R, C, n_mp, n_dp = plan.rows, plan.cols, plan.n_mp, plan.n_dp
    small = (ln1_gain, ln1_bias, q_bias, v_bias, out_bias, ln2_gain, ln2_bias, up_bias, down_bias)
    widths = [s.shape[0] for s in small]
    gap = lambda a, w: jnp.pad(a, ((0, 0), (0, w - a.shape[1])))
    row = jnp.concatenate(small)[None]
    packed = jnp.concatenate(
        [
            jnp.concatenate([gap(w_qkv, plan.out_at), gap(w_out, C - plan.out_at)], axis=1),
            w_up,
            w_down.T,
            jnp.pad(row, ((0, 15), (0, C - row.shape[1]))),
        ],
        axis=0,
    )
    g, x, f, y = gather(plan, packed, tokens, first_values, out_cot)

    def wide(lo, at, width):
        part = g[:, :, lo : lo + R, at : at + width]
        return part.reshape(n_mp, D, width).transpose(1, 0, 2).reshape(D, n_mp * width)

    weights = (
        wide(0, 0, plan.qkv),
        wide(0, plan.out_at, plan.out),
        wide(R, 0, C),
        wide(2 * R, 0, C),
    )
    vecs = g[:, :, 3 * R, :].astype(f32).transpose(1, 0, 2)
    ends = [sum(widths[:n]) for n in range(len(widths) + 1)]
    vectors = [vecs[:, :, a:b].reshape(-1) for a, b in zip(ends[:-1], ends[1:])]
    out, dx, dfirst, grads, small_grads = layer(
        x.reshape(SEQ, D), f.reshape(SEQ, -1), y.reshape(SEQ, D), weights, vectors
    )
    split = lambda a: a.astype(bf).reshape(n_dp, R, n_mp, -1).transpose(2, 0, 1, 3)
    gap4 = lambda a, w: jnp.pad(a, ((0, 0), (0, 0), (0, 0), (0, w - a.shape[3])))
    rows = jnp.concatenate([v.astype(bf).reshape(n_dp, n_mp, 1, -1) for v in small_grads], axis=3)
    rows = rows.transpose(1, 0, 2, 3)
    full = jnp.concatenate(
        [
            jnp.concatenate(
                [gap4(split(grads[0]), plan.out_at), gap4(split(grads[1]), C - plan.out_at)], axis=3
            ),
            split(grads[2]),
            split(grads[3]),
            jnp.pad(rows, ((0, 0), (0, 0), (0, 15), (0, C - rows.shape[3]))),
        ],
        axis=2,
    )
    total, r1, r2, r3 = reduce(
        plan,
        full,
        out.reshape(tokens.shape),
        dx.reshape(tokens.shape),
        dfirst.reshape(first_values.shape),
    )
    s = [total[3 * R, a:b] for a, b in zip(ends[:-1], ends[1:])]
    return (
        r1, r2, r3,
        s[0], s[1],
        total[:R, : plan.qkv],
        s[2], s[3],
        total[:R, plan.out_at : plan.out_at + plan.out],
        s[4], s[5], s[6],
        total[R : 2 * R],
        s[7],
        total[2 * R : 3 * R].T,
        s[8],
    )


def solution(mesh):
    plan = Plan(mesh)
    line = P(("dp", "mp"))
    rows = P(None, ("dp", "mp"), None)
    block = P("dp", "mp")
    grads = (line, line, block, line, line, block, line, line, line, block, line, P("mp", "dp"), line)
    return jax.shard_map(
        functools.partial(shards, plan),
        mesh=mesh,
        in_specs=(rows, rows, rows) + grads,
        out_specs=(rows, rows, rows) + grads,
        check_vma=False,
    )
```

time: 1560 us -> 470 us (0.30)
  waiting for transfers between devices: 895 us -> 0 us
  blocking collectives: 246 us -> 0 us
  Pallas kernels: 0 us -> 195 us
  matrix products: 165 us -> 96.9 us
  other arithmetic: 71.1 us -> 36.3 us
  between operations: 24.5 us -> 1.35 us
    reduce_scatter x28 -> x0, waiting for transfers between devices: 646 us -> none  [the longest x4 131 us: reduce_grads(): lax.psum_scatter(local_grads[9].astype(jnp.bfloat16), 'dp', scatter_dimen...]
    unnamed x50 -> x0, waiting for transfers between devices: 249 us -> none
    all_gather x19 -> x0, blocking collectives: 196 us -> none  [the longest x4 47 us: shards(): back_row_piece = lax.all_gather(cot_low, 'mp', axis=0, tiled=True)]
    pallas_call x0 -> x2, Pallas kernels: none -> 195 us  [the longest x1 103 us: reduce(): pl.pallas_call(functools.partial(reduce_kernel, plan), name='reduce', out...]
    dot_general x72 -> x17, matrix products: 165 us -> 89.3 us  [mm(): return jnp.einsum(eq, a, b, preferred_element_type=jnp.float32)]
    unnamed x472 -> x57, local copies, waits for them, and re-layouts: 78.2 us -> 7.65 us
    reshape x8 -> x20, local copies, waits for them, and re-layouts: 14.6 us -> 72.6 us  [the longest x6 40.8 us: shards(): a.astype(bf).reshape(n_dp, R, n_mp, -1).transpose(2, 0, 1, 3)]
    unnamed x3 -> x0, blocking collectives: 50.1 us -> none
  transfers between devices with their start and end apart: 41 -> 0, of which waited for: 31 -> 0; matrix products, arithmetic and copies ran while one was open for 18% -> 0% of each run, Pallas kernels for 0% -> 0%
where the time goes in v1:
time: 470 us; the launch traced here: 464 us
  Pallas kernels  195 us (41%)
  local copies, waits for them, and re-layouts  134 us (29%)
  matrix products  96.9 us (21%)
  other arithmetic  36.3 us (8%)
    pallas_call x1, Pallas kernels, reduce(): pl.pallas_call(functools.partial(reduce_kernel, plan), name='reduce', out...  103 us
    pallas_call x1, Pallas kernels, gather(): pl.pallas_call(functools.partial(gather_kernel, plan), name='gather', out...  91.6 us
    dot_general x17, matrix products, mm(): return jnp.einsum(eq, a, b, preferred_element_type=jnp.float32)  89.3 us
    reshape x6, local copies, waits for them, and re-layouts, shards(): a.astype(bf).reshape(n_dp, R, n_mp, -1).transpose(2, 0, 1, 3)  40.8 us
    reshape x4, local copies, waits for them, and re-layouts, wide(): part.reshape(n_mp, D, width).transpose(1, 0, 2).reshape(D, n_mp * width)  18.4 us
    reshape x10, local copies, waits for them, and re-layouts, shards(): v.astype(bf).reshape(n_dp, n_mp, 1, -1)  13.4 us
    slice x3, local copies, waits for them, and re-layouts, wide(): part = g[:, :, lo:lo + R, at:at + width]  11.8 us
    concatenate x1, other arithmetic, shards(): jnp.concatenate([jnp.concatenate([gap4(split(grads[0]), plan.out_at), gap...  11.3 us

profile of v1, /device:TPU:1, one launch (start us, length us, event | category | flops | bytes accessed | tf_op | source)
XLA Modules:
  0.0 463.5 jit_solution(15928415885796896444)
XLA Ops:
  0.6 6.1 %concatenate.30 = bf16[276]{0:T(512)(128)(2,1)S(1)} concatenate(bf16[24]{0:T(256)(128)(2,1)} %param.19, bf16[24]{0:T(256)(128)(2,1)} %param.20, bf16[24]{0:T(256)(128)(2,1)} %param.22, bf16[12]{0:T(256)(128)(2,1)} %param.23, bf16[24]{0:T(256)(128)(2,1)} %param.25, bf16[24]{0:T(256)(128)(2,1)} %param.26, bf16[24]{0:T(256)(128)(2,1)} %param.27, bf16[96]{0:T(256)(128)(2,1)} %param.29, ...), dimensions={0} | concatenate | bytes 1104 | tf_op jit(solution)/shard_map/concatenate | solution.py:454
  6.8 1.9 fusion.65.pk
  8.6 91.6 %gather.1 = (bf16[4,8,304,768]{3,2,1,0:T(8,128)(2,1)}, bf16[4,128,768]{2,1,0:T(8,128)(2,1)}, bf16[4,128,384]{2,1,0:T(8,128)(2,1)}, bf16[4,128,768]{2,1,0:T(8,128)(2,1)}) custom-call(bf16[304,768]{1,0:T(8,128)(2,1)} %fusion.65.pk, bf16[4,128,768]{2,1,0:T(8,128)(2,1)} %tok.1, bf16[4,128,384]{2,1,0:T(8,128)(2,1)} %fv.1, bf16[4,128,768]{2,1,0:T(8,128)(2,1)} %cot.1), custom_call_target="tpu_custom_call" | custom-call | tf_op jit(solution)/shard_map/gather/pallas_call | solution.py:169
  104.5 2.4 fusion.33
  106.8 2.2 slice.101
  109.0 3.1 copy.44
  112.1 5.9 %fusion.87 = f32[512,1920]{1,0:T(8,128)} fusion(bf16[512,768]{1,0:T(8,128)(2,1)} %bitcast.180, bf16[768,1920]{0,1:T(8,128)(2,1)} %bitcast.166), kind=kOutput, calls=%fused_computation.150 | convolution fusion | flops 1509949440 | bytes 7667712 | tf_op jit(solution)/shard_map/rd,dc->rc/dot_general | solution.py:381
  119.9 1.8 slice.163
  122.1 7.6 %fusion.83 = (f32[12,512]{1,0:T(8,128)S(1)}, f32[12,512,512]{1,2,0:T(8,128)}) fusion(pred[512,512]{0,1:T(8,128)(4,1)S(1)} %iota_compare_fusion.4, bf16[12,512,64]{1,2,0:T(8,128)(2,1)S(1)} %bitcast.176, bf16[12,512,64]{1,2,0:T(8,128)(2,1)S(1)} %bitcast.155), kind=kOutput, calls=%fused_computation.146 | convolution fusion | flops 415236608 | bytes 14442496 | tf_op jit(solution)/shard_map/sub | solution.py:403
  131.7 6.8 %fusion.47 = bf16[12,512,64]{1,2,0:T(8,128)(2,1)} fusion(bf16[512,6,64]{0,2,1:T(8,128)(2,1)S(1)} %concatenate.33, bf16[512,6,64]{0,2,1:T(8,128)(2,1)S(1)} %bitcast.185, f32[12,512,512]{1,2,0:T(8,128)} %get-tuple-element.70, f32[12,512]{1,0:T(8,128)S(1)} %get-tuple-element.69), kind=kOutput, calls=%fused_computation.84 | convolution fusion | flops 410910720 | bytes 14180352 | tf_op jit(solution)/shard_map/hqk,hkd->hqd/dot_general | solution.py:381
  138.7 1.6 slice.107
  141.8 2.4 fusion.84
  144.7 8.0 %fusion.80 = (bf16[4,8,96,768]{3,2,1,0:T(8,128)(2,1)}, bf16[4,8,96,768]{3,2,1,0:T(8,128)(2,1)}) fusion(bf16[4,8,304,768]{3,2,1,0:T(8,128)(2,1)} %get-tuple-element.25), kind=kLoop, calls=%fused_computation.143 | loop fusion | bytes 18874368 | tf_op jit(solution)/shard_map/slice | solution.py:467
  152.7 6.7 %copy.57 = bf16[4,768,768]{1,2,0:T(8,128)(2,1)} copy(bf16[4,768,768]{2,1,0:T(8,128)(2,1)} %bitcast.150) | data formatting | bytes 9437184 | tf_op jit(solution)/shard_map/reshape | solution.py:468
  159.4 7.1 %fusion.79 = f32[512,3072]{1,0:T(8,128)} fusion(bf16[768,3072]{0,1:T(8,128)(2,1)} %bitcast.159, f32[512,768]{1,0:T(8,128)S(1)} %get-tuple-element.72, f32[768]{0:T(1024)S(1)} %add.147, f32[768]{0:T(1024)S(1)} %mul.191, f32[512]{0:T(512)S(1)} %add_rsqrt_fusion, f32[512]{0:T(512)S(1)} %broadcast_multiply_fusion.4), kind=kOutput, calls=%fused_computation.142 | convolution fusion | flops 2417885184 | bytes 12593152 | tf_op jit(solution)/shard_map/rd,df->rf/dot_general | solution.py:381
  166.8 7.1 %copy.54 = bf16[4,768,768]{1,2,0:T(8,128)(2,1)} copy(bf16[4,768,768]{2,1,0:T(8,128)(2,1)} %bitcast.149) | data formatting | bytes 9437184 | tf_op jit(solution)/shard_map/reshape | solution.py:468
  173.9 9.1 %add_convert_fusion = bf16[512,768]{1,0:T(8,128)(2,1)} fusion(f32[512,768]{1,0:T(8,128)S(1)} %get-tuple-element.72, bf16[768,3072]{0,1:T(8,128)(2,1)} %bitcast.161, f32[768]{0:T(1024)S(1)} %add.158, f32[512,3072]{1,0:T(8,128)} %fusion.79, f32[3072]{0:T(1024)S(1)} %add.150), kind=kOutput, calls=%fused_computation.73 | convolution fusion | flops 2432827392 | bytes 13384704 | tf_op jit(solution)/shard_map/rf,df->rd/dot_general | solution.py:381
  183.1 6.8 %fusion.86 = (bf16[3072]{0:T(1024)(128)(2,1)}, bf16[512,3072]{1,0:T(8,128)(2,1)S(1)}) fusion(f32[512,3072]{1,0:T(8,128)S(1)} %copy-done.20, f32[3072]{0:T(1024)S(1)} %add.150, bf16[512,768]{1,0:T(8,128)(2,1)S(1)} %bitcast.165, bf16[768,3072]{0,1:T(8,128)(2,1)S(1)} %bitcast.162), kind=kOutput, calls=%fused_computation.149 | convolution fusion | flops 2448946176 | bytes 14960640 | tf_op jit(solution)/shard_map/rd,df->rf/dot_general | solution.py:381
  189.8 1.7 copy-done.21
  191.6 4.8 %convolution_convert_fusion.1 = bf16[768,3072]{1,0:T(8,128)(2,1)} fusion(bf16[512,3072]{1,0:T(8,128)(2,1)S(1)} %get-tuple-element.80, f32[512,768]{1,0:T(8,128)S(1)} %get-tuple-element.72, f32[768]{0:T(1024)S(1)} %add.147, f32[768]{0:T(1024)S(1)} %mul.191, f32[512]{0:T(512)S(1)} %add_rsqrt_fusion, f32[512]{0:T(512)S(1)} %broadcast_multiply_fusion.4), kind=kOutput, calls=%fused_computation.36 | convolution fusion | flops 2420244480 | bytes 9447424 | tf_op jit(solution)/shard_map/rd,rf->df/dot_general | solution.py:381
  196.4 9.7 %reshape.292 = bf16[8,96,4,768]{3,2,1,0:T(4,128)(2,1)} reshape(bf16[768,3072]{1,0:T(8,128)(2,1)} %convolution_convert_fusion.1) | data formatting | bytes 9437184 | tf_op jit(solution)/shard_map/reshape | solution.py:482
  206.1 8.3 %convolution_convert_fusion = bf16[768,3072]{1,0:T(8,128)(2,1)} fusion(bf16[512,768]{1,0:T(8,128)(2,1)} %bitcast.164, f32[512,3072]{1,0:T(8,128)} %fusion.79, f32[3072]{0:T(1024)S(1)} %add.150), kind=kOutput, calls=%fused_computation.35 | convolution fusion | flops 2434007040 | bytes 11808768 | tf_op jit(solution)/shard_map/rd,rf->df/dot_general | solution.py:381
  214.5 9.9 %reshape.293 = bf16[8,96,4,768]{3,2,1,0:T(4,128)(2,1)} reshape(bf16[768,3072]{1,0:T(8,128)(2,1)} %convolution_convert_fusion) | data formatting | bytes 9437184 | tf_op jit(solution)/shard_map/reshape | solution.py:482
  224.3 9.2 %copy_bitcast_fusion = (bf16[4,8,96,768]{3,2,1,0:T(8,128)(2,1)}, bf16[4,8,96,768]{3,2,1,0:T(8,128)(2,1)}) fusion(bf16[8,96,4,768]{3,2,1,0:T(4,128)(2,1)} %reshape.293, bf16[8,96,4,768]{3,2,1,0:T(4,128)(2,1)} %reshape.292), kind=kLoop, calls=%fused_computation.37 | loop fusion | bytes 18874368 | tf_op jit(solution)/shard_map/transpose | solution.py:482
  233.6 5.9 %multiply_reduce_fusion.1 = (bf16[768]{0:T(1024)(128)(2,1)}, f32[512]{0:T(512)S(1)}, f32[512]{0:T(512)S(1)}, bf16[768]{0:T(1024)(128)(2,1)}, f32[512,768]{1,0:T(8,128)S(1)}) fusion(f32[512,768]{1,0:T(8,128)S(1)} %get-tuple-element.72, f32[512]{0:T(512)S(1)} %add_rsqrt_fusion, f32[512]{0:T(512)S(1)} %broadcast_multiply_fusion.4, f32[768]{0:T(1024)S(1)} %mul.191, ...), kind=kOutput, calls=%fused_computation.74 | convolution fusion | flops 2419455488 | bytes 11024384 | tf_op jit(solution)/shard_map/rf,df->rd/dot_general | solution.py:381
  239.5 2.7 convert_reduce_fusion.1
  242.3 1.7 convolution_convert_fusion.4
  243.9 2.3 copy.59
  246.3 11.9 %multiply_reduce_fusion = (f32[12,512]{1,0:T(8,128)S(1)}, f32[12,512,512]{1,2,0:T(8,128)}) fusion(f32[12,512,512]{1,2,0:T(8,128)} %get-tuple-element.70, f32[12,512]{1,0:T(8,128)} %copy-done.17, bf16[12,512,64]{1,2,0:T(8,128)(2,1)} %bitcast.178, bf16[512,6,64]{0,2,1:T(8,128)(2,1)} %copy-done.14, bf16[512,6,64]{0,2,1:T(8,128)(2,1)S(1)} %bitcast.186), kind=kOutput, calls=%fused_computation.17 | convolution fusion | flops 412477440 | bytes 26787840 | tf_op jit(solution)/shard_map/hqd,hkd->hqk/dot_general | solution.py:381
  258.2 6.9 %multiply_convert_fusion = bf16[12,512,512]{1,2,0:T(8,128)(2,1)S(1)} fusion(f32[12,512,512]{1,2,0:T(8,128)} %get-tuple-element.75, f32[12,512]{1,0:T(8,128)S(1)} %get-tuple-element.74, f32[12,512,512]{1,2,0:T(8,128)S(1)} %bitcast.153, f32[12,512]{1,0:T(8,128)S(1)} %copy-done.18), kind=kLoop, calls=%fused_computation.16 | loop fusion | flops 12582912 | bytes 31506432 | tf_op jit(solution)/shard_map/convert_element_type | solution.py:429
  265.2 1.8 fusion.85
  267.0 2.0 multiply_convert_fusion.2
  269.0 6.8 %fusion.50 = bf16[12,512,64]{1,2,0:T(8,128)(2,1)S(1)} fusion(bf16[12,512,64]{1,2,0:T(8,128)(2,1)S(1)} %bitcast.179, f32[12,512,512]{1,2,0:T(8,128)} %get-tuple-element.70, f32[12,512]{1,0:T(8,128)S(1)} %copy-done.18), kind=kOutput, calls=%fused_computation.85 | convolution fusion | flops 409337856 | bytes 14180352 | tf_op jit(solution)/shard_map/hqk,hqd->hkd/dot_general | solution.py:381
  276.5 2.8 fusion.42
  280.8 3.4 convolution_convert_fusion.2
  284.2 9.2 %reshape.290 = bf16[8,96,4,480]{3,2,1,0:T(4,128)(2,1)} reshape(bf16[768,1920]{1,0:T(8,128)(2,1)} %convolution_convert_fusion.2) | data formatting | bytes 5898240 | tf_op jit(solution)/shard_map/reshape | solution.py:482
  293.4 4.3 copy.92
  297.8 1.8 convolution_convert_fusion.3
  299.6 4.8 %reshape.304 = bf16[8,96,4,192]{3,2,1,0:T(4,128)(2,1)} reshape(bf16[768,768]{1,0:T(8,128)(2,1)} %convolution_convert_fusion.3) | data formatting | bytes 2359296 | tf_op jit(solution)/shard_map/reshape | solution.py:482
  304.4 2.8 copy.93
  327.4 1.9 reduce_sum.202
  332.0 1.9 concatenate.37
  333.8 11.3 %fusion.8.grads = bf16[4,8,304,768]{3,2,1,0:T(8,128)(2,1)} fusion(bf16[4,8,1,276]{3,2,1,0:T(2,128)(2,1)} %bitcast.187, bf16[4,8,96,192]{3,2,1,0:T(8,128)(2,1)} %bitcast.158, bf16[4,8,96,480]{3,2,1,0:T(8,128)(2,1)S(1)} %bitcast.154, bf16[4,8,96,768]{3,2,1,0:T(8,128)(2,1)} %get-tuple-element.83, bf16[4,8,96,768]{3,2,1,0:T(8,128)(2,1)} %get-tuple-element.84), kind=kLoop, calls=%fused_computation.12 | loop fusion | flops 156893184 | bytes 28525824 | tf_op jit(solution)/shard_map/concatenate | solution.py:486
  346.0 103.3 %reduce.11 = (f32[304,768]{1,0:T(8,128)}, bf16[4,128,768]{2,1,0:T(8,128)(2,1)}, bf16[4,128,768]{2,1,0:T(8,128)(2,1)}, bf16[4,128,384]{2,1,0:T(8,128)(2,1)}) custom-call(bf16[4,8,304,768]{3,2,1,0:T(8,128)(2,1)} %fusion.8.grads, bf16[4,128,768]{2,1,0:T(8,128)(2,1)} %bitcast.173, bf16[4,128,768]{2,1,0:T(8,128)(2,1)} %bitcast.163, bf16[4,128,384]{2,1,0:T(8,128)(2,1)} %bitcast.170), custom_call_target="tpu_custom_call" | custom-call | tf_op jit(solution)/shard_map/reduce/pallas_call | solution.py:321
  449.3 2.0 slice_bitcast_fusion
  451.2 1.6 slice.119
  458.4 2.1 copy.98
  460.4 2.1 copy.99
  (121 shorter events, 43.1 us)
Async XLA Ops:
  119.9 9.8 %copy-start.9 = (bf16[512,768]{0,1:T(8,128)(2,1)}, bf16[512,768]{0,1:T(8,128)(2,1)S(1)}, u32[]{:S(2)}) copy-start(bf16[512,768]{0,1:T(8,128)(2,1)S(1)} %copy.46) | copy-start | bytes 2359300
  122.1 9.2 %copy-start.15 = (bf16[4,128,384]{2,1,0:T(8,128)(2,1)S(1)}, bf16[4,128,384]{2,1,0:T(8,128)(2,1)}, u32[]{:S(2)}) copy-start(bf16[4,128,384]{2,1,0:T(8,128)(2,1)} %get-tuple-element.27) | copy-start | bytes 1179652
  129.7 2.0 copy-start.17
  131.3 7.3 %copy-start.12 = (bf16[512,384]{0,1:T(8,128)(2,1)}, bf16[512,384]{0,1:T(8,128)(2,1)S(1)}, u32[]{:S(2)}) copy-start(bf16[512,384]{0,1:T(8,128)(2,1)S(1)} %copy.49) | copy-start | bytes 1179652
  131.7 6.8 %copy-start.14 = (bf16[512,6,64]{0,2,1:T(8,128)(2,1)}, bf16[512,6,64]{0,2,1:T(8,128)(2,1)S(1)}, u32[]{:S(2)}) copy-start(bf16[512,6,64]{0,2,1:T(8,128)(2,1)S(1)} %concatenate.33) | copy-start | bytes 1179652
  138.6 3.2 copy-start
  144.2 89.4 %copy-start.2 = (f32[512,768]{1,0:T(8,128)}, f32[512,768]{1,0:T(8,128)S(1)}, u32[]{:S(2)}) copy-start(f32[512,768]{1,0:T(8,128)S(1)} %get-tuple-element.72) | copy-start | bytes 4718596
  173.9 9.2 %copy-start.3 = (bf16[4,768,768]{1,2,0:T(8,128)(2,1)S(1)}, bf16[4,768,768]{1,2,0:T(8,128)(2,1)}, u32[]{:S(2)}) copy-start(bf16[4,768,768]{1,2,0:T(8,128)(2,1)} %copy.54) | copy-start | bytes 14155780
  173.9 9.2 %copy-start.4 = (bf16[4,128,768]{2,1,0:T(8,128)(2,1)S(1)}, bf16[4,128,768]{2,1,0:T(8,128)(2,1)}, u32[]{:S(2)}) copy-start(bf16[4,128,768]{2,1,0:T(8,128)(2,1)} %get-tuple-element.26) | copy-start | bytes 2359300
  173.9 9.1 %copy-start.20 = (f32[512,3072]{1,0:T(8,128)S(1)}, f32[512,3072]{1,0:T(8,128)}, u32[]{:S(2)}) copy-start(f32[512,3072]{1,0:T(8,128)} %fusion.79) | copy-start | bytes 18874372
  189.8 1.8 copy-start.21
  224.3 9.2 %copy-start.22 = (bf16[512,3072]{1,0:T(8,128)(2,1)S(1)}, bf16[512,3072]{1,0:T(8,128)(2,1)}, u32[]{:S(2)}) copy-start(bf16[512,3072]{1,0:T(8,128)(2,1)} %copy-done.21) | copy-start | bytes 9437188
  233.6 6.0 %copy-start.5 = (bf16[4,128,768]{2,1,0:T(8,128)(2,1)S(1)}, bf16[4,128,768]{2,1,0:T(8,128)(2,1)}, u32[]{:S(2)}) copy-start(bf16[4,128,768]{2,1,0:T(8,128)(2,1)} %get-tuple-element.26) | copy-start | bytes 2359300
  239.5 2.7 copy-start.7
  242.2 4.0 copy-start.13
  246.3 11.9 %slice-start = ((s8[12582912]{0:T(1024)(128)(4,1)}), s8[4194304]{0:T(1024)(128)(4,1)S(1)}, s32[]{:S(2)}) async-start(s8[12582912]{0:T(1024)(128)(4,1)} %bitcast.152), calls=%async_computation | async-start | bytes 8388608
  246.3 11.9 %slice-start.1 = ((s8[12582912]{0:T(1024)(128)(4,1)}), s8[4194304]{0:T(1024)(128)(4,1)S(1)}, s32[]{:S(2)}) async-start(s8[12582912]{0:T(1024)(128)(4,1)} %bitcast.152), calls=%async_computation.1 | async-start | bytes 8388608
  246.3 11.9 %slice-start.2 = ((s8[12582912]{0:T(1024)(128)(4,1)}), s8[4194304]{0:T(1024)(128)(4,1)S(1)}, s32[]{:S(2)}) async-start(s8[12582912]{0:T(1024)(128)(4,1)} %bitcast.152), calls=%async_computation.2 | async-start | bytes 8388608
  246.3 11.9 %copy-start.18 = (f32[12,512]{1,0:T(8,128)S(1)}, f32[12,512]{1,0:T(8,128)}, u32[]{:S(2)}) copy-start(f32[12,512]{1,0:T(8,128)} %copy-done.17) | copy-start | bytes 73732
  265.2 1.8 copy-start.10
  266.9 2.0 copy-start.11
  269.0 7.5 %copy-start.6 = (bf16[4,768,480]{1,2,0:T(8,128)(2,1)S(1)}, bf16[4,768,480]{1,2,0:T(8,128)(2,1)}, u32[]{:S(2)}) copy-start(bf16[4,768,480]{1,2,0:T(8,128)(2,1)} %copy.44) | copy-start | bytes 8847364
  293.4 4.3 copy-start.8
  297.8 9.5 %copy-start.19 = (bf16[768]{0:T(1024)(128)(2,1)S(1)}, bf16[768]{0:T(1024)(128)(2,1)}, u32[]{:S(2)}) copy-start(bf16[768]{0:T(1024)(128)(2,1)} %get-tuple-element.35) | copy-start | bytes 4612
  299.6 34.2 %copy-start.1 = (bf16[8,96,4,480]{3,1,0,2:T(8,128)(2,1)S(1)}, bf16[8,96,4,480]{3,1,0,2:T(8,128)(2,1)}, u32[]{:S(2)}) copy-start(bf16[8,96,4,480]{3,1,0,2:T(8,128)(2,1)} %copy.92) | copy-start | bytes 8847364
  449.3 13.2 %copy-start.16 = (bf16[4,128,384]{2,1,0:T(8,128)(2,1)S(1)}, bf16[4,128,384]{2,1,0:T(8,128)(2,1)}, u32[]{:S(2)}) copy-start(bf16[4,128,384]{2,1,0:T(8,128)(2,1)} %get-tuple-element.103) | copy-start | bytes 1179652

commit v2 on v1

--- a/solution.py
+++ b/solution.py
@@ -2,6 +2,7 @@
 
 import jax
 import jax.numpy as jnp
+import numpy as np
 from jax import lax
 from jax.experimental import pallas as pl
 from jax.experimental.pallas import tpu as pltpu
@@ -350,150 +351,330 @@
     )(grads, o1, o2, o3)
 
 
-def layer_norm(inputs, gain_vec, shift_vec):
-    average = jnp.mean(inputs, axis=-1, keepdims=True)
-    centred = inputs - average
+WIDE = (0, 1, 2, 4, 5, 6, 8)
+V_BIAS, UP_BIAS = 3, 7
+G1, B1, QB, OB, G2, B2, DB = WIDE
+
+
+def dot(a, b):
+    return jnp.dot(a, b, preferred_element_type=jnp.float32)
+
+
+def dot_nt(a, b):
+    return lax.dot_general(a, b, (((1,), (1,)), ((), ())), preferred_element_type=jnp.float32)
+
+
+def chunks(rows, step, body):
+    @pl.loop(0, rows // step)
+    def _(at):
+        body(pl.ds(pl.multiple_of(at * step, step), step))
+
+
+def norm_stats(r):
+    average = jnp.mean(r, axis=-1, keepdims=True)
+    centred = r - average
     variance = jnp.mean(centred * centred, axis=-1, keepdims=True)
     inv_std = lax.rsqrt(variance + EPS)
-    scaled = centred * inv_std
-    return (scaled * gain_vec + shift_vec, scaled, inv_std)
-
-
-def norm_back(grad_out, scaled, inv_std, gain_vec):
-    grad_scaled = grad_out * gain_vec
-    first_term = jnp.mean(grad_scaled, axis=-1, keepdims=True)
-    second_term = jnp.mean(grad_scaled * scaled, axis=-1, keepdims=True)
-    grad_in = inv_std * (grad_scaled - first_term - scaled * second_term)
-    return (grad_in, jnp.sum(grad_out * scaled, axis=0), jnp.sum(grad_out, axis=0))
-
-
-def gelu_both(inputs):
-    cubic_term = inputs + GELU_A * inputs * inputs * inputs
-    tangent = jnp.tanh(GELU_C * cubic_term)
-    gelu_out = 0.5 * inputs * (1.0 + tangent)
-    gelu_slope = 0.5 * (1.0 + tangent) + 0.5 * inputs * (1.0 - tangent * tangent) * GELU_C * (
-        1.0 + 3.0 * GELU_A * inputs * inputs
-    )
-    return (gelu_out, gelu_slope)
-
-
-def mm(eq, a, b):
-    return jnp.einsum(eq, a, b, preferred_element_type=jnp.float32)
-
-
-def layer(x_low, first, cot, weights, vectors):
-    w_qkv, w_out, w_up, w_downt = weights
-    g1, b1, qb, vb, ob, g2, b2, ub, db_ = vectors
+    return centred * inv_std, inv_std
+
+
+def norm_back(grad_out, scaled, inv_std, gain):
+    e = grad_out * gain
+    first = jnp.mean(e, axis=-1, keepdims=True)
+    second = jnp.mean(e * scaled, axis=-1, keepdims=True)
+    return inv_std * (e - first - scaled * second)
+
+
+def layer_kernel(
+    plan, tab, dev, x_ref, f_ref, y_ref, g_hbm, out_ref, dx_ref, df_ref, gr,
+    w, wq, wo, sv, vec, ub, hl, hlt, qkv, ot, otb, lse, mid, n2, inv2, h2, h2t, yt,
+    big, acc, act, du, do, dm, dv, dk, dqt, sums, ubg, sem,
+):
     bf, f32 = jnp.bfloat16, jnp.float32
-    rows = x_low.shape[0]
-    x = x_low.astype(f32)
-    normed, scaled_one, inv_one = layer_norm(x, g1, b1)
-    hl = normed.astype(bf)
-    mixed = mm("rd,dc->rc", hl, w_qkv)
-    heads = lambda t: t.reshape(rows, HEADS, HEAD).transpose(1, 0, 2)
-    q = heads((mixed[:, :D] + qb).astype(bf))
-    k = heads(mixed[:, D : 2 * D].astype(bf))
-    v = heads(jnp.concatenate([(mixed[:, 2 * D :] + vb).astype(bf), first], axis=1))
-    scale = HEAD**-0.5
-    s = mm("hqd,hkd->hqk", q, k) * scale
-    at = jnp.arange(rows, dtype=jnp.int32)
-    allowed = (at[None, :] <= at[:, None])[None]
-    s = jnp.where(allowed, s, -BIG)
-    top = jnp.max(s, axis=-1, keepdims=True)
-    e = jnp.exp(s - top)
-    prob = e / jnp.sum(e, axis=-1, keepdims=True)
-    prob_low = prob.astype(bf)
-    flat = lambda t: t.transpose(1, 0, 2).reshape(rows, D)
-    ol = flat(mm("hqk,hkd->hqd", prob_low, v)).astype(bf)
-    middle = x + (mm("rd,de->re", ol, w_out) + ob)
-    n2, scaled_two, inv_two = layer_norm(middle, g2, b2)
-    h2 = n2.astype(bf)
-    u = mm("rd,df->rf", h2, w_up) + ub
-    act, slope = gelu_both(u)
-    act = act.astype(bf)
-    out = (middle + (mm("rf,df->rd", act, w_downt) + db_)).astype(bf)
-    dy = cot.astype(f32)
-    g_downt = mm("rd,rf->df", cot, act)
-    du = (mm("rd,df->rf", cot, w_downt) * slope).astype(bf)
-    g_up = mm("rd,rf->df", h2, du)
-    g_ub = jnp.sum(du.astype(f32), axis=0)
-    dh2 = mm("rf,df->rd", du, w_up)
-    dr, g_g2, g_b2 = norm_back(dh2, scaled_two, inv_two, g2)
-    dmid = dy + dr
-    dbr = dmid.astype(bf)
-    g_ob = jnp.sum(dbr.astype(f32), axis=0)
-    g_out = mm("rd,re->de", ol, dbr)
-    do = heads(mm("re,de->rd", dbr, w_out).astype(bf))
-    dp = mm("hqd,hkd->hqk", do, v)
-    delta = jnp.sum(prob * dp, axis=-1, keepdims=True)
-    ds = (prob * (dp - delta)).astype(bf)
-    dq = flat(mm("hqk,hkd->hqd", ds, k) * scale).astype(bf)
-    dk = flat(mm("hqk,hqd->hkd", ds, q) * scale).astype(bf)
-    dv = flat(mm("hqk,hqd->hkd", prob_low, do)).astype(bf)
-    dm = jnp.concatenate([dq, dk, dv[:, :VFRESH]], axis=1)
-    g_qb = jnp.sum(dq.astype(f32), axis=0)
-    g_vb = jnp.sum(dv[:, :VFRESH].astype(f32), axis=0)
-    g_qkv = mm("rd,rc->dc", hl, dm)
-    dh = mm("rc,dc->rd", dm, w_qkv)
-    dr1, g_g1, g_b1 = norm_back(dh, scaled_one, inv_one, g1)
-    dx = (dmid + dr1).astype(bf)
-    grads = (g_qkv, g_out, g_up, g_downt)
-    small = (g_g1, g_b1, g_qb, g_vb, g_ob, g_g2, g_b2, g_ub, jnp.sum(dy, axis=0))
-    return out, dx, dv[:, VFRESH:], grads, small
+    R, C, n_mp, n_dp = plan.rows, plan.cols, plan.n_mp, plan.n_dp
+    n = n_mp * n_dp
+    spr = C // 128
+    load = pltpu.make_async_copy(g_hbm, w, sem)
+    load.start()
+    load.wait()
+    step = 64
+
+    def panel(j, at):
+        return w[j, :, at * R : (at + 1) * R, :].reshape(D, C)
+
+    for r in range(-(-9 // spr)):
+        for j in range(n_mp):
+            for d in range(n_dp):
+                at = j * n_dp + d
+                sv[r, at : at + 1, :] = w[j, d, 3 * R + r : 3 * R + r + 1, :].astype(f32)
+    rowdev = dev[:, 0:1]
+    lanes = lambda v: slice((v % spr) * 128, (v % spr) * 128 + 128)
+    onehot = lambda t, width: (lax.broadcasted_iota(jnp.int32, (128, width), 0) == tab[t : t + 1, :width]).astype(bf)
+
+    def expand(v, e, owner):
+        got = dot(sv[v // spr, :, lanes(v)].astype(bf), e)
+        return jnp.sum(jnp.where(owner == rowdev, got, 0.0), axis=0, keepdims=True)
+
+    e24 = onehot(0, D)
+    for v in WIDE:
+        vec[v : v + 1, :] = expand(v, e24, tab[1:2, :])
+    vec[V_BIAS : V_BIAS + 1, :] = expand(V_BIAS, onehot(2, D), tab[3:4, :])
+    e96 = onehot(4, C)
+    for j in range(n_mp):
+        ub[j : j + 1, :] = expand(UP_BIAS, e96, tab[5:6, :C] + j * n_dp)
+    row = lambda v: vec[v : v + 1, :]
+
+    for j in range(n_mp):
+        for d in range(n_dp):
+            rows = slice(d * R, (d + 1) * R)
+            wq[rows, j * plan.qkv : (j + 1) * plan.qkv] = w[j, d, 0:R, 0 : plan.qkv]
+            wo[rows, j * plan.out : (j + 1) * plan.out] = w[j, d, 0:R, plan.out_at : plan.out_at + plan.out]
+
+    def first_norm(at):
+        n1, _ = norm_stats(x_ref[at, :].astype(f32))
+        hl[at, :] = (n1 * row(G1) + row(B1)).astype(bf)
+
+    chunks(SEQ, step, first_norm)
+    hlt[...] = hl[...].T
+    yt[...] = y_ref[...].T
+
+    def project(at):
+        h = hl[at, :]
+        q = dot(h, wq[:, 0:D]) + row(QB)
+        qkv[at, 0:D] = q.astype(bf) * 0.125
+        qkv[at, D : 2 * D] = dot(h, wq[:, D : 2 * D]).astype(bf)
+        v = dot(h, wq[:, 2 * D : QKV]) + row(V_BIAS)[:, :VFRESH]
+        qkv[at, 2 * D : QKV] = v.astype(bf)
+        qkv[at, QKV : 3 * D] = f_ref[at, :]
+
+    chunks(SEQ, 256, project)
+
+    B = 256
+    head_of = lax.broadcasted_iota(jnp.int32, (1, 128), 1) // HEAD
+    keep = lax.broadcasted_iota(jnp.int32, (B, B), 0) <= lax.broadcasted_iota(jnp.int32, (B, B), 1)
+
+    def scores(k2, qm, at):
+        s = dot_nt(k2, qm)
+        last = jnp.where(keep, s[at * B :, :], -BIG)
+        return last if at == 0 else jnp.concatenate([s[: at * B, :], last], axis=0)
+
+    @pl.loop(0, HEADS // 2)
+    def _(t):
+        cols = lambda base: pl.ds(pl.multiple_of(base + t * 128, 128), 128)
+        vt = qkv[:, cols(2 * D)].T
+        for e in range(2):
+            mask = (head_of == e).astype(bf)
+            for at in range(SEQ // B):
+                kk = (at + 1) * B
+                span = slice(at * B, kk)
+                s = scores(qkv[0:kk, cols(D)], qkv[span, cols(0)] * mask, at)
+                top = jnp.max(s, axis=0, keepdims=True)
+                ex = jnp.exp(s - top)
+                total = jnp.sum(ex, axis=0, keepdims=True)
+                o = dot(vt[e * HEAD : (e + 1) * HEAD, 0:kk], ex.astype(bf)) / total
+                ot[pl.ds(pl.multiple_of(t * 128 + e * HEAD, HEAD), HEAD), span] = o
+                lse[t, e : e + 1, span] = top + jnp.log(total)
+
+    otb[...] = ot[...].astype(bf)
+    du[:, 0:D] = otb[...].T
+
+    def second_norm(at):
+        m = x_ref[at, :].astype(f32) + (dot(du[at, 0:D], wo[...]) + row(OB))
+        mid[at, :] = m
+        scaled, inv = norm_stats(m)
+        n2[at, :] = scaled
+        inv2[at, :] = jnp.broadcast_to(inv, (B, 128))
+        h2[at, :] = (scaled * row(G2) + row(B2)).astype(bf)
+
+    chunks(SEQ, B, second_norm)
+    h2t[...] = h2[...].T
+    acc[...] = jnp.zeros_like(acc)
+    big[...] = jnp.zeros_like(big)
+
+    @pl.loop(0, n_mp)
+    def _(j):
+        bias = ub[pl.ds(j, 1), :]
+
+        def rows(at):
+            up, down = panel(j, 1), panel(j, 2)
+            u = dot(h2[at, :], up) + bias
+            u2 = u * u
+            tangent = jnp.tanh(GELU_C * (u + GELU_A * u2 * u))
+            half = 0.5 * (1.0 + tangent)
+            a = (u * half).astype(bf)
+            slope = half + 0.5 * u * (1.0 - tangent * tangent) * GELU_C * (1.0 + 3.0 * GELU_A * u2)
+            act[at, :] = a
+            acc[at, :] += dot_nt(a, down)
+            g = (dot(y_ref[at, :], down) * slope).astype(bf)
+            du[at, 0:C] = g
+            big[at, :] += dot_nt(g, up)
+
+        chunks(SEQ, 128, rows)
+        gr[j, :, 2 * R : 3 * R, :] = dot(yt[...], act[...]).astype(bf).reshape(n_dp, R, C)
+        gr[j, :, R : 2 * R, :] = dot(h2t[...], du[:, 0:C]).astype(bf).reshape(n_dp, R, C)
+        ubg[pl.ds(j, 1), :] = jnp.sum(du[:, 0:C].astype(f32), axis=0, keepdims=True)
+
+    sums[...] = jnp.zeros_like(sums)
+
+    def second_back(at):
+        out_ref[at, :] = (mid[at, :] + (acc[at, :] + row(DB))).astype(bf)
+        dh = big[at, :]
+        dy = y_ref[at, :].astype(f32)
+        scaled = n2[at, :]
+        dr = norm_back(dh, scaled, inv2[at, 0:1], row(G2))
+        dmid = dy + dr
+        mid[at, :] = dmid
+        low = dmid.astype(bf)
+        du[at, 0:D] = low
+        total = lambda a: jnp.sum(a, axis=0, keepdims=True)
+        sums[G2 : G2 + 1, :] += total(dh * scaled)
+        sums[B2 : B2 + 1, :] += total(dh)
+        sums[OB : OB + 1, :] += total(low.astype(f32))
+        sums[DB : DB + 1, :] += total(dy)
+
+    chunks(SEQ, step, second_back)
+    for j in range(n_mp):
+        g = dot(otb[...], du[:, j * plan.out : (j + 1) * plan.out]).astype(bf)
+        gr[j, :, 0:R, plan.out_at : plan.out_at + plan.out] = g.reshape(n_dp, R, plan.out)
+
+    def out_back(at):
+        do[at, :] = dot_nt(du[at, 0:D], wo[...]).astype(bf)
+
+    chunks(SEQ, B, out_back)
+
+    @pl.loop(0, HEADS // 2)
+    def _(t):
+        cols = lambda base: pl.ds(pl.multiple_of(base + t * 128, 128), 128)
+        kt = qkv[:, cols(D)].T
+        dot_ = do[:, cols(0)].astype(f32).T
+        prod = dot_ * ot[cols(0), :]
+        dv[...] = jnp.zeros_like(dv)
+        dk[...] = jnp.zeros_like(dk)
+        for e in range(2):
+            mask = (head_of == e).astype(bf)
+            delta = jnp.sum(prod[e * HEAD : (e + 1) * HEAD, :], axis=0, keepdims=True)
+            for at in range(SEQ // B):
+                kk = (at + 1) * B
+                span = slice(at * B, kk)
+                qm = qkv[span, cols(0)] * mask
+                dom = do[span, cols(0)] * mask
+                s = scores(qkv[0:kk, cols(D)], qm, at)
+                p = jnp.exp(s - lse[t, e : e + 1, span])
+                dp = dot_nt(qkv[0:kk, cols(2 * D)], dom)
+                ds = (p * (dp - delta[:, span])).astype(bf)
+                dv[0:kk, :] += dot(p.astype(bf), dom)
+                dk[0:kk, :] += dot(ds, qm)
+                dqt[e * HEAD : (e + 1) * HEAD, span] = dot(kt[e * HEAD : (e + 1) * HEAD, 0:kk], ds)
+        dm[:, cols(0)] = (dqt[...].T * 0.125).astype(bf)
+        dm[:, cols(D)] = dk[...].astype(bf)
+        dm[:, cols(2 * D)] = dv[...].astype(bf)
+
+    df_ref[...] = dm[:, QKV : 3 * D]
+    for j in range(n_mp):
+        g = dot(hlt[...], dm[:, j * plan.qkv : (j + 1) * plan.qkv]).astype(bf)
+        gr[j, :, 0:R, 0 : plan.qkv] = g.reshape(n_dp, R, plan.qkv)
+
+    def project_back(at):
+        acc[at, :] = dot_nt(dm[at, 0:QKV], wq[...])
+
+    chunks(SEQ, B, project_back)
+
+    def first_back(at):
+        n1, inv = norm_stats(x_ref[at, :].astype(f32))
+        dh = acc[at, :]
+        dr = norm_back(dh, n1, inv, row(G1))
+        dx_ref[at, :] = (mid[at, :] + dr).astype(bf)
+        total = lambda a: jnp.sum(a, axis=0, keepdims=True)
+        sums[G1 : G1 + 1, :] += total(dh * n1)
+        sums[B1 : B1 + 1, :] += total(dh)
+        sums[QB : QB + 1, :] += total(dm[at, 0:D].astype(f32))
+        sums[V_BIAS : V_BIAS + 1, 0:VFRESH] += total(dm[at, 2 * D : QKV].astype(f32))
+
+    chunks(SEQ, step, first_back)
+
+    def collect(g, e, owner):
+        return dot_nt(jnp.where(owner == rowdev, g, 0.0).astype(bf), e)
+
+    for v in WIDE:
+        sv[v // spr, :, lanes(v)] = collect(sums[v : v + 1, :], e24, tab[1:2, :])
+    sv[V_BIAS // spr, :, lanes(V_BIAS)] = collect(sums[V_BIAS : V_BIAS + 1, :], onehot(2, D), tab[3:4, :])
+    got = collect(ubg[0:1, :], e96, tab[5:6, :C])
+    for j in range(1, n_mp):
+        got = got + collect(ubg[j : j + 1, :], e96, tab[5:6, :C] + j * n_dp)
+    sv[UP_BIAS // spr, :, lanes(UP_BIAS)] = got
+    at16 = lax.broadcasted_iota(jnp.int32, (16, C), 0)
+    for j in range(n_mp):
+        for d in range(n_dp):
+            at = j * n_dp + d
+            value = jnp.zeros((16, C), f32)
+            for r in range(-(-9 // spr)):
+                value = jnp.where(at16 == r, sv[r, at : at + 1, :], value)
+            gr[j, d, 3 * R :, :] = value.astype(bf)
+
+
+def layer(plan, g, x, f, y):
+    R, C, n_mp, n_dp = plan.rows, plan.cols, plan.n_mp, plan.n_dp
+    n = n_mp * n_dp
+    bf, f32 = jnp.bfloat16, jnp.float32
+    spr = C // 128
+    count = np.arange(D, dtype=np.int32)
+    tab = np.zeros((8, D), np.int32)
+    for at, width in ((0, D // n), (2, VFRESH // n), (4, FF // n)):
+        tab[at], tab[at + 1] = count % width, count // width
+    r = np.arange(n, dtype=np.int32)
+    dev = np.tile(((r % n_dp) * n_mp + r // n_dp)[:, None], (1, 128))
+    vm = pltpu.VMEM
+    vmem = pl.BlockSpec(memory_space=vm)
+    wide = lambda t: vm((SEQ, D), t)
+    tall = lambda t: vm((D, SEQ), t)
+    return pl.pallas_call(
+        functools.partial(layer_kernel, plan),
+        name="layer",
+        out_shape=(
+            jax.ShapeDtypeStruct((SEQ, D), bf),
+            jax.ShapeDtypeStruct((SEQ, D), bf),
+            jax.ShapeDtypeStruct((SEQ, D // 2), bf),
+            jax.ShapeDtypeStruct(g.shape, bf),
+        ),
+        in_specs=[vmem] * 5 + [ANY],
+        out_specs=(vmem,) * 4,
+        scratch_shapes=[
+            vm(g.shape, bf), vm((D, QKV), bf), vm((D, D), bf),
+            vm((-(-9 // spr), n, C), f32), vm((16, D), f32), vm((max(8, n_mp), C), f32),
+            wide(bf), tall(bf), vm((SEQ, 3 * D), bf), tall(f32), tall(bf),
+            vm((HEADS // 2, 8, SEQ), f32),
+            wide(f32), wide(f32), vm((SEQ, 128), f32), wide(bf), tall(bf), tall(bf),
+            wide(f32), wide(f32), vm((SEQ, C), bf), wide(bf), wide(bf), vm((SEQ, 3 * D), bf),
+            vm((SEQ, 128), f32), vm((SEQ, 128), f32), vm((128, SEQ), f32),
+            vm((16, D), f32), vm((max(8, n_mp), C), f32),
+            pltpu.SemaphoreType.DMA,
+        ],
+        compiler_params=pltpu.CompilerParams(vmem_limit_bytes=63 << 20),
+    )(jnp.asarray(tab), jnp.asarray(dev), x, f, y, g)
 
 
 def shards(
     plan, tokens, first_values, out_cot, ln1_gain, ln1_bias, w_qkv, q_bias, v_bias, w_out, out_bias,
     ln2_gain, ln2_bias, w_up, up_bias, w_down, down_bias,
 ):
-    bf, f32 = jnp.bfloat16, jnp.float32
-    R, C, n_mp, n_dp = plan.rows, plan.cols, plan.n_mp, plan.n_dp
+    R, C = plan.rows, plan.cols
     small = (ln1_gain, ln1_bias, q_bias, v_bias, out_bias, ln2_gain, ln2_bias, up_bias, down_bias)
     widths = [s.shape[0] for s in small]
     gap = lambda a, w: jnp.pad(a, ((0, 0), (0, w - a.shape[1])))
-    row = jnp.concatenate(small)[None]
+    spr = C // 128
+    slots = jnp.concatenate([jnp.pad(s, (0, 128 - s.shape[0])) for s in small])
+    slots = jnp.pad(slots, (0, 16 * C - slots.shape[0])).reshape(16, C)
     packed = jnp.concatenate(
         [
             jnp.concatenate([gap(w_qkv, plan.out_at), gap(w_out, C - plan.out_at)], axis=1),
             w_up,
             w_down.T,
-            jnp.pad(row, ((0, 15), (0, C - row.shape[1]))),
+            slots,
         ],
         axis=0,
     )
     g, x, f, y = gather(plan, packed, tokens, first_values, out_cot)
-
-    def wide(lo, at, width):
-        part = g[:, :, lo : lo + R, at : at + width]
-        return part.reshape(n_mp, D, width).transpose(1, 0, 2).reshape(D, n_mp * width)
-
-    weights = (
-        wide(0, 0, plan.qkv),
-        wide(0, plan.out_at, plan.out),
-        wide(R, 0, C),
-        wide(2 * R, 0, C),
-    )
-    vecs = g[:, :, 3 * R, :].astype(f32).transpose(1, 0, 2)
-    ends = [sum(widths[:n]) for n in range(len(widths) + 1)]
-    vectors = [vecs[:, :, a:b].reshape(-1) for a, b in zip(ends[:-1], ends[1:])]
-    out, dx, dfirst, grads, small_grads = layer(
-        x.reshape(SEQ, D), f.reshape(SEQ, -1), y.reshape(SEQ, D), weights, vectors
-    )
-    split = lambda a: a.astype(bf).reshape(n_dp, R, n_mp, -1).transpose(2, 0, 1, 3)
-    gap4 = lambda a, w: jnp.pad(a, ((0, 0), (0, 0), (0, 0), (0, w - a.shape[3])))
-    rows = jnp.concatenate([v.astype(bf).reshape(n_dp, n_mp, 1, -1) for v in small_grads], axis=3)
-    rows = rows.transpose(1, 0, 2, 3)
-    full = jnp.concatenate(
-        [
-            jnp.concatenate(
-                [gap4(split(grads[0]), plan.out_at), gap4(split(grads[1]), C - plan.out_at)], axis=3
-            ),
-            split(grads[2]),
-            split(grads[3]),
-            jnp.pad(rows, ((0, 0), (0, 0), (0, 15), (0, C - rows.shape[3]))),
-        ],
-        axis=2,
-    )
+    out, dx, dfirst, full = layer(plan, g, x.reshape(SEQ, D), f.reshape(SEQ, -1), y.reshape(SEQ, D))
     total, r1, r2, r3 = reduce(
         plan,
         full,
@@ -501,7 +682,7 @@
         dx.reshape(tokens.shape),
         dfirst.reshape(first_values.shape),
     )
-    s = [total[3 * R, a:b] for a, b in zip(ends[:-1], ends[1:])]
+    s = [total[3 * R + v // spr, (v % spr) * 128 : (v % spr) * 128 + w] for v, w in enumerate(widths)]
     return (
         r1, r2, r3,
         s[0], s[1],

time: 470 us -> 296 us (0.63)
  local copies, waits for them, and re-layouts: 134 us -> 22.3 us
  matrix products: 96.9 us -> 0 us
  Pallas kernels: 195 us -> 269 us
  other arithmetic: 36.3 us -> 1.87 us
    dot_general x17 -> x0, matrix products: 89.3 us -> none  [mm(): return jnp.einsum(eq, a, b, preferred_element_type=jnp.float32)]
    pallas_call x0 -> x1, Pallas kernels: none -> 74.3 us  [layer(): pl.pallas_call(functools.partial(layer_kernel, plan), name='layer', out_s...]
    reshape x20 -> x1, local copies, waits for them, and re-layouts: 72.6 us -> 0.05 us  [shards(): slots = jnp.pad(slots, (0, 16 * C - slots.shape[0])).reshape(16, C)]
    slice x17 -> x0, local copies, waits for them, and re-layouts: 14.1 us -> none  [the longest x3 11.8 us: wide(): part = g[:, :, lo:lo + R, at:at + width]]
    convert_element_type x5 -> x0, other arithmetic: 13.6 us -> none  [the longest x1 6.94 us: layer(): ds = (prob * (dp - delta)).astype(bf)]
    convert_element_type x11 -> x0, local copies, waits for them, and re-layouts: 12.2 us -> none  [the longest x8 9.43 us: shards(): v.astype(bf).reshape(n_dp, n_mp, 1, -1)]
    concatenate x1 -> x0, other arithmetic: 11.3 us -> none  [shards(): jnp.concatenate([jnp.concatenate([gap4(split(grads[0]), plan.out_at), gap...]
    transpose x1 -> x0, local copies, waits for them, and re-layouts: 9.23 us -> none  [shards(): a.astype(bf).reshape(n_dp, R, n_mp, -1).transpose(2, 0, 1, 3)]
where the time goes in v2:
time: 296 us; the launch traced here: 294 us
  Pallas kernels  269 us (91%)
  local copies, waits for them, and re-layouts  22.3 us (8%)
    pallas_call x1, Pallas kernels, reduce(): pl.pallas_call(functools.partial(reduce_kernel, plan), name='reduce', out...  103 us
    pallas_call x1, Pallas kernels, gather(): pl.pallas_call(functools.partial(gather_kernel, plan), name='gather', out...  91.6 us
    pallas_call x1, Pallas kernels, layer(): pl.pallas_call(functools.partial(layer_kernel, plan), name='layer', out_s...  74.3 us
    unnamed x11, local copies, waits for them, and re-layouts  7.52 us

profile of v2, /device:TPU:1, one launch (start us, length us, event | category | flops | bytes accessed | tf_op | source)
XLA Modules:
  0.0 294.1 jit_solution(2859703833626800511)
XLA Ops:
  0.6 0.7 pad.44
  1.3 0.7 pad.45
  2.0 0.7 pad.46
  2.6 0.7 pad.47
  3.3 0.7 pad.48
  3.9 0.7 pad.49
  4.6 0.7 pad.50
  5.3 0.7 pad.51
  5.9 0.2 dynamic-update-slice
  6.1 0.2 dynamic-update-slice.1
  6.3 0.2 dynamic-update-slice.2
  6.5 0.2 dynamic-update-slice.3
  6.7 0.2 dynamic-update-slice.4
  6.9 0.2 dynamic-update-slice.5
  7.1 0.2 dynamic-update-slice.6
  7.3 0.2 dynamic-update-slice.7
  7.6 0.7 constant_dynamic-update-slice_fusion
  8.3 1.9 fusion.9.pk
  10.1 91.6 %gather.1 = (bf16[4,8,304,768]{3,2,1,0:T(8,128)(2,1)}, bf16[4,128,768]{2,1,0:T(8,128)(2,1)}, bf16[4,128,384]{2,1,0:T(8,128)(2,1)}, bf16[4,128,768]{2,1,0:T(8,128)(2,1)}) custom-call(bf16[304,768]{1,0:T(8,128)(2,1)} %fusion.9.pk, bf16[4,128,768]{2,1,0:T(8,128)(2,1)} %tok.1, bf16[4,128,384]{2,1,0:T(8,128)(2,1)} %fv.1, bf16[4,128,768]{2,1,0:T(8,128)(2,1)} %cot.1), custom_call_target="tpu_custom_call" | custom-call | tf_op jit(solution)/shard_map/gather/pallas_call | solution.py:170
  101.8 74.3 %layer.1 = (bf16[512,768]{1,0:T(8,128)(2,1)}, bf16[512,768]{1,0:T(8,128)(2,1)}, bf16[512,384]{1,0:T(8,128)(2,1)}, bf16[4,8,304,768]{3,2,1,0:T(8,128)(2,1)}) custom-call(s32[8,768]{1,0:T(8,128)} %constant.7.clone.tab, s32[32,128]{1,0:T(8,128)} %constant.8.clone.dev, bf16[512,768]{1,0:T(8,128)(2,1)} %bitcast.29, bf16[512,384]{1,0:T(8,128)(2,1)} %bitcast.32, ...), custom_call_target="tpu_custom_call" | custom-call | tf_op jit(solution)/shard_map/layer/pallas_call | solution.py:630
  176.1 103.3 %reduce.1 = (f32[304,768]{1,0:T(8,128)}, bf16[4,128,768]{2,1,0:T(8,128)(2,1)}, bf16[4,128,768]{2,1,0:T(8,128)(2,1)}, bf16[4,128,384]{2,1,0:T(8,128)(2,1)}) custom-call(bf16[4,8,304,768]{3,2,1,0:T(8,128)(2,1)} %get-tuple-element.32.grads, bf16[4,128,768]{2,1,0:T(8,128)(2,1)} %bitcast.27, bf16[4,128,768]{2,1,0:T(8,128)(2,1)} %bitcast.28, ...), custom_call_target="tpu_custom_call" | custom-call | tf_op jit(solution)/shard_map/reduce/pallas_call | solution.py:322
  279.5 1.2 slice_bitcast_fusion.6
  280.7 1.2 slice_bitcast_fusion.2
  281.9 1.3 slice_bitcast_fusion.1
  283.2 1.5 slice.44
  284.7 1.6 slice.41
  286.3 1.9 slice_bitcast_fusion
  288.2 2.1 copy.46
  290.3 2.1 copy.47
  292.4 1.8 copy.48
  (3 shorter events, 0.1 us)

commit v3 on v2

v3 whole, which is shorter than its diff:
```python
import functools

import jax
import jax.numpy as jnp
import numpy as np
from jax import lax
from jax.experimental import pallas as pl
from jax.experimental.pallas import tpu as pltpu
from jax.sharding import PartitionSpec as P

D = 768
HEADS = 12
HEAD = 64
FF = 3072
MICRO = 4
QKV = 1920
SEQ = 512
VFRESH = 384

EPS = 1e-05
BIG = 1e30
GELU_C = 0.7978845608028654
GELU_A = 0.044715
MESH = pl.DeviceIdType.MESH
ANY = pl.BlockSpec(memory_space=pl.ANY)
IN_VMEM = pl.BlockSpec(memory_space=pltpu.VMEM)
BF, F32 = jnp.bfloat16, jnp.float32

WIDE = (0, 1, 2, 4, 5, 6, 8)
V_BIAS, UP_BIAS = 3, 7
G1, B1, QB, OB, G2, B2, DB = WIDE
N_VEC = 9


class Plan:
    def __init__(self, mesh):
        self.n_dp = mesh.shape["dp"]
        self.n_mp = mesh.shape["mp"]
        self.n = self.n_dp * self.n_mp
        self.n_z = self.n_dp // 2
        self.rows = D // self.n_dp
        self.cols = FF // self.n_mp
        self.qkv = QKV // self.n_mp
        self.out = D // self.n_mp
        self.qw = -(-self.qkv // 128) * 128
        self.group = self.cols // 3
        self.spr = self.qw // 128
        self.vec_rows = -(-N_VEC // self.spr)
        self.half = self.n_mp // 2
        self.per_seq = SEQ // (SEQ // MICRO)
        self.n_seq = self.n_mp // MICRO
        assert self.out <= self.group and self.rows % 48 == 0 and self.vec_rows <= 16
        assert self.n_seq * MICRO == self.n_mp and self.n_z % 2 == 0

    def ring_at(self, i):
        return i + (i // self.half) * (self.n_mp - 1 + self.half - 2 * i)

    def slots(self, d):
        if d == self.half:
            return 0, self.n_z // 2
        return self.n_z // 2 + (d - 1) * self.n_z, self.n_z


def dot(a, b):
    return jnp.dot(a, b, preferred_element_type=F32)


def dot_nt(a, b):
    return lax.dot_general(a, b, (((1,), (1,)), ((), ())), preferred_element_type=F32)


def chunks(rows, step, body):
    @pl.loop(0, rows // step)
    def _(at):
        body(pl.ds(pl.multiple_of(at * step, step), step))


def norm_stats(r):
    average = jnp.mean(r, axis=-1, keepdims=True)
    centred = r - average
    variance = jnp.mean(centred * centred, axis=-1, keepdims=True)
    inv_std = lax.rsqrt(variance + EPS)
    return centred * inv_std, inv_std


def norm_back(grad_out, scaled, inv_std, gain):
    e = grad_out * gain
    first = jnp.mean(e, axis=-1, keepdims=True)
    second = jnp.mean(e * scaled, axis=-1, keepdims=True)
    return inv_std * (e - first - scaled * second)


class Exchange:
    def __init__(self, plan):
        self.plan = plan
        dp, i = lax.axis_index("dp"), lax.axis_index("mp")
        self.dp, self.i, self.c, self.z = dp, i, dp % 2, dp // 2
        self.sib = (dp + 1 - 2 * self.c, i)
        self.p = plan.ring_at(i)

    def at(self, pos):
        return self.plan.ring_at((pos + 2 * self.plan.n_mp) % self.plan.n_mp)

    def z_peer(self, k):
        return ((self.z + k) % self.plan.n_z) * 2 + self.c

    def greet(self):
        plan = self.plan
        barrier = pltpu.get_barrier_semaphore()
        partners = [self.sib]
        partners += [(self.z_peer(k), self.i) for k in range(1, plan.n_z)]
        partners += [(self.dp, (self.i + k) % plan.n_mp) for k in range(1, plan.n_mp)]
        for partner in partners:
            pl.semaphore_signal(barrier, inc=1, device_id=partner, device_id_type=MESH)
        pl.semaphore_wait(barrier, len(partners))

    def push(self, src, dst, send, recv, device):
        return pltpu.make_async_remote_copy(
            src_ref=src, dst_ref=dst, send_sem=send, recv_sem=recv, device_id=device, device_id_type=MESH
        )


class Gather:
    def __init__(self, ex, ref, sems):
        self.ex, self.ref = ex, ref
        self.zs, self.zr, self.rs, self.rr, self.ss, self.sr = sems

    def units(self, s, d):
        plan = self.ex.plan
        return pl.ds(s * (plan.n_z // 2), plan.n_z // 2) if d == plan.half else pl.ds(0, plan.n_z)

    def own(self):
        return self.ref.at[self.ex.i, self.ex.z, self.ex.c]

    def z_copy(self, k):
        ex = self.ex
        return ex.push(self.own(), self.own(), self.zs.at[k - 1], self.zr.at[k - 1], (ex.z_peer(k), ex.i))

    def ring_copy(self, s, d):
        ex = self.ex
        sign = 1 - 2 * s
        view = self.ref.at[ex.at(ex.p - sign * (d - 1)), self.units(s, d), ex.c]
        return ex.push(view, view, self.rs.at[s, d - 1], self.rr.at[s, d - 1], (ex.dp, ex.at(ex.p + sign)))

    def sib_copy(self, offset):
        ex = self.ex
        at = (offset + ex.plan.n_mp) % ex.plan.n_mp
        view = self.ref.at[ex.at(ex.p + offset), :, ex.c]
        return ex.push(view, view, self.ss.at[at], self.sr.at[at], ex.sib)

    def start(self):
        for k in range(1, self.ex.plan.n_z):
            self.z_copy(k).start()

    def column(self):
        for k in range(1, self.ex.plan.n_z):
            self.z_copy(k).wait_recv()
        for s in range(2):
            self.ring_copy(s, 1).start()
        self.sib_copy(0).start()

    def hop(self, d):
        half = self.ex.plan.half
        for s in range(2):
            self.ring_copy(s, d).wait_recv()
            if d < half:
                self.ring_copy(s, d + 1).start()
                self.sib_copy(-d if s == 0 else d).start()
        if d == half:
            self.sib_copy(half).start()

    def wait_sib(self, offset):
        self.sib_copy(offset).wait_recv()

    def wait_sent(self, offset):
        half = self.ex.plan.half
        self.sib_copy(offset).wait_send()
        if offset == 0:
            for k in range(1, self.ex.plan.n_z):
                self.z_copy(k).wait_send()
            for s in range(2):
                self.ring_copy(s, 1).wait_send()
        elif abs(offset) < half:
            self.ring_copy(0 if offset < 0 else 1, abs(offset) + 1).wait_send()


class Reduce:
    def __init__(self, ex, ref, tile, other, ring, last, sems):
        self.ex, self.ref, self.tile = ex, ref, tile
        self.other, self.ring, self.last = other, ring, last
        self.ss, self.sr, self.rs, self.rr, self.zs, self.zr = sems

    def units(self, s, d):
        n_z = self.ex.plan.n_z
        return pl.ds(s * (n_z // 2), n_z // 2) if d == self.ex.plan.half else pl.ds(0, n_z)

    def sib_copy(self, offset):
        ex = self.ex
        at = (offset + ex.plan.n_mp) % ex.plan.n_mp
        view = self.ref.at[ex.at(ex.p + offset), :, 1 - ex.c, self.tile]
        return ex.push(view, self.other.at[at], self.ss.at[at], self.sr.at[at], ex.sib)

    def ring_copy(self, s, d, part=None):
        ex = self.ex
        plan = ex.plan
        sign = 1 - 2 * s
        at, count = plan.slots(d)
        if part is None:
            units, slot = self.units(s, d), pl.ds(at, count)
            sem = d - 1
        else:
            units, slot = pl.ds(part * (plan.n_z // 2), plan.n_z // 2), pl.ds(at + part * (plan.n_z // 2), plan.n_z // 2)
            sem = plan.half - 2 + 2 * part
        view = self.ref.at[ex.at(ex.p + sign * d), units, ex.c, self.tile]
        return ex.push(view, self.ring.at[s, slot], self.rs.at[s, sem], self.rr.at[s, sem], (ex.dp, ex.at(ex.p + sign)))

    def z_copy(self, k):
        ex = self.ex
        to = (ex.z + ex.plan.n_z - k) % ex.plan.n_z
        view = self.ref.at[ex.i, to, ex.c, self.tile]
        return ex.push(view, self.last.at[k - 1], self.zs.at[k - 1], self.zr.at[k - 1], (to * 2 + ex.c, ex.i))

    def to_sibling(self, offset):
        self.sib_copy(offset).start()

    def add(self, offset, first, count, *terms):
        j = self.ex.at(self.ex.p + offset)

        @pl.loop(0, count)
        def _(u):
            value = self.ref[j, first + u, self.ex.c, self.tile, :].astype(F32)
            for buf, at in terms:
                value = value + buf(at + u).astype(F32)
            self.ref[j, first + u, self.ex.c, self.tile, :] = value.astype(BF)

    def from_sibling(self, offset):
        at = (offset + self.ex.plan.n_mp) % self.ex.plan.n_mp
        self.sib_copy(offset).wait_recv()
        self.add(offset, 0, self.ex.plan.n_z, (lambda u: self.other[at, u], 0))

    def far(self):
        half = self.ex.plan.half
        self.from_sibling(half)
        for s in range(2):
            self.ring_copy(s, half).start()

    def free(self, s):
        half = self.ex.plan.half
        self.from_sibling((1 - 2 * s) * (half - 1))
        self.ring_copy(s, half - 1, 1 - s).start()

    def bound(self, s):
        plan = self.ex.plan
        half = plan.half
        self.ring_copy(s, half).wait_recv()
        at, count = plan.slots(half)
        self.add((1 - 2 * s) * (half - 1), s * count, count, (lambda u: self.ring[s, u], at))
        self.ring_copy(s, half - 1, s).start()

    def wait_ring(self, s, d):
        if d == self.ex.plan.half - 1:
            for part in range(2):
                self.ring_copy(s, d, part).wait_recv()
        else:
            self.ring_copy(s, d).wait_recv()

    def nearer(self):
        plan = self.ex.plan
        for d in range(plan.half - 2, 0, -1):
            for s in range(2):
                offset = (1 - 2 * s) * d
                self.from_sibling(offset)
                self.wait_ring(s, d + 1)
                self.add(offset, 0, plan.n_z, (lambda u: self.ring[s, u], plan.slots(d + 1)[0]))
                self.ring_copy(s, d).start()

    def home(self):
        plan = self.ex.plan
        for s in range(2):
            self.wait_ring(s, 1)
        self.sib_copy(0).wait_recv()
        at = plan.slots(1)[0]
        self.add(
            0, 0, plan.n_z,
            (lambda u: self.other[0, u], 0),
            (lambda u: self.ring[0, u], at),
            (lambda u: self.ring[1, u], at),
        )
        for k in range(1, plan.n_z):
            self.z_copy(k).start()

    def finish(self):
        ex = self.ex
        value = self.ref[ex.i, ex.z, ex.c, self.tile, :].astype(F32)
        for k in range(1, ex.plan.n_z):
            self.z_copy(k).wait_recv()
            value = value + self.last[k - 1].astype(F32)
        return value

    def wait_sent(self):
        plan = self.ex.plan
        for offset in range(plan.n_mp):
            self.sib_copy(offset).wait_send()
        for s in range(2):
            for d in range(1, plan.half + 1):
                if d == plan.half - 1:
                    for part in range(2):
                        self.ring_copy(s, d, part).wait_send()
                else:
                    self.ring_copy(s, d).wait_send()
        for k in range(1, plan.n_z):
            self.z_copy(k).wait_send()


class Rows:
    def __init__(self, ex, src, dst, send, recv, out):
        self.ex, self.src, self.dst, self.send, self.recv, self.out = ex, src, dst, send, recv, out

    def move(self, start):
        ex = self.ex
        plan, i = ex.plan, ex.i
        q = plan.per_seq
        for m in range(MICRO):
            if self.out:
                target, place = (i % plan.n_seq) * q + m, i // plan.n_seq
            else:
                target, place = m * plan.n_seq + i // q, i % q
            far = ex.push(self.src.at[m], self.dst.at[place], self.send.at[m], self.recv.at[place], (ex.dp, target))
            near = pltpu.make_async_copy(self.src.at[m], self.dst.at[place], self.send.at[m])

            @pl.when(target != i)
            def _():
                far.start() if start else far.wait_send()

            @pl.when(target == i)
            def _():
                near.start() if start else near.wait()

    def start(self):
        self.move(True)

    def wait_sent(self):
        self.move(False)

    def wait_here(self):
        ex = self.ex
        plan, i = ex.plan, ex.i
        q = plan.per_seq
        for m in range(MICRO):
            origin = m * plan.n_seq + i // q if self.out else (i % plan.n_seq) * q + m

            @pl.when(origin != i)
            def _():
                ex.push(self.dst.at[m], self.dst.at[m], self.send.at[0], self.recv.at[m], ex.sib).wait_recv()


def step_kernel(plan, n_in, *refs):
    (tab, dev, slots, w_qkv, w_out, w_up, w_down, tok, fv, cot) = refs[:n_in]
    (o_out, o_dx, o_df, o_q, o_s, o_o, o_f) = refs[n_in : n_in + 7]
    (
        gq, go, gf, x3, f3, y3, out3, dx3, df3,
        q_other, q_ring, q_last, s_other, s_ring, s_last, o_other, o_ring, o_last, f_other, f_ring, f_last,
        wq, wo, sv, vec, ub, hl, hlt, qkv, ot, otb, lse, mid, n2, inv2, h2, h2t, yt,
        big, acc, act, du, dv, dk, dqt, sums, ubg,
    ) = refs[n_in + 7 : n_in + 7 + 47]
    sems = refs[n_in + 7 + 47 :]
    R, C, n_mp, n_dp, n_z = plan.rows, plan.cols, plan.n_mp, plan.n_dp, plan.n_z
    step = 64
    ex = Exchange(plan)
    i, z, c = ex.i, ex.z, ex.c
    Q = Gather(ex, gq, sems[0:6])
    O = Gather(ex, go, sems[6:12])
    F = Gather(ex, gf, sems[12:18])
    RQ = Reduce(ex, gq, slice(0, R), q_other, q_ring, q_last, sems[18:24])
    RS = Reduce(ex, gq, slice(R, R + 16), s_other, s_ring, s_last, sems[24:30])
    RO = Reduce(ex, go, slice(0, R // 3), o_other, o_ring, o_last, sems[30:36])
    RF = Reduce(ex, gf, slice(0, 2 * R), f_other, f_ring, f_last, sems[36:42])
    a2a = sems[42:54]
    XT = Rows(ex, tok, x3, a2a[0], a2a[1], False)
    XF = Rows(ex, fv, f3, a2a[2], a2a[3], False)
    XY = Rows(ex, cot, y3, a2a[4], a2a[5], False)
    YO = Rows(ex, out3, o_out, a2a[6], a2a[7], True)
    YX = Rows(ex, dx3, o_dx, a2a[8], a2a[9], True)
    YF = Rows(ex, df3, o_df, a2a[10], a2a[11], True)

    third = R // 3
    gq[i, z, c, 0:R, 0 : plan.qkv] = w_qkv[...]
    gq[i, z, c, R:, :] = slots[...]
    for t in range(3):
        go[i, z, c, :, t * plan.group : t * plan.group + plan.out] = w_out[t * third : (t + 1) * third, :]
    gf[i, z, c, 0:R, :] = w_up[...]
    gf[i, z, c, R:, :] = w_down[...].T
    ex.greet()
    Q.start()
    O.start()
    XT.start()
    XF.start()
    F.start()
    Q.column()
    O.column()
    for d in range(1, plan.half):
        Q.hop(d)
        O.hop(d)
    F.column()
    XY.start()

    rowdev = dev[:, 0:1]
    row = lambda v: vec[v : v + 1, :]
    lanes = lambda v: slice((v % plan.spr) * 128, (v % plan.spr) * 128 + 128)
    onehot = lambda t, width: (lax.broadcasted_iota(jnp.int32, (128, width), 0) == tab[t : t + 1, :width]).astype(BF)
    e24 = onehot(0, D)
    e96 = onehot(4, C)

    def rows_of(ref3, at, step):
        part = SEQ // MICRO
        return ref3.at[at // (part // step), pl.ds(pl.multiple_of((at % (part // step)) * step, step), step)]

    def blocks(step, body):
        @pl.loop(0, SEQ // step)
        def _(at):
            body(at, pl.ds(pl.multiple_of(at * step, step), step))

    Q.hop(plan.half)
    O.hop(plan.half)
    for piece in (Q, O):
        for offset in range(-plan.half + 1, plan.half + 1):
            piece.wait_sib(offset)

    for j in range(n_mp):
        for d in range(n_dp):
            rows = slice(d * R, (d + 1) * R)
            wq[rows, j * plan.qkv : (j + 1) * plan.qkv] = gq[j, d // 2, d % 2, 0:R, 0 : plan.qkv]
            for t in range(3):
                rows = slice(d * R + t * third, d * R + (t + 1) * third)
                wo[rows, j * plan.out : (j + 1) * plan.out] = go[
                    j, d // 2, d % 2, :, t * plan.group : t * plan.group + plan.out
                ]
    for r in range(plan.vec_rows):
        for j in range(n_mp):
            for d in range(n_dp):
                at = j * n_dp + d
                sv[r, at : at + 1, :] = gq[j, d // 2, d % 2, R + r : R + r + 1, :].astype(F32)

    def expand(v, e, owner):
        got = dot(sv[v // plan.spr, :, lanes(v)].astype(BF), e)
        return jnp.sum(jnp.where(owner == rowdev, got, 0.0), axis=0, keepdims=True)

    for v in WIDE:
        vec[v : v + 1, :] = expand(v, e24, tab[1:2, :])
    vec[V_BIAS : V_BIAS + 1, :] = expand(V_BIAS, onehot(2, D), tab[3:4, :])
    for j in range(n_mp):
        ub[j : j + 1, :] = expand(UP_BIAS, e96, tab[5:6, :C] + j * n_dp)

    XT.wait_here()
    XT.wait_sent()

    def first_norm(at, rows):
        n1, _ = norm_stats(rows_of(x3, at, step)[...].astype(F32))
        hl[rows, :] = (n1 * row(G1) + row(B1)).astype(BF)

    blocks(step, first_norm)
    hlt[...] = hl[...].T
    XF.wait_here()
    XF.wait_sent()

    def project(at, rows):
        h = hl[rows, :]
        q = dot(h, wq[:, 0:D]) + row(QB)
        qkv[rows, 0:D] = q.astype(BF) * 0.125
        qkv[rows, D : 2 * D] = dot(h, wq[:, D : 2 * D]).astype(BF)
        v = dot(h, wq[:, 2 * D : QKV]) + row(V_BIAS)[:, :VFRESH]
        qkv[rows, 2 * D : QKV] = v.astype(BF)

    blocks(256, project)
    qkv[:, QKV : 3 * D] = f3[...].reshape(SEQ, D // 2)

    B = 256
    head_of = lax.broadcasted_iota(jnp.int32, (1, 128), 1) // HEAD
    keep = lax.broadcasted_iota(jnp.int32, (B, B), 0) <= lax.broadcasted_iota(jnp.int32, (B, B), 1)

    def scores(k2, qm, at):
        s = dot_nt(k2, qm)
        last = jnp.where(keep, s[at * B :, :], -BIG)
        return last if at == 0 else jnp.concatenate([s[: at * B, :], last], axis=0)

    @pl.loop(0, HEADS // 2)
    def _(t):
        cols = lambda base: pl.ds(pl.multiple_of(base + t * 128, 128), 128)
        vt = qkv[:, cols(2 * D)].T
        for e in range(2):
            mask = (head_of == e).astype(BF)
            for at in range(SEQ // B):
                kk = (at + 1) * B
                span = slice(at * B, kk)
                s = scores(qkv[0:kk, cols(D)], qkv[span, cols(0)] * mask, at)
                top = jnp.max(s, axis=0, keepdims=True)
                ex_ = jnp.exp(s - top)
                total = jnp.sum(ex_, axis=0, keepdims=True)
                o = dot(vt[e * HEAD : (e + 1) * HEAD, 0:kk], ex_.astype(BF)) / total
                ot[pl.ds(pl.multiple_of(t * 128 + e * HEAD, HEAD), HEAD), span] = o
                lse[t, e : e + 1, span] = top + jnp.log(total)

        for d in range(1, plan.half):

            @pl.when(t == 2 + d)
            def _():
                F.hop(d)

    otb[...] = ot[...].astype(BF)
    du[:, 0:D] = otb[...].T

    def second_norm(at, rows):
        m = rows_of(x3, at, 128)[...].astype(F32) + (dot(du[rows, 0:D], wo[...]) + row(OB))
        mid[rows, :] = m
        scaled, inv = norm_stats(m)
        n2[rows, :] = scaled
        inv2[rows, :] = jnp.broadcast_to(inv, (128, 128))
        h2[rows, :] = (scaled * row(G2) + row(B2)).astype(BF)

    blocks(128, second_norm)
    h2t[...] = h2[...].T
    XY.wait_here()
    XY.wait_sent()
    yt[...] = y3[...].reshape(SEQ, D).T
    acc[...] = jnp.zeros_like(acc)
    big[...] = jnp.zeros_like(big)

    offset_of = lambda q: (q + 1) // 2 * (1 - 2 * (q % 2))

    @pl.loop(0, n_mp)
    def _(q):
        j = ex.at(ex.p + offset_of(q))
        for s in range(n_mp):

            @pl.when(q == s)
            def _():
                if s == n_mp - 1:
                    F.hop(plan.half)
                F.wait_sib(plan.half if s == n_mp - 1 else offset_of(s))

        bias = ub[pl.ds(j, 1), :]

        def rows(at, rows):
            up = gf[j, :, :, 0:R, :].reshape(D, C)
            down = gf[j, :, :, R : 2 * R, :].reshape(D, C)
            u = dot(h2[rows, :], up) + bias
            u2 = u * u
            tangent = jnp.tanh(GELU_C * (u + GELU_A * u2 * u))
            half = 0.5 * (1.0 + tangent)
            a = (u * half).astype(BF)
            slope = half + 0.5 * u * (1.0 - tangent * tangent) * GELU_C * (1.0 + 3.0 * GELU_A * u2)
            act[rows, :] = a
            acc[rows, :] += dot_nt(a, down)
            g = (dot(rows_of(y3, at, 128)[...], down) * slope).astype(BF)
            du[rows, 0:C] = g
            big[rows, :] += dot_nt(g, up)

        blocks(128, rows)
        for s in range(n_mp):

            @pl.when(q == s)
            def _():
                F.wait_sent(plan.half if s == n_mp - 1 else offset_of(s))

        gf[j, :, :, R : 2 * R, :] = dot(yt[...], act[...]).astype(BF).reshape(n_z, 2, R, C)
        gf[j, :, :, 0:R, :] = dot(h2t[...], du[:, 0:C]).astype(BF).reshape(n_z, 2, R, C)
        ubg[pl.ds(j, 1), :] = jnp.sum(du[:, 0:C].astype(F32), axis=0, keepdims=True)
        for s in range(n_mp):

            @pl.when(q == s)
            def _():
                RF.to_sibling(plan.half if s == n_mp - 1 else offset_of(s))
                if s == n_mp - 1:
                    RF.free(1)
                    RF.free(0)

    sums[...] = jnp.zeros_like(sums)

    def second_back(at, rows):
        rows_of(out3, at, step)[...] = (mid[rows, :] + (acc[rows, :] + row(DB))).astype(BF)
        dh = big[rows, :]
        dy = rows_of(y3, at, step)[...].astype(F32)
        scaled = n2[rows, :]
        dr = norm_back(dh, scaled, inv2[rows, 0:1], row(G2))
        dmid = dy + dr
        mid[rows, :] = dmid
        low = dmid.astype(BF)
        du[rows, 0:D] = low
        total = lambda a: jnp.sum(a, axis=0, keepdims=True)
        sums[G2 : G2 + 1, :] += total(dh * scaled)
        sums[B2 : B2 + 1, :] += total(dh)
        sums[OB : OB + 1, :] += total(low.astype(F32))
        sums[DB : DB + 1, :] += total(dy)

    blocks(step, second_back)
    RF.far()
    YO.start()
    for offset in range(-plan.half + 1, plan.half + 1):
        O.wait_sent(offset)
        Q.wait_sent(offset)
    for j in range(n_mp):
        g = dot(otb[...], du[:, j * plan.out : (j + 1) * plan.out]).astype(BF).reshape(n_z, 2, 3, third, plan.out)
        for t in range(3):
            go[j, :, :, :, t * plan.group : t * plan.group + plan.out] = g[:, :, t]
    for offset in range(n_mp):
        RO.to_sibling(offset)
    do = hl

    def out_back(at, rows):
        do[rows, :] = dot_nt(du[rows, 0:D], wo[...]).astype(BF)

    blocks(256, out_back)
    RO.far()
    RO.free(0)
    RO.free(1)

    @pl.loop(0, HEADS // 2)
    def _(t):
        cols = lambda base: pl.ds(pl.multiple_of(base + t * 128, 128), 128)
        kt = qkv[:, cols(D)].T
        dot_ = do[:, cols(0)].astype(F32).T
        prod = dot_ * ot[cols(0), :]
        dv[...] = jnp.zeros_like(dv)
        dk[...] = jnp.zeros_like(dk)
        for e in range(2):
            mask = (head_of == e).astype(BF)
            delta = jnp.sum(prod[e * HEAD : (e + 1) * HEAD, :], axis=0, keepdims=True)
            for at in range(SEQ // B):
                kk = (at + 1) * B
                span = slice(at * B, kk)
                qm = qkv[span, cols(0)] * mask
                dom = do[span, cols(0)] * mask
                s = scores(qkv[0:kk, cols(D)], qm, at)
                p = jnp.exp(s - lse[t, e : e + 1, span])
                dp = dot_nt(qkv[0:kk, cols(2 * D)], dom)
                ds = (p * (dp - delta[:, span])).astype(BF)
                dv[0:kk, :] += dot(p.astype(BF), dom)
                dk[0:kk, :] += dot(ds, qm)
                dqt[e * HEAD : (e + 1) * HEAD, span] = dot(kt[e * HEAD : (e + 1) * HEAD, 0:kk], ds)
        qkv[:, cols(0)] = (dqt[...].T * 0.125).astype(BF)
        qkv[:, cols(D)] = dk[...].astype(BF)
        qkv[:, cols(2 * D)] = dv[...].astype(BF)

        @pl.when(t == 1)
        def _():
            for s in range(2):
                RF.bound(s)

        @pl.when(t == 3)
        def _():
            RF.nearer()
            for s in range(2):
                RO.bound(s)

        @pl.when(t == 5)
        def _():
            RO.nearer()

    df3[...] = qkv[:, QKV : 3 * D].reshape(df3.shape)
    YF.start()
    for j in range(n_mp):
        g = dot(hlt[...], qkv[:, j * plan.qkv : (j + 1) * plan.qkv]).astype(BF)
        gq[j, :, :, 0:R, 0 : plan.qkv] = g.reshape(n_z, 2, R, plan.qkv)
    for offset in (plan.half, *range(-plan.half + 1, plan.half)):
        RQ.to_sibling(offset)
    RF.home()
    RQ.far()
    RQ.free(0)
    RQ.free(1)
    RO.home()

    def project_back(at, rows):
        acc[rows, :] = dot_nt(qkv[rows, 0:QKV], wq[...])

    blocks(256, project_back)

    def first_back(at, rows):
        n1, inv = norm_stats(rows_of(x3, at, step)[...].astype(F32))
        dh = acc[rows, :]
        dr = norm_back(dh, n1, inv, row(G1))
        rows_of(dx3, at, step)[...] = (mid[rows, :] + dr).astype(BF)
        total = lambda a: jnp.sum(a, axis=0, keepdims=True)
        sums[G1 : G1 + 1, :] += total(dh * n1)
        sums[B1 : B1 + 1, :] += total(dh)
        sums[QB : QB + 1, :] += total(qkv[rows, 0:D].astype(F32))
        sums[V_BIAS : V_BIAS + 1, 0:VFRESH] += total(qkv[rows, 2 * D : QKV].astype(F32))

    blocks(step, first_back)
    YX.start()
    for s in range(2):
        RQ.bound(s)

    def collect(g, e, owner):
        return dot_nt(jnp.where(owner == rowdev, g, 0.0).astype(BF), e)

    for v in WIDE:
        sv[v // plan.spr, :, lanes(v)] = collect(sums[v : v + 1, :], e24, tab[1:2, :])
    sv[V_BIAS // plan.spr, :, lanes(V_BIAS)] = collect(sums[V_BIAS : V_BIAS + 1, :], onehot(2, D), tab[3:4, :])
    got = collect(ubg[0:1, :], e96, tab[5:6, :C])
    for j in range(1, n_mp):
        got = got + collect(ubg[j : j + 1, :], e96, tab[5:6, :C] + j * n_dp)
    sv[UP_BIAS // plan.spr, :, lanes(UP_BIAS)] = got
    at16 = lax.broadcasted_iota(jnp.int32, (16, plan.qw), 0)
    for j in range(n_mp):
        for d in range(n_dp):
            at = j * n_dp + d
            value = jnp.zeros((16, plan.qw), F32)
            for r in range(plan.vec_rows):
                value = jnp.where(at16 == r, sv[r, at : at + 1, :], value)
            gq[j, d // 2, d % 2, R:, :] = value.astype(BF)
    for offset in range(n_mp):
        RS.to_sibling(offset)
    o_f[...] = RF.finish()
    RS.far()
    RS.free(0)
    RS.free(1)
    RQ.nearer()
    o_o[...] = RO.finish()
    for s in range(2):
        RS.bound(s)
    RQ.home()
    RS.nearer()
    RS.home()
    o_q[...] = RQ.finish()
    o_s[...] = RS.finish()
    for r in (RF, RO, RQ, RS):
        r.wait_sent()
    for r in (YO, YF, YX):
        r.wait_sent()
        r.wait_here()


def step(plan, slots, w_qkv, w_out, w_up, w_down, tok, fv, cot):
    R, C, n_mp, n_z, n = plan.rows, plan.cols, plan.n_mp, plan.n_z, plan.n
    count = np.arange(D, dtype=np.int32)
    tab = np.zeros((8, D), np.int32)
    for at, width in ((0, D // n), (2, VFRESH // n), (4, FF // n)):
        tab[at], tab[at + 1] = count % width, count // width
    r = np.arange(n, dtype=np.int32)
    dev = np.tile(((r % plan.n_dp) * n_mp + r // plan.n_dp)[:, None], (1, 128))
    vm = pltpu.VMEM
    dma = pltpu.SemaphoreType.DMA
    wide = lambda t: vm((SEQ, D), t)
    tall = lambda t: vm((D, SEQ), t)
    panel = lambda rows, cols: vm((n_mp, n_z, 2, rows, cols), BF)

    def sums(rows, cols):
        ring = n_z // 2 + (plan.half - 1) * n_z
        return [
            vm((n_mp, n_z, rows, cols), BF),
            vm((2, ring, rows, cols), BF),
            vm((n_z - 1, rows, cols), BF),
        ]

    gather_sems = [dma((n_z - 1,))] * 2 + [dma((2, plan.half))] * 2 + [dma((n_mp,))] * 2
    reduce_sems = [dma((n_mp,))] * 2 + [dma((2, plan.half + 1))] * 2 + [dma((n_z - 1,))] * 2
    shape = jax.ShapeDtypeStruct
    ins = (jnp.asarray(tab), jnp.asarray(dev), slots, w_qkv, w_out, w_up, w_down, tok, fv, cot)
    return pl.pallas_call(
        functools.partial(step_kernel, plan, len(ins)),
        name="step",
        out_shape=(
            shape(tok.shape, BF),
            shape(tok.shape, BF),
            shape(fv.shape, BF),
            shape((R, plan.qw), F32),
            shape((16, plan.qw), F32),
            shape((R // 3, C), F32),
            shape((2 * R, C), F32),
        ),
        in_specs=[IN_VMEM] * 7 + [ANY] * 3,
        out_specs=(ANY,) * 3 + (IN_VMEM,) * 4,
        scratch_shapes=[
            panel(R + 16, plan.qw), panel(R // 3, C), panel(2 * R, C),
            vm(tok.shape, BF), vm(fv.shape, BF), vm(cot.shape, BF),
            vm(tok.shape, BF), vm(tok.shape, BF), vm(fv.shape, BF),
            *sums(R, plan.qw), *sums(16, plan.qw), *sums(R // 3, C), *sums(2 * R, C),
            vm((D, QKV), BF), vm((D, D), BF),
            vm((plan.vec_rows, n, plan.qw), F32), vm((16, D), F32), vm((max(8, n_mp), C), F32),
            wide(BF), tall(BF), vm((SEQ, 3 * D), BF), tall(F32), tall(BF),
            vm((HEADS // 2, 8, SEQ), F32),
            wide(F32), wide(F32), vm((SEQ, 128), F32), wide(BF), tall(BF), tall(BF),
            wide(F32), wide(F32), vm((SEQ, C), BF), wide(BF),
            vm((SEQ, 128), F32), vm((SEQ, 128), F32), vm((128, SEQ), F32),
            vm((16, D), F32), vm((max(8, n_mp), C), F32),
            *(gather_sems * 3),
            *(reduce_sems * 4),
            *([dma((MICRO,))] * 12),
        ],
        compiler_params=pltpu.CompilerParams(
            collective_id=0, has_side_effects=True, vmem_limit_bytes=63 << 20
        ),
    )(*ins)


def shards(
    plan, tokens, first_values, out_cot, ln1_gain, ln1_bias, w_qkv, q_bias, v_bias, w_out, out_bias,
    ln2_gain, ln2_bias, w_up, up_bias, w_down, down_bias,
):
    small = (ln1_gain, ln1_bias, q_bias, v_bias, out_bias, ln2_gain, ln2_bias, up_bias, down_bias)
    widths = [s.shape[0] for s in small]
    slots = jnp.concatenate([jnp.pad(s, (0, 128 - s.shape[0])) for s in small])
    slots = jnp.pad(slots, (0, 16 * plan.qw - slots.shape[0])).reshape(16, plan.qw)
    r1, r2, r3, t_q, t_s, t_o, t_f = step(
        plan, slots, w_qkv, w_out, w_up, w_down, tokens, first_values, out_cot
    )
    R, spr = plan.rows, plan.spr
    s = [t_s[v // spr, (v % spr) * 128 : (v % spr) * 128 + w] for v, w in enumerate(widths)]
    t_o = jnp.concatenate([t_o[:, t * plan.group : t * plan.group + plan.out] for t in range(3)], axis=0)
    return (
        r1, r2, r3,
        s[0], s[1],
        t_q[:, : plan.qkv],
        s[2], s[3],
        t_o,
        s[4], s[5], s[6],
        t_f[:R],
        s[7],
        t_f[R:].T,
        s[8],
    )


def solution(mesh):
    plan = Plan(mesh)
    line = P(("dp", "mp"))
    rows = P(None, ("dp", "mp"), None)
    block = P("dp", "mp")
    grads = (line, line, block, line, line, block, line, line, line, block, line, P("mp", "dp"), line)
    return jax.shard_map(
        functools.partial(shards, plan),
        mesh=mesh,
        in_specs=(rows, rows, rows) + grads,
        out_specs=(rows, rows, rows) + grads,
        check_vma=False,
    )
```

time: 296 us -> 230 us (0.78)
  Pallas kernels: 269 us -> 209 us
  local copies, waits for them, and re-layouts: 22.3 us -> 19.2 us
    pallas_call x3 -> x1, Pallas kernels: 269 us -> 209 us  [step(): pl.pallas_call(functools.partial(step_kernel, plan, len(ins)), name='step...]
    pad x8, local copies, waits for them, and re-layouts: 5.28 us -> 0.04 us  [shards(): slots = jnp.concatenate([jnp.pad(s, (0, 128 - s.shape[0])) for s in small])]
    unnamed x11 -> x39, local copies, waits for them, and re-layouts: 7.52 us -> 12 us
where the time goes in v3:
time: 230 us
  Pallas kernels  209 us (91%)
  local copies, waits for them, and re-layouts  19.2 us (8%)
    pallas_call x1, Pallas kernels, step(): pl.pallas_call(functools.partial(step_kernel, plan, len(ins)), name='step...  209 us
    unnamed x39, local copies, waits for them, and re-layouts  12 us

profile of v3, /device:TPU:1, one launch (start us, length us, event | category | flops | bytes accessed | tf_op | source)
XLA Modules:
  0.0 229.6 jit_solution(11668614817880722699)
XLA Ops:
  0.6 1.7 copy.34.refs_6_
  2.4 0.0 copy-start.4
  2.4 0.7 copy-done.4
  3.0 0.0 copy-start.5
  3.0 0.2 dynamic-update-slice
  3.2 0.4 copy-done.5
  3.7 0.0 copy-start.6
  3.7 0.2 dynamic-update-slice.1
  3.9 0.4 copy-done.6
  4.4 0.0 copy-start.7
  4.4 0.2 dynamic-update-slice.2
  4.6 0.4 copy-done.7
  5.0 0.0 copy-start.8
  5.0 0.2 dynamic-update-slice.3
  5.2 0.4 copy-done.8
  5.7 0.0 copy-start.9
  5.7 0.2 dynamic-update-slice.4
  5.9 0.4 copy-done.9
  6.3 0.0 copy-start.10
  6.3 0.2 dynamic-update-slice.5
  6.6 0.4 copy-done.10
  7.0 0.0 copy-start.11
  7.0 0.2 dynamic-update-slice.6
  7.2 0.4 copy-done.11
  7.7 0.0 copy-start.12
  7.7 0.2 dynamic-update-slice.7
  7.9 0.4 copy-done.12
  8.3 0.6 reshape.35.refs_2_
  9.0 209.1 %step.1 = (bf16[4,128,768]{2,1,0:T(8,128)(2,1)}, bf16[4,128,768]{2,1,0:T(8,128)(2,1)}, bf16[4,128,384]{2,1,0:T(8,128)(2,1)}, f32[96,512]{1,0:T(8,128)}, f32[16,5...) custom-call(s32[8,768]{1,0:T(8,128)} %constant.7.clone.refs_0_, s32[32,128]{1,0:T(8,128)} %constant.8.clone.refs_1_, ...), custom_call_target="tpu_custom_call" | custom-call | tf_op jit(solution)/shard_map/step/pallas_call | solution.py:759
  218.1 0.0 copy-start.1
  218.1 0.9 fusion
  219.0 0.6 pad_maximum_fusion
  219.6 1.3 slice_bitcast_fusion.1
  220.9 1.2 slice_bitcast_fusion.2
  222.1 1.2 slice_bitcast_fusion.6
  223.3 1.9 slice_bitcast_fusion
  225.2 0.0 copy-done.1
  225.2 0.0 copy-start
  225.2 0.9 copy.48
  226.1 0.5 copy-done
  226.6 0.0 copy-start.2
  226.6 0.9 copy.49
  227.5 0.4 copy-done.2
  227.9 0.0 copy-start.3
  227.9 0.7 copy.50
  228.6 0.3 copy-done.3
  228.9 0.7 copy.51
  (11 shorter events, 0.1 us)
Async XLA Ops:
  2.4 0.7 copy-start.4
  3.0 0.7 copy-start.5
  3.7 0.7 copy-start.6
  4.4 0.7 copy-start.7
  5.0 0.7 copy-start.8
  5.7 0.7 copy-start.9
  6.3 0.7 copy-start.10
  7.0 0.7 copy-start.11
  7.7 0.7 copy-start.12
  218.1 7.1 %copy-start.1 = (bf16[4,128,768]{2,1,0:T(8,128)(2,1)S(1)}, bf16[4,128,768]{2,1,0:T(8,128)(2,1)}, u32[]{:S(2)}) copy-start(bf16[4,128,768]{2,1,0:T(8,128)(2,1)} %get-tuple-element.58) | copy-start | bytes 2359300
  225.2 1.4 copy-start
  226.6 1.2 copy-start.2
  227.9 1.1 copy-start.3

commit v4 on v3

--- a/solution.py
+++ b/solution.py
@@ -50,10 +50,15 @@
         self.per_seq = SEQ // (SEQ // MICRO)
         self.n_seq = self.n_mp // MICRO
         assert self.out <= self.group and self.rows % 48 == 0 and self.vec_rows <= 16
-        assert self.n_seq * MICRO == self.n_mp and self.n_z % 2 == 0
+        self.bits = self.n_z.bit_length() - 1
+        assert self.n_seq * MICRO == self.n_mp and self.n_z == 1 << self.bits and self.bits > 0
 
     def ring_at(self, i):
         return i + (i // self.half) * (self.n_mp - 1 + self.half - 2 * i)
+
+    def row_half(self, s, rows):
+        middle = -(-rows // 32) * 16 if rows > 16 else 8
+        return slice(middle, rows) if s else slice(0, middle)
 
     def slots(self, d):
         if d == self.half:
@@ -101,14 +106,25 @@
     def at(self, pos):
         return self.plan.ring_at((pos + 2 * self.plan.n_mp) % self.plan.n_mp)
 
-    def z_peer(self, k):
-        return ((self.z + k) % self.plan.n_z) * 2 + self.c
+    def across(self, b):
+        return self.z + (1 << b) * (1 - 2 * (self.z // (1 << b) % 2))
+
+    def z_units(self, b, far):
+        n_z = self.plan.n_z
+        base = self.across(b) if far else self.z
+        return [(base + m * (2 << b)) % n_z for m in range(n_z // (2 << b))]
+
+    def z_slot(self, b, m):
+        return self.plan.n_z // (2 << b) - 1 + m
+
+    def z_device(self, b):
+        return (self.across(b) * 2 + self.c, self.i)
 
     def greet(self):
         plan = self.plan
         barrier = pltpu.get_barrier_semaphore()
         partners = [self.sib]
-        partners += [(self.z_peer(k), self.i) for k in range(1, plan.n_z)]
+        partners += [self.z_device(b) for b in range(plan.bits)]
         partners += [(self.dp, (self.i + k) % plan.n_mp) for k in range(1, plan.n_mp)]
         for partner in partners:
             pl.semaphore_signal(barrier, inc=1, device_id=partner, device_id_type=MESH)
@@ -125,21 +141,21 @@
         self.ex, self.ref = ex, ref
         self.zs, self.zr, self.rs, self.rr, self.ss, self.sr = sems
 
-    def units(self, s, d):
-        plan = self.ex.plan
-        return pl.ds(s * (plan.n_z // 2), plan.n_z // 2) if d == plan.half else pl.ds(0, plan.n_z)
-
-    def own(self):
-        return self.ref.at[self.ex.i, self.ex.z, self.ex.c]
-
-    def z_copy(self, k):
-        ex = self.ex
-        return ex.push(self.own(), self.own(), self.zs.at[k - 1], self.zr.at[k - 1], (ex.z_peer(k), ex.i))
+    def z_copy(self, b, m):
+        ex = self.ex
+        view = self.ref.at[ex.i, ex.z_units(b, False)[m], ex.c]
+        at = ex.z_slot(b, m)
+        return ex.push(view, view, self.zs.at[at], self.zr.at[at], ex.z_device(b))
+
+    def ring_view(self, origin, s, d):
+        n_z, half = self.ex.plan.n_z, self.ex.plan.half
+        units = pl.ds(s * (n_z // 2), n_z // 2) if d == half else pl.ds(0, n_z)
+        return self.ref.at[origin, units, self.ex.c]
 
     def ring_copy(self, s, d):
         ex = self.ex
         sign = 1 - 2 * s
-        view = self.ref.at[ex.at(ex.p - sign * (d - 1)), self.units(s, d), ex.c]
+        view = self.ring_view(ex.at(ex.p - sign * (d - 1)), s, d)
         return ex.push(view, view, self.rs.at[s, d - 1], self.rr.at[s, d - 1], (ex.dp, ex.at(ex.p + sign)))
 
     def sib_copy(self, offset):
@@ -149,12 +165,24 @@
         return ex.push(view, view, self.ss.at[at], self.sr.at[at], ex.sib)
 
     def start(self):
-        for k in range(1, self.ex.plan.n_z):
-            self.z_copy(k).start()
+        for b in range(self.ex.plan.bits):
+            self.z_copy(b, 0).start()
+
+    def z_sizes(self):
+        n_z = self.ex.plan.n_z
+        return [(b, n_z // (2 << b)) for b in range(self.ex.plan.bits)]
+
+    def spread(self):
+        sizes = self.z_sizes()
+        for b, count in reversed(sizes[:-1]):
+            for m in range(sizes[b + 1][1]):
+                self.z_copy(b + 1, m).wait_recv()
+            for m in range(1, count):
+                self.z_copy(b, m).start()
 
     def column(self):
-        for k in range(1, self.ex.plan.n_z):
-            self.z_copy(k).wait_recv()
+        for m in range(self.z_sizes()[0][1]):
+            self.z_copy(0, m).wait_recv()
         for s in range(2):
             self.ring_copy(s, 1).start()
         self.sib_copy(0).start()
@@ -176,8 +204,68 @@
         half = self.ex.plan.half
         self.sib_copy(offset).wait_send()
         if offset == 0:
-            for k in range(1, self.ex.plan.n_z):
-                self.z_copy(k).wait_send()
+            for b, count in self.z_sizes():
+                for m in range(count):
+                    self.z_copy(b, m).wait_send()
+            for s in range(2):
+                self.ring_copy(s, 1).wait_send()
+        elif abs(offset) < half:
+            self.ring_copy(0 if offset < 0 else 1, abs(offset) + 1).wait_send()
+
+
+class RingFirst(Gather):
+    def ring_view(self, origin, s, d):
+        ex = self.ex
+        rows = ex.plan.row_half(s, self.ref.shape[3]) if d == ex.plan.half else slice(None)
+        return self.ref.at[origin, ex.z, ex.c, rows]
+
+    def panel_copy(self, offset, b, m):
+        ex = self.ex
+        view = self.ref.at[ex.at(ex.p + offset), ex.z_units(b, False)[m], ex.c]
+        at = (offset + ex.plan.n_mp) % ex.plan.n_mp, ex.z_slot(b, m)
+        return ex.push(view, view, self.zs.at[at], self.zr.at[at], ex.z_device(b))
+
+    def begin(self, offset):
+        for b in range(self.ex.plan.bits):
+            self.panel_copy(offset, b, 0).start()
+
+    def start(self):
+        for s in range(2):
+            self.ring_copy(s, 1).start()
+        self.begin(0)
+
+    def hop(self, d):
+        half = self.ex.plan.half
+        for s in range(2):
+            self.ring_copy(s, d).wait_recv()
+            if d < half:
+                self.ring_copy(s, d + 1).start()
+        if d < half:
+            self.begin(-d)
+            self.begin(d)
+        else:
+            self.begin(half)
+
+    def spread(self, offset):
+        sizes = self.z_sizes()
+        for b, count in reversed(sizes[:-1]):
+            for m in range(sizes[b + 1][1]):
+                self.panel_copy(offset, b + 1, m).wait_recv()
+            for m in range(1, count):
+                self.panel_copy(offset, b, m).start()
+
+    def column(self, offset):
+        for m in range(self.z_sizes()[0][1]):
+            self.panel_copy(offset, 0, m).wait_recv()
+        self.sib_copy(offset).start()
+
+    def wait_sent(self, offset):
+        half = self.ex.plan.half
+        self.sib_copy(offset).wait_send()
+        for b, count in self.z_sizes():
+            for m in range(count):
+                self.panel_copy(offset, b, m).wait_send()
+        if offset == 0:
             for s in range(2):
                 self.ring_copy(s, 1).wait_send()
         elif abs(offset) < half:
@@ -190,35 +278,45 @@
         self.other, self.ring, self.last = other, ring, last
         self.ss, self.sr, self.rs, self.rr, self.zs, self.zr = sems
 
-    def units(self, s, d):
-        n_z = self.ex.plan.n_z
-        return pl.ds(s * (n_z // 2), n_z // 2) if d == self.ex.plan.half else pl.ds(0, n_z)
-
     def sib_copy(self, offset):
         ex = self.ex
         at = (offset + ex.plan.n_mp) % ex.plan.n_mp
         view = self.ref.at[ex.at(ex.p + offset), :, 1 - ex.c, self.tile]
         return ex.push(view, self.other.at[at], self.ss.at[at], self.sr.at[at], ex.sib)
 
+    def ring_views(self, dest, s, d, part):
+        plan = self.ex.plan
+        at, count = plan.slots(d)
+        first = 0
+        if d == plan.half:
+            first = s * count
+        elif part is not None:
+            count = plan.n_z // 2
+            first, at = part * count, at + part * count
+        return self.ref.at[dest, pl.ds(first, count), self.ex.c, self.tile], self.ring.at[s, pl.ds(at, count)]
+
     def ring_copy(self, s, d, part=None):
         ex = self.ex
         plan = ex.plan
         sign = 1 - 2 * s
-        at, count = plan.slots(d)
-        if part is None:
-            units, slot = self.units(s, d), pl.ds(at, count)
-            sem = d - 1
-        else:
-            units, slot = pl.ds(part * (plan.n_z // 2), plan.n_z // 2), pl.ds(at + part * (plan.n_z // 2), plan.n_z // 2)
-            sem = plan.half - 2 + 2 * part
-        view = self.ref.at[ex.at(ex.p + sign * d), units, ex.c, self.tile]
-        return ex.push(view, self.ring.at[s, slot], self.rs.at[s, sem], self.rr.at[s, sem], (ex.dp, ex.at(ex.p + sign)))
-
-    def z_copy(self, k):
-        ex = self.ex
-        to = (ex.z + ex.plan.n_z - k) % ex.plan.n_z
-        view = self.ref.at[ex.i, to, ex.c, self.tile]
-        return ex.push(view, self.last.at[k - 1], self.zs.at[k - 1], self.zr.at[k - 1], (to * 2 + ex.c, ex.i))
+        sem = d - 1 if part is None else plan.half - 2 + 2 * part
+        view, there = self.ring_views(ex.at(ex.p + sign * d), s, d, part)
+        return ex.push(view, there, self.rs.at[s, sem], self.rr.at[s, sem], (ex.dp, ex.at(ex.p + sign)))
+
+    def ring_copies(self, s, d):
+        if d == self.ex.plan.half - 1:
+            return [self.ring_copy(s, d, part) for part in range(2)]
+        return [self.ring_copy(s, d)]
+
+    def z_copy(self, b, m):
+        ex = self.ex
+        view = self.ref.at[ex.i, ex.z_units(b, True)[m], ex.c, self.tile]
+        at = ex.z_slot(b, m)
+        return ex.push(view, self.last.at[at], self.zs.at[at], self.zr.at[at], ex.z_device(b))
+
+    def z_sizes(self):
+        n_z = self.ex.plan.n_z
+        return [(b, n_z // (2 << b)) for b in range(self.ex.plan.bits)]
 
     def to_sibling(self, offset):
         self.sib_copy(offset).start()
@@ -258,11 +356,8 @@
         self.ring_copy(s, half - 1, s).start()
 
     def wait_ring(self, s, d):
-        if d == self.ex.plan.half - 1:
-            for part in range(2):
-                self.ring_copy(s, d, part).wait_recv()
-        else:
-            self.ring_copy(s, d).wait_recv()
+        for copy in self.ring_copies(s, d):
+            copy.wait_recv()
 
     def nearer(self):
         plan = self.ex.plan
@@ -286,16 +381,28 @@
             (lambda u: self.ring[0, u], at),
             (lambda u: self.ring[1, u], at),
         )
-        for k in range(1, plan.n_z):
-            self.z_copy(k).start()
+        for m in range(self.z_sizes()[0][1]):
+            self.z_copy(0, m).start()
+
+    def along(self):
+        ex = self.ex
+        for b, count in self.z_sizes()[:-1]:
+            for m, unit in enumerate(ex.z_units(b, False)):
+                self.z_copy(b, m).wait_recv()
+                at = ex.z_slot(b, m)
+                self.add(0, unit, 1, (lambda u: self.last[u], at))
+            for m in range(count // 2):
+                self.z_copy(b + 1, m).start()
 
     def finish(self):
         ex = self.ex
-        value = self.ref[ex.i, ex.z, ex.c, self.tile, :].astype(F32)
-        for k in range(1, ex.plan.n_z):
-            self.z_copy(k).wait_recv()
-            value = value + self.last[k - 1].astype(F32)
-        return value
+        self.z_copy(ex.plan.bits - 1, 0).wait_recv()
+        return self.ref[ex.i, ex.z, ex.c, self.tile, :].astype(F32) + self.last[0].astype(F32)
+
+    def wait_z_sent(self):
+        for b, count in self.z_sizes():
+            for m in range(count):
+                self.z_copy(b, m).wait_send()
 
     def wait_sent(self):
         plan = self.ex.plan
@@ -303,13 +410,90 @@
             self.sib_copy(offset).wait_send()
         for s in range(2):
             for d in range(1, plan.half + 1):
-                if d == plan.half - 1:
-                    for part in range(2):
-                        self.ring_copy(s, d, part).wait_send()
-                else:
-                    self.ring_copy(s, d).wait_send()
-        for k in range(1, plan.n_z):
-            self.z_copy(k).wait_send()
+                for copy in self.ring_copies(s, d):
+                    copy.wait_send()
+        self.wait_z_sent()
+
+
+class RingLast(Reduce):
+    def panel_copy(self, offset, b, m):
+        ex = self.ex
+        view = self.ref.at[ex.at(ex.p + offset), ex.z_units(b, True)[m], ex.c, self.tile]
+        at = (offset + ex.plan.n_mp) % ex.plan.n_mp, ex.z_slot(b, m)
+        return ex.push(view, self.last.at[at], self.zs.at[at], self.zr.at[at], ex.z_device(b))
+
+    def begin(self, offset):
+        self.from_sibling(offset)
+        for m in range(self.z_sizes()[0][1]):
+            self.panel_copy(offset, 0, m).start()
+
+    def take(self, offset, b):
+        ex = self.ex
+        q = (offset + ex.plan.n_mp) % ex.plan.n_mp
+        for m, unit in enumerate(ex.z_units(b, False)):
+            self.panel_copy(offset, b, m).wait_recv()
+            self.add(offset, unit, 1, (lambda u: self.last[q, u], ex.z_slot(b, m)))
+
+    def along(self, offset):
+        for b, count in self.z_sizes()[:-1]:
+            self.take(offset, b)
+            for m in range(count // 2):
+                self.panel_copy(offset, b + 1, m).start()
+
+    def end(self, offset):
+        self.take(offset, self.ex.plan.bits - 1)
+
+    def ring_views(self, dest, s, d, part):
+        ex = self.ex
+        rows = slice(None)
+        if d == ex.plan.half:
+            rows = ex.plan.row_half(s, ex.plan.rows)
+        elif part is not None:
+            rows = ex.plan.row_half(part, ex.plan.rows)
+        return self.ref.at[dest, ex.z, ex.c, rows], self.ring.at[s, d - 1, rows]
+
+    def add_rows(self, offset, rows, *terms):
+        ex = self.ex
+        j = ex.at(ex.p + offset)
+        value = self.ref[j, ex.z, ex.c, rows, :].astype(F32)
+        for term in terms:
+            value = value + term.astype(F32)
+        self.ref[j, ex.z, ex.c, rows, :] = value.astype(BF)
+
+    def far(self):
+        for s in range(2):
+            self.ring_copy(s, self.ex.plan.half).start()
+
+    def free(self, s):
+        self.ring_copy(s, self.ex.plan.half - 1, 1 - s).start()
+
+    def bound(self, s):
+        plan = self.ex.plan
+        half = plan.half
+        self.ring_copy(s, half).wait_recv()
+        rows = plan.row_half(s, plan.rows)
+        self.add_rows((1 - 2 * s) * (half - 1), rows, self.ring[s, half - 1, rows, :])
+        self.ring_copy(s, half - 1, s).start()
+
+    def nearer(self):
+        for d in range(self.ex.plan.half - 2, 0, -1):
+            for s in range(2):
+                self.wait_ring(s, d + 1)
+                self.add_rows((1 - 2 * s) * d, slice(None), self.ring[s, d])
+                self.ring_copy(s, d).start()
+
+    def finish(self):
+        ex = self.ex
+        for s in range(2):
+            self.wait_ring(s, 1)
+        value = self.ref[ex.i, ex.z, ex.c].astype(F32)
+        return value + self.ring[0, 0].astype(F32) + self.ring[1, 0].astype(F32)
+
+    def wait_z_sent(self):
+        for offset in range(self.ex.plan.n_mp):
+            for b, count in self.z_sizes():
+                for m in range(count):
+                    self.panel_copy(offset, b, m).wait_send()
 
 
 class Rows:
@@ -355,54 +539,76 @@
 
 
 def step_kernel(plan, n_in, *refs):
-    (tab, dev, slots, w_qkv, w_out, w_up, w_down, tok, fv, cot) = refs[:n_in]
-    (o_out, o_dx, o_df, o_q, o_s, o_o, o_f) = refs[n_in : n_in + 7]
+    (tab, dev, w_qkv, w_out, w_up, w_down, tok, fv, cot), small = refs[:9], refs[9:n_in]
+    (o_out, o_dx, o_df, o_q, o_s, o_o, o_u, o_d) = refs[n_in : n_in + 8]
     (
-        gq, go, gf, x3, f3, y3, out3, dx3, df3,
-        q_other, q_ring, q_last, s_other, s_ring, s_last, o_other, o_ring, o_last, f_other, f_ring, f_last,
+        gq, go, gu, gd, x3, f3, y3, out3, dx3, df3,
+        q_other, q_ring, q_last, s_other, s_ring, s_last, o_other, o_ring, o_last, u_other, u_ring, u_last,
+        d_other, d_ring, d_last,
         wq, wo, sv, vec, ub, hl, hlt, qkv, ot, otb, lse, mid, n2, inv2, h2, h2t, yt,
         big, acc, act, du, dv, dk, dqt, sums, ubg,
-    ) = refs[n_in + 7 : n_in + 7 + 47]
-    sems = refs[n_in + 7 + 47 :]
+    ) = refs[n_in + 8 : n_in + 8 + 51]
+    sems = refs[n_in + 8 + 51 :]
     R, C, n_mp, n_dp, n_z = plan.rows, plan.cols, plan.n_mp, plan.n_dp, plan.n_z
     step = 64
     ex = Exchange(plan)
     i, z, c = ex.i, ex.z, ex.c
     Q = Gather(ex, gq, sems[0:6])
-    O = Gather(ex, go, sems[6:12])
-    F = Gather(ex, gf, sems[12:18])
-    RQ = Reduce(ex, gq, slice(0, R), q_other, q_ring, q_last, sems[18:24])
-    RS = Reduce(ex, gq, slice(R, R + 16), s_other, s_ring, s_last, sems[24:30])
-    RO = Reduce(ex, go, slice(0, R // 3), o_other, o_ring, o_last, sems[30:36])
-    RF = Reduce(ex, gf, slice(0, 2 * R), f_other, f_ring, f_last, sems[36:42])
-    a2a = sems[42:54]
+    O = RingFirst(ex, go, sems[6:12])
+    U = Gather(ex, gu, sems[12:18])
+    W = RingFirst(ex, gd, sems[18:24])
+    RQ = Reduce(ex, gq, slice(0, R), q_other, q_ring, q_last, sems[24:30])
+    RS = Reduce(ex, gq, slice(R, R + 16), s_other, s_ring, s_last, sems[30:36])
+    RO = Reduce(ex, go, slice(0, R // 3), o_other, o_ring, o_last, sems[36:42])
+    RU = Reduce(ex, gu, slice(0, R), u_other, u_ring, u_last, sems[42:48])
+    RD = RingLast(ex, gd, slice(0, R), d_other, d_ring, d_last, sems[48:54])
+    a2a = sems[54:66]
     XT = Rows(ex, tok, x3, a2a[0], a2a[1], False)
     XF = Rows(ex, fv, f3, a2a[2], a2a[3], False)
     XY = Rows(ex, cot, y3, a2a[4], a2a[5], False)
     YO = Rows(ex, out3, o_out, a2a[6], a2a[7], True)
     YX = Rows(ex, dx3, o_dx, a2a[8], a2a[9], True)
     YF = Rows(ex, df3, o_df, a2a[10], a2a[11], True)
+    near = range(-plan.half + 1, plan.half)
 
     third = R // 3
     gq[i, z, c, 0:R, 0 : plan.qkv] = w_qkv[...]
-    gq[i, z, c, R:, :] = slots[...]
+    sv[0, 0:16, :] = jnp.zeros((16, plan.qw), F32)
+    for r in range(plan.vec_rows):
+        pieces = [small[v][...] for v in range(r * plan.spr, min((r + 1) * plan.spr, N_VEC))]
+        for k, piece in enumerate(pieces):
+            sv[0, r : r + 1, k * 128 : k * 128 + piece.shape[0]] = piece.astype(F32)[None]
+    gq[i, z, c, R:, :] = sv[0, 0:16, :].astype(BF)
     for t in range(3):
         go[i, z, c, :, t * plan.group : t * plan.group + plan.out] = w_out[t * third : (t + 1) * third, :]
-    gf[i, z, c, 0:R, :] = w_up[...]
-    gf[i, z, c, R:, :] = w_down[...].T
+    gu[i, z, c] = w_up[...]
+    gd[i, z, c] = w_down[...]
     ex.greet()
     Q.start()
     O.start()
     XT.start()
+    Q.spread()
+    Q.column()
+    U.start()
+    W.start()
+    O.hop(1)
+    for d in range(2, plan.half + 1):
+        O.hop(d)
+    O.spread(0)
     XF.start()
-    F.start()
-    Q.column()
-    O.column()
-    for d in range(1, plan.half):
+    U.spread()
+    Q.hop(1)
+    W.hop(1)
+    W.spread(0)
+    for offset in (*near, plan.half):
+        if offset:
+            O.spread(offset)
+        O.column(offset)
+    XY.start()
+    U.column()
+    for d in range(2, plan.half + 1):
         Q.hop(d)
-        O.hop(d)
-    F.column()
-    XY.start()
+        W.hop(d)
 
     rowdev = dev[:, 0:1]
     row = lambda v: vec[v : v + 1, :]
@@ -420,10 +626,8 @@
         def _(at):
             body(at, pl.ds(pl.multiple_of(at * step, step), step))
 
-    Q.hop(plan.half)
-    O.hop(plan.half)
     for piece in (Q, O):
-        for offset in range(-plan.half + 1, plan.half + 1):
+        for offset in (*near, plan.half):
             piece.wait_sib(offset)
 
     for j in range(n_mp):
@@ -500,11 +704,16 @@
                 ot[pl.ds(pl.multiple_of(t * 128 + e * HEAD, HEAD), HEAD), span] = o
                 lse[t, e : e + 1, span] = top + jnp.log(total)
 
+        @pl.when(t == 0)
+        def _():
+            W.column(0)
+
         for d in range(1, plan.half):
 
-            @pl.when(t == 2 + d)
+            @pl.when(t == 2 * d)
             def _():
-                F.hop(d)
+                W.spread(-d)
+                W.spread(d)
 
     otb[...] = ot[...].astype(BF)
     du[:, 0:D] = otb[...].T
@@ -518,6 +727,9 @@
         h2[rows, :] = (scaled * row(G2) + row(B2)).astype(BF)
 
     blocks(128, second_norm)
+    W.spread(plan.half)
+    for d in range(1, plan.half):
+        U.hop(d)
     h2t[...] = h2[...].T
     XY.wait_here()
     XY.wait_sent()
@@ -525,54 +737,71 @@
     acc[...] = jnp.zeros_like(acc)
     big[...] = jnp.zeros_like(big)
 
-    offset_of = lambda q: (q + 1) // 2 * (1 - 2 * (q % 2))
+    order = [0, plan.half]
+    for d in range(plan.half - 1, 0, -1):
+        order += [-d, d]
+
+    def nth(q):
+        d = plan.half - q // 2
+        return jnp.where(q == 0, 0, jnp.where(q == 1, plan.half, d * (2 * (q % 2) - 1)))
+
+    def ring_turn(r, offset):
+        if offset == plan.half:
+            r.far()
+        elif abs(offset) == plan.half - 1:
+            r.free(0 if offset > 0 else 1)
 
     @pl.loop(0, n_mp)
     def _(q):
-        j = ex.at(ex.p + offset_of(q))
-        for s in range(n_mp):
+        j = ex.at(ex.p + nth(q))
+        for s, offset in enumerate(order):
 
             @pl.when(q == s)
             def _():
-                if s == n_mp - 1:
-                    F.hop(plan.half)
-                F.wait_sib(plan.half if s == n_mp - 1 else offset_of(s))
-
-        bias = ub[pl.ds(j, 1), :]
-
-        def rows(at, rows):
-            up = gf[j, :, :, 0:R, :].reshape(D, C)
-            down = gf[j, :, :, R : 2 * R, :].reshape(D, C)
-            u = dot(h2[rows, :], up) + bias
-            u2 = u * u
-            tangent = jnp.tanh(GELU_C * (u + GELU_A * u2 * u))
-            half = 0.5 * (1.0 + tangent)
-            a = (u * half).astype(BF)
-            slope = half + 0.5 * u * (1.0 - tangent * tangent) * GELU_C * (1.0 + 3.0 * GELU_A * u2)
-            act[rows, :] = a
-            acc[rows, :] += dot_nt(a, down)
-            g = (dot(rows_of(y3, at, 128)[...], down) * slope).astype(BF)
-            du[rows, 0:C] = g
-            big[rows, :] += dot_nt(g, up)
-
-        blocks(128, rows)
-        for s in range(n_mp):
+                if s == 1:
+                    U.hop(plan.half)
+                    for other in (*near, plan.half):
+                        if other:
+                            W.column(other)
+                U.wait_sib(offset)
+                W.wait_sib(offset)
+
+        up = gu[j].reshape(D, C)
+        down = gd[j].reshape(D, C)
+        u = dot(h2[...], up) + ub[pl.ds(j, 1), :]
+        u2 = u * u
+        tangent = jnp.tanh(GELU_C * (u + GELU_A * u2 * u))
+        half = 0.5 * (1.0 + tangent)
+        a = (u * half).astype(BF)
+        slope = half + 0.5 * u * (1.0 - tangent * tangent) * GELU_C * (1.0 + 3.0 * GELU_A * u2)
+        act[...] = a
+        acc[...] += dot_nt(a, down)
+        g = (dot(y3[...].reshape(SEQ, D), down) * slope).astype(BF)
+        du[:, 0:C] = g
+        big[...] += dot_nt(g, up)
+        for s, offset in enumerate(order):
 
             @pl.when(q == s)
             def _():
-                F.wait_sent(plan.half if s == n_mp - 1 else offset_of(s))
-
-        gf[j, :, :, R : 2 * R, :] = dot(yt[...], act[...]).astype(BF).reshape(n_z, 2, R, C)
-        gf[j, :, :, 0:R, :] = dot(h2t[...], du[:, 0:C]).astype(BF).reshape(n_z, 2, R, C)
+                if s >= 1:
+                    RD.begin(order[s - 1])
+                    ring_turn(RU, order[s - 1])
+                W.wait_sent(offset)
+                U.wait_sent(offset)
+
+        gd[j] = dot(yt[...], act[...]).astype(BF).reshape(n_z, 2, R, C)
+        gu[j] = dot(h2t[...], du[:, 0:C]).astype(BF).reshape(n_z, 2, R, C)
         ubg[pl.ds(j, 1), :] = jnp.sum(du[:, 0:C].astype(F32), axis=0, keepdims=True)
-        for s in range(n_mp):
+        for s, offset in enumerate(order):
 
             @pl.when(q == s)
             def _():
-                RF.to_sibling(plan.half if s == n_mp - 1 else offset_of(s))
-                if s == n_mp - 1:
-                    RF.free(1)
-                    RF.free(0)
+                RD.to_sibling(offset)
+                RU.to_sibling(offset)
+                if s >= 3:
+                    RD.along(order[s - 3])
+                if s >= 4:
+                    RD.end(order[s - 4])
 
     sums[...] = jnp.zeros_like(sums)
 
@@ -593,9 +822,11 @@
         sums[DB : DB + 1, :] += total(dy)
 
     blocks(step, second_back)
-    RF.far()
+    RD.begin(order[-1])
+    ring_turn(RU, order[-1])
     YO.start()
-    for offset in range(-plan.half + 1, plan.half + 1):
+    RD.along(order[-3])
+    for offset in (*near, plan.half):
         O.wait_sent(offset)
         Q.wait_sent(offset)
     for j in range(n_mp):
@@ -641,33 +872,54 @@
         qkv[:, cols(D)] = dk[...].astype(BF)
         qkv[:, cols(2 * D)] = dv[...].astype(BF)
 
+        @pl.when(t == 0)
+        def _():
+            for s in range(2):
+                RU.bound(s)
+            RD.end(order[-4])
+
         @pl.when(t == 1)
         def _():
+            RD.along(order[-2])
+
+        @pl.when(t == 2)
+        def _():
+            RU.nearer()
             for s in range(2):
-                RF.bound(s)
+                RO.bound(s)
 
         @pl.when(t == 3)
         def _():
-            RF.nearer()
-            for s in range(2):
-                RO.bound(s)
+            RD.along(order[-1])
+            RD.end(order[-3])
+            RO.nearer()
+            if plan.half == 2:
+                RD.far()
+
+        @pl.when(t == 4)
+        def _():
+            RU.home()
 
         @pl.when(t == 5)
         def _():
-            RO.nearer()
+            RO.home()
 
     df3[...] = qkv[:, QKV : 3 * D].reshape(df3.shape)
     YF.start()
     for j in range(n_mp):
         g = dot(hlt[...], qkv[:, j * plan.qkv : (j + 1) * plan.qkv]).astype(BF)
         gq[j, :, :, 0:R, 0 : plan.qkv] = g.reshape(n_z, 2, R, plan.qkv)
-    for offset in (plan.half, *range(-plan.half + 1, plan.half)):
+    for offset in (plan.half, *near):
         RQ.to_sibling(offset)
-    RF.home()
     RQ.far()
     RQ.free(0)
     RQ.free(1)
-    RO.home()
+    RD.end(order[-2])
+    RD.end(order[-1])
+    if plan.half != 2:
+        RD.far()
+    RD.free(0)
+    RD.free(1)
 
     def project_back(at, rows):
         acc[rows, :] = dot_nt(qkv[rows, 0:QKV], wq[...])
@@ -710,27 +962,35 @@
             gq[j, d // 2, d % 2, R:, :] = value.astype(BF)
     for offset in range(n_mp):
         RS.to_sibling(offset)
-    o_f[...] = RF.finish()
+    RQ.nearer()
     RS.far()
     RS.free(0)
     RS.free(1)
-    RQ.nearer()
-    o_o[...] = RO.finish()
+    RU.along()
+    RO.along()
+    for s in range(2):
+        RD.bound(s)
+    RD.nearer()
     for s in range(2):
         RS.bound(s)
     RQ.home()
     RS.nearer()
     RS.home()
+    o_u[...] = RU.finish()
+    o_o[...] = RO.finish()
+    RQ.along()
+    RS.along()
+    o_d[...] = RD.finish()
     o_q[...] = RQ.finish()
     o_s[...] = RS.finish()
-    for r in (RF, RO, RQ, RS):
+    for r in (RU, RD, RO, RQ, RS):
         r.wait_sent()
     for r in (YO, YF, YX):
         r.wait_sent()
         r.wait_here()
 
 
-def step(plan, slots, w_qkv, w_out, w_up, w_down, tok, fv, cot):
+def step(plan, w_qkv, w_out, w_up, w_down, tok, fv, cot, small):
     R, C, n_mp, n_z, n = plan.rows, plan.cols, plan.n_mp, plan.n_z, plan.n
     count = np.arange(D, dtype=np.int32)
     tab = np.zeros((8, D), np.int32)
@@ -752,10 +1012,16 @@
             vm((n_z - 1, rows, cols), BF),
         ]
 
+    down_sums = [
+        vm((n_mp, n_z, R, C), BF),
+        vm((2, plan.half, R, C), BF),
+        vm((n_mp, n_z - 1, R, C), BF),
+    ]
+    panel_z = [dma((n_mp, n_z - 1))] * 2
     gather_sems = [dma((n_z - 1,))] * 2 + [dma((2, plan.half))] * 2 + [dma((n_mp,))] * 2
     reduce_sems = [dma((n_mp,))] * 2 + [dma((2, plan.half + 1))] * 2 + [dma((n_z - 1,))] * 2
     shape = jax.ShapeDtypeStruct
-    ins = (jnp.asarray(tab), jnp.asarray(dev), slots, w_qkv, w_out, w_up, w_down, tok, fv, cot)
+    ins = (jnp.asarray(tab), jnp.asarray(dev), w_qkv, w_out, w_up, w_down, tok, fv, cot, *small)
     return pl.pallas_call(
         functools.partial(step_kernel, plan, len(ins)),
         name="step",
@@ -766,15 +1032,16 @@
             shape((R, plan.qw), F32),
             shape((16, plan.qw), F32),
             shape((R // 3, C), F32),
-            shape((2 * R, C), F32),
+            shape((R, C), F32),
+            shape((R, C), F32),
         ),
-        in_specs=[IN_VMEM] * 7 + [ANY] * 3,
-        out_specs=(ANY,) * 3 + (IN_VMEM,) * 4,
+        in_specs=[IN_VMEM] * 6 + [ANY] * 3 + [IN_VMEM] * N_VEC,
+        out_specs=(ANY,) * 3 + (IN_VMEM,) * 5,
         scratch_shapes=[
-            panel(R + 16, plan.qw), panel(R // 3, C), panel(2 * R, C),
+            panel(R + 16, plan.qw), panel(R // 3, C), panel(R, C), panel(R, C),
             vm(tok.shape, BF), vm(fv.shape, BF), vm(cot.shape, BF),
             vm(tok.shape, BF), vm(tok.shape, BF), vm(fv.shape, BF),
-            *sums(R, plan.qw), *sums(16, plan.qw), *sums(R // 3, C), *sums(2 * R, C),
+            *sums(R, plan.qw), *sums(16, plan.qw), *sums(R // 3, C), *sums(R, C), *down_sums,
             vm((D, QKV), BF), vm((D, D), BF),
             vm((plan.vec_rows, n, plan.qw), F32), vm((16, D), F32), vm((max(8, n_mp), C), F32),
             wide(BF), tall(BF), vm((SEQ, 3 * D), BF), tall(F32), tall(BF),
@@ -783,8 +1050,12 @@
             wide(F32), wide(F32), vm((SEQ, C), BF), wide(BF),
             vm((SEQ, 128), F32), vm((SEQ, 128), F32), vm((128, SEQ), F32),
             vm((16, D), F32), vm((max(8, n_mp), C), F32),
-            *(gather_sems * 3),
+            *gather_sems,
+            *(panel_z + gather_sems[2:]),
+            *gather_sems,
+            *(panel_z + gather_sems[2:]),
             *(reduce_sems * 4),
+            *(reduce_sems[:4] + panel_z),
             *([dma((MICRO,))] * 12),
         ],
         compiler_params=pltpu.CompilerParams(
@@ -793,32 +1064,49 @@
     )(*ins)
 
 
+def unpack_kernel(plan, widths, *refs):
+    (r1, r2, r3, t_q, t_s, t_o, t_u, t_d), outs, sem = refs[:8], refs[8:24], refs[24]
+    moves = [pltpu.make_async_copy(src, dst, sem.at[k]) for k, (src, dst) in enumerate(zip((r1, r2, r3), outs[:3]))]
+    for move in moves:
+        move.start()
+    outs[5][...] = t_q[:, 0 : plan.qkv]
+    third = plan.rows // 3
+    for t in range(3):
+        outs[8][t * third : (t + 1) * third, :] = t_o[:, t * plan.group : t * plan.group + plan.out]
+    outs[12][...] = t_u[...]
+    outs[14][...] = t_d[...]
+    for v, at in enumerate((3, 4, 6, 7, 9, 10, 11, 13, 15)):
+        row, lane = v // plan.spr, (v % plan.spr) * 128
+        outs[at][...] = t_s[row, lane : lane + widths[v]]
+    for move in moves:
+        move.wait()
+
+
+def unpack(plan, summed, widths):
+    shape = lambda *dims: jax.ShapeDtypeStruct(dims, F32)
+    vec = [shape(w) for w in widths]
+    R, C = plan.rows, plan.cols
+    out_shape = [jax.ShapeDtypeStruct(r.shape, BF) for r in summed[:3]]
+    out_shape += [vec[0], vec[1], shape(R, plan.qkv), vec[2], vec[3], shape(R, plan.out)]
+    out_shape += [vec[4], vec[5], vec[6], shape(R, C), vec[7], shape(R, C), vec[8]]
+    return pl.pallas_call(
+        functools.partial(unpack_kernel, plan, widths),
+        name="unpack",
+        out_shape=tuple(out_shape),
+        in_specs=[IN_VMEM] * 3 + [IN_VMEM] * 5,
+        out_specs=(ANY,) * 3 + (IN_VMEM,) * 13,
+        scratch_shapes=[pltpu.SemaphoreType.DMA((3,))],
+    )(*summed)
+
+
 def shards(
     plan, tokens, first_values, out_cot, ln1_gain, ln1_bias, w_qkv, q_bias, v_bias, w_out, out_bias,
     ln2_gain, ln2_bias, w_up, up_bias, w_down, down_bias,
 ):
     small = (ln1_gain, ln1_bias, q_bias, v_bias, out_bias, ln2_gain, ln2_bias, up_bias, down_bias)
-    widths = [s.shape[0] for s in small]
-    slots = jnp.concatenate([jnp.pad(s, (0, 128 - s.shape[0])) for s in small])
-    slots = jnp.pad(slots, (0, 16 * plan.qw - slots.shape[0])).reshape(16, plan.qw)
-    r1, r2, r3, t_q, t_s, t_o, t_f = step(
-        plan, slots, w_qkv, w_out, w_up, w_down, tokens, first_values, out_cot
-    )
-    R, spr = plan.rows, plan.spr
-    s = [t_s[v // spr, (v % spr) * 128 : (v % spr) * 128 + w] for v, w in enumerate(widths)]
-    t_o = jnp.concatenate([t_o[:, t * plan.group : t * plan.group + plan.out] for t in range(3)], axis=0)
-    return (
-        r1, r2, r3,
-        s[0], s[1],
-        t_q[:, : plan.qkv],
-        s[2], s[3],
-        t_o,
-        s[4], s[5], s[6],
-        t_f[:R],
-        s[7],
-        t_f[R:].T,
-        s[8],
-    )
+    summed = step(plan, w_qkv, w_out, w_up, w_down.T, tokens, first_values, out_cot, small)
+    outs = unpack(plan, summed, [s.shape[0] for s in small])
+    return (*outs[:14], outs[14].T, outs[15])
 
 
 def solution(mesh):

time: 230 us -> 196 us (0.85)
  local copies, waits for them, and re-layouts: 19.2 us -> 0 us
  Pallas kernels: 209 us -> 194 us
    pallas_call x1, Pallas kernels: 209 us -> 190 us  [step(): pl.pallas_call(functools.partial(step_kernel, plan, len(ins)), name='step...]
    unnamed x39 -> x0, local copies, waits for them, and re-layouts: 12 us -> none
    pallas_call x0 -> x1, Pallas kernels: none -> 3.98 us  [unpack(): pl.pallas_call(functools.partial(unpack_kernel, plan, widths), name='unpa...]
    squeeze x3 -> x0, local copies, waits for them, and re-layouts: 3.69 us -> none  [shards(): t_s[v // spr, v % spr * 128:v % spr * 128 + w]]
where the time goes in v4:
time: 196 us; the launch traced here: 195 us
  Pallas kernels  194 us (99%)
    pallas_call x1, Pallas kernels, step(): pl.pallas_call(functools.partial(step_kernel, plan, len(ins)), name='step...  190 us
    pallas_call x1, Pallas kernels, unpack(): pl.pallas_call(functools.partial(unpack_kernel, plan, widths), name='unpa...  3.98 us

profile of v4, /device:TPU:1, one launch (start us, length us, event | category | flops | bytes accessed | tf_op | source)
XLA Modules:
  0.0 195.1 jit_solution(3401666261076272468)
XLA Ops:
  0.7 190.3 %step.1 = (bf16[4,128,768]{2,1,0:T(8,128)(2,1)}, bf16[4,128,768]{2,1,0:T(8,128)(2,1)}, bf16[4,128,384]{2,1,0:T(8,128)(2,1)}, f32[96,512]{1,0:T(8,128)}, f32[16,5...) custom-call(s32[8,768]{1,0:T(8,128)} %constant.4.clone.refs_0_, ...), custom_call_target="tpu_custom_call" | custom-call | tf_op jit(solution)/shard_map/step/pallas_call | solution.py:1025
  191.0 4.0 %unpack.1 = (bf16[4,128,768]{2,1,0:T(8,128)(2,1)}, bf16[4,128,768]{2,1,0:T(8,128)(2,1)}, bf16[4,128,384]{2,1,0:T(8,128)(2,1)}, f32[24]{0:T(128)}, f32[24]{0:T(12...) custom-call(bf16[4,128,768]{2,1,0:T(8,128)(2,1)} %get-tuple-element., ...), custom_call_target="tpu_custom_call" | custom-call | tf_op jit(solution)/shard_map/unpack/pallas_call | solution.py:1092

commit v5 on v4

--- a/solution.py
+++ b/solution.py
@@ -137,20 +137,20 @@
 
 
 class Gather:
-    def __init__(self, ex, ref, sems):
-        self.ex, self.ref = ex, ref
+    def __init__(self, ex, ref, sems, tile=slice(None)):
+        self.ex, self.ref, self.tile = ex, ref, tile
         self.zs, self.zr, self.rs, self.rr, self.ss, self.sr = sems
 
     def z_copy(self, b, m):
         ex = self.ex
-        view = self.ref.at[ex.i, ex.z_units(b, False)[m], ex.c]
+        view = self.ref.at[ex.i, ex.z_units(b, False)[m], ex.c, self.tile]
         at = ex.z_slot(b, m)
         return ex.push(view, view, self.zs.at[at], self.zr.at[at], ex.z_device(b))
 
     def ring_view(self, origin, s, d):
         n_z, half = self.ex.plan.n_z, self.ex.plan.half
         units = pl.ds(s * (n_z // 2), n_z // 2) if d == half else pl.ds(0, n_z)
-        return self.ref.at[origin, units, self.ex.c]
+        return self.ref.at[origin, units, self.ex.c, self.tile]
 
     def ring_copy(self, s, d):
         ex = self.ex
@@ -161,7 +161,7 @@
     def sib_copy(self, offset):
         ex = self.ex
         at = (offset + ex.plan.n_mp) % ex.plan.n_mp
-        view = self.ref.at[ex.at(ex.p + offset), :, ex.c]
+        view = self.ref.at[ex.at(ex.p + offset), :, ex.c, self.tile]
         return ex.push(view, view, self.ss.at[at], self.sr.at[at], ex.sib)
 
     def start(self):
@@ -229,10 +229,9 @@
         for b in range(self.ex.plan.bits):
             self.panel_copy(offset, b, 0).start()
 
-    def start(self):
+    def circle(self):
         for s in range(2):
             self.ring_copy(s, 1).start()
-        self.begin(0)
 
     def hop(self, d):
         half = self.ex.plan.half
@@ -416,6 +415,9 @@
 
 
 class RingLast(Reduce):
+    def half_rows(self, s):
+        return self.ex.plan.row_half(s, self.ref.shape[3])
+
     def panel_copy(self, offset, b, m):
         ex = self.ex
         view = self.ref.at[ex.at(ex.p + offset), ex.z_units(b, True)[m], ex.c, self.tile]
@@ -447,9 +449,9 @@
         ex = self.ex
         rows = slice(None)
         if d == ex.plan.half:
-            rows = ex.plan.row_half(s, ex.plan.rows)
+            rows = self.half_rows(s)
         elif part is not None:
-            rows = ex.plan.row_half(part, ex.plan.rows)
+            rows = self.half_rows(part)
         return self.ref.at[dest, ex.z, ex.c, rows], self.ring.at[s, d - 1, rows]
 
     def add_rows(self, offset, rows, *terms):
@@ -471,7 +473,7 @@
         plan = self.ex.plan
         half = plan.half
         self.ring_copy(s, half).wait_recv()
-        rows = plan.row_half(s, plan.rows)
+        rows = self.half_rows(s)
         self.add_rows((1 - 2 * s) * (half - 1), rows, self.ring[s, half - 1, rows, :])
         self.ring_copy(s, half - 1, s).start()
 
@@ -554,15 +556,16 @@
     ex = Exchange(plan)
     i, z, c = ex.i, ex.z, ex.c
     Q = Gather(ex, gq, sems[0:6])
-    O = RingFirst(ex, go, sems[6:12])
-    U = Gather(ex, gu, sems[12:18])
-    W = RingFirst(ex, gd, sems[18:24])
-    RQ = Reduce(ex, gq, slice(0, R), q_other, q_ring, q_last, sems[24:30])
-    RS = Reduce(ex, gq, slice(R, R + 16), s_other, s_ring, s_last, sems[30:36])
-    RO = Reduce(ex, go, slice(0, R // 3), o_other, o_ring, o_last, sems[36:42])
+    O = Gather(ex, go, sems[6:12])
+    U1 = Gather(ex, gu, sems[12:18], plan.row_half(0, R))
+    U2 = Gather(ex, gu, sems[18:24], plan.row_half(1, R))
+    W = RingFirst(ex, gd, sems[24:30])
+    RQ = Reduce(ex, gq, slice(0, R), q_other, q_ring, q_last, sems[30:36])
+    RS = Reduce(ex, gq, slice(R, R + 16), s_other, s_ring, s_last, sems[36:42])
     RU = Reduce(ex, gu, slice(0, R), u_other, u_ring, u_last, sems[42:48])
-    RD = RingLast(ex, gd, slice(0, R), d_other, d_ring, d_last, sems[48:54])
-    a2a = sems[54:66]
+    RO = RingLast(ex, go, slice(0, R // 3), o_other, o_ring, o_last, sems[48:54])
+    RD = RingLast(ex, gd, slice(0, R), d_other, d_ring, d_last, sems[54:60])
+    a2a = sems[60:72]
     XT = Rows(ex, tok, x3, a2a[0], a2a[1], False)
     XF = Rows(ex, fv, f3, a2a[2], a2a[3], False)
     XY = Rows(ex, cot, y3, a2a[4], a2a[5], False)
@@ -585,30 +588,28 @@
     gd[i, z, c] = w_down[...]
     ex.greet()
     Q.start()
-    O.start()
     XT.start()
     Q.spread()
     Q.column()
-    U.start()
-    W.start()
-    O.hop(1)
+    O.start()
+    W.circle()
+    W.begin(0)
+    U1.start()
+    U2.start()
+    W.hop(1)
+    O.spread()
     for d in range(2, plan.half + 1):
-        O.hop(d)
-    O.spread(0)
+        W.hop(d)
+    Q.hop(1)
     XF.start()
-    U.spread()
-    Q.hop(1)
-    W.hop(1)
-    W.spread(0)
-    for offset in (*near, plan.half):
-        if offset:
-            O.spread(offset)
-        O.column(offset)
-    XY.start()
-    U.column()
+    U1.spread()
+    U2.spread()
+    O.column()
     for d in range(2, plan.half + 1):
         Q.hop(d)
-        W.hop(d)
+    XY.start()
+    for d in range(1, plan.half):
+        O.hop(d)
 
     rowdev = dev[:, 0:1]
     row = lambda v: vec[v : v + 1, :]
@@ -626,19 +627,13 @@
         def _(at):
             body(at, pl.ds(pl.multiple_of(at * step, step), step))
 
-    for piece in (Q, O):
-        for offset in (*near, plan.half):
-            piece.wait_sib(offset)
+    for offset in (*near, plan.half):
+        Q.wait_sib(offset)
 
     for j in range(n_mp):
         for d in range(n_dp):
             rows = slice(d * R, (d + 1) * R)
             wq[rows, j * plan.qkv : (j + 1) * plan.qkv] = gq[j, d // 2, d % 2, 0:R, 0 : plan.qkv]
-            for t in range(3):
-                rows = slice(d * R + t * third, d * R + (t + 1) * third)
-                wo[rows, j * plan.out : (j + 1) * plan.out] = go[
-                    j, d // 2, d % 2, :, t * plan.group : t * plan.group + plan.out
-                ]
     for r in range(plan.vec_rows):
         for j in range(n_mp):
             for d in range(n_dp):
@@ -655,6 +650,9 @@
     for j in range(n_mp):
         ub[j : j + 1, :] = expand(UP_BIAS, e96, tab[5:6, :C] + j * n_dp)
 
+    W.spread(0)
+    U1.column()
+    U2.column()
     XT.wait_here()
     XT.wait_sent()
 
@@ -667,15 +665,14 @@
     XF.wait_here()
     XF.wait_sent()
 
-    def project(at, rows):
-        h = hl[rows, :]
-        q = dot(h, wq[:, 0:D]) + row(QB)
-        qkv[rows, 0:D] = q.astype(BF) * 0.125
-        qkv[rows, D : 2 * D] = dot(h, wq[:, D : 2 * D]).astype(BF)
-        v = dot(h, wq[:, 2 * D : QKV]) + row(V_BIAS)[:, :VFRESH]
-        qkv[rows, 2 * D : QKV] = v.astype(BF)
-
-    blocks(256, project)
+    q = dot(hl[...], wq[:, 0:D]) + row(QB)
+    qkv[:, 0:D] = q.astype(BF) * 0.125
+    qkv[:, D : 2 * D] = dot(hl[...], wq[:, D : 2 * D]).astype(BF)
+    v = dot(hl[...], wq[:, 2 * D : QKV]) + row(V_BIAS)[:, :VFRESH]
+    qkv[:, 2 * D : QKV] = v.astype(BF)
+    for offset in near:
+        if offset:
+            W.spread(offset)
     qkv[:, QKV : 3 * D] = f3[...].reshape(SEQ, D // 2)
 
     B = 256
@@ -706,30 +703,43 @@
 
         @pl.when(t == 0)
         def _():
+            O.hop(plan.half)
+            W.spread(plan.half)
+
+        @pl.when(t == 4)
+        def _():
             W.column(0)
 
-        for d in range(1, plan.half):
-
-            @pl.when(t == 2 * d)
-            def _():
-                W.spread(-d)
-                W.spread(d)
-
+    for offset in (*near, plan.half):
+        O.wait_sib(offset)
+    for j in range(n_mp):
+        for d in range(n_dp):
+            for t in range(3):
+                rows = slice(d * R + t * third, d * R + (t + 1) * third)
+                wo[rows, j * plan.out : (j + 1) * plan.out] = go[
+                    j, d // 2, d % 2, :, t * plan.group : t * plan.group + plan.out
+                ]
     otb[...] = ot[...].astype(BF)
     du[:, 0:D] = otb[...].T
 
+    acc[...] = dot(du[:, 0:D], wo[...]) + row(OB)
+
     def second_norm(at, rows):
-        m = rows_of(x3, at, 128)[...].astype(F32) + (dot(du[rows, 0:D], wo[...]) + row(OB))
+        m = rows_of(x3, at, step)[...].astype(F32) + acc[rows, :]
         mid[rows, :] = m
         scaled, inv = norm_stats(m)
         n2[rows, :] = scaled
-        inv2[rows, :] = jnp.broadcast_to(inv, (128, 128))
+        inv2[rows, :] = jnp.broadcast_to(inv, (step, 128))
         h2[rows, :] = (scaled * row(G2) + row(B2)).astype(BF)
 
-    blocks(128, second_norm)
-    W.spread(plan.half)
+    blocks(step, second_norm)
+    W.column(plan.half)
+    for offset in near:
+        if offset:
+            W.column(offset)
     for d in range(1, plan.half):
-        U.hop(d)
+        U1.hop(d)
+        U2.hop(d)
     h2t[...] = h2[...].T
     XY.wait_here()
     XY.wait_sent()
@@ -759,11 +769,11 @@
             @pl.when(q == s)
             def _():
                 if s == 1:
-                    U.hop(plan.half)
-                    for other in (*near, plan.half):
-                        if other:
-                            W.column(other)
-                U.wait_sib(offset)
+                    U1.hop(plan.half)
+                    U2.hop(plan.half)
+                    RD.begin(order[0])
+                U1.wait_sib(offset)
+                U2.wait_sib(offset)
                 W.wait_sib(offset)
 
         up = gu[j].reshape(D, C)
@@ -783,11 +793,16 @@
 
             @pl.when(q == s)
             def _():
-                if s >= 1:
+                if s == 2:
+                    RD.along(order[0])
+                if s >= 3:
                     RD.begin(order[s - 1])
                     ring_turn(RU, order[s - 1])
+                if s >= 4:
+                    RD.along(order[s - 3])
                 W.wait_sent(offset)
-                U.wait_sent(offset)
+                U1.wait_sent(offset)
+                U2.wait_sent(offset)
 
         gd[j] = dot(yt[...], act[...]).astype(BF).reshape(n_z, 2, R, C)
         gu[j] = dot(h2t[...], du[:, 0:C]).astype(BF).reshape(n_z, 2, R, C)
@@ -798,10 +813,9 @@
             def _():
                 RD.to_sibling(offset)
                 RU.to_sibling(offset)
-                if s >= 3:
-                    RD.along(order[s - 3])
-                if s >= 4:
-                    RD.end(order[s - 4])
+                if s == 2:
+                    RD.begin(order[1])
+                    ring_turn(RU, order[1])
 
     sums[...] = jnp.zeros_like(sums)
 
@@ -822,10 +836,9 @@
         sums[DB : DB + 1, :] += total(dy)
 
     blocks(step, second_back)
-    RD.begin(order[-1])
-    ring_turn(RU, order[-1])
+    for offset in order[:-3]:
+        RD.end(offset)
     YO.start()
-    RD.along(order[-3])
     for offset in (*near, plan.half):
         O.wait_sent(offset)
         Q.wait_sent(offset)
@@ -833,17 +846,17 @@
         g = dot(otb[...], du[:, j * plan.out : (j + 1) * plan.out]).astype(BF).reshape(n_z, 2, 3, third, plan.out)
         for t in range(3):
             go[j, :, :, :, t * plan.group : t * plan.group + plan.out] = g[:, :, t]
-    for offset in range(n_mp):
+    for offset in order:
         RO.to_sibling(offset)
+    RD.begin(order[-1])
+    ring_turn(RU, order[-1])
+    for side in range(2):
+        RU.bound(side)
+    RD.along(order[-3])
+    for offset in order[1:] + order[:1]:
+        RO.begin(offset)
     do = hl
-
-    def out_back(at, rows):
-        do[rows, :] = dot_nt(du[rows, 0:D], wo[...]).astype(BF)
-
-    blocks(256, out_back)
-    RO.far()
-    RO.free(0)
-    RO.free(1)
+    do[...] = dot_nt(du[:, 0:D], wo[...]).astype(BF)
 
     @pl.loop(0, HEADS // 2)
     def _(t):
@@ -872,38 +885,6 @@
         qkv[:, cols(D)] = dk[...].astype(BF)
         qkv[:, cols(2 * D)] = dv[...].astype(BF)
 
-        @pl.when(t == 0)
-        def _():
-            for s in range(2):
-                RU.bound(s)
-            RD.end(order[-4])
-
-        @pl.when(t == 1)
-        def _():
-            RD.along(order[-2])
-
-        @pl.when(t == 2)
-        def _():
-            RU.nearer()
-            for s in range(2):
-                RO.bound(s)
-
-        @pl.when(t == 3)
-        def _():
-            RD.along(order[-1])
-            RD.end(order[-3])
-            RO.nearer()
-            if plan.half == 2:
-                RD.far()
-
-        @pl.when(t == 4)
-        def _():
-            RU.home()
-
-        @pl.when(t == 5)
-        def _():
-            RO.home()
-
     df3[...] = qkv[:, QKV : 3 * D].reshape(df3.shape)
     YF.start()
     for j in range(n_mp):
@@ -911,20 +892,11 @@
         gq[j, :, :, 0:R, 0 : plan.qkv] = g.reshape(n_z, 2, R, plan.qkv)
     for offset in (plan.half, *near):
         RQ.to_sibling(offset)
-    RQ.far()
-    RQ.free(0)
-    RQ.free(1)
-    RD.end(order[-2])
-    RD.end(order[-1])
-    if plan.half != 2:
-        RD.far()
-    RD.free(0)
-    RD.free(1)
-
-    def project_back(at, rows):
-        acc[rows, :] = dot_nt(qkv[rows, 0:QKV], wq[...])
-
-    blocks(256, project_back)
+    acc[...] = dot_nt(qkv[:, 0:QKV], wq[...])
+    RO.along(plan.half)
+    RD.along(order[-2])
+    for offset in near:
+        RO.along(offset)
 
     def first_back(at, rows):
         n1, inv = norm_stats(rows_of(x3, at, step)[...].astype(F32))
@@ -938,9 +910,9 @@
         sums[V_BIAS : V_BIAS + 1, 0:VFRESH] += total(qkv[rows, 2 * D : QKV].astype(F32))
 
     blocks(step, first_back)
-    YX.start()
-    for s in range(2):
-        RQ.bound(s)
+    RQ.far()
+    RQ.free(0)
+    RQ.free(1)
 
     def collect(g, e, owner):
         return dot_nt(jnp.where(owner == rowdev, g, 0.0).astype(BF), e)
@@ -960,29 +932,49 @@
             for r in range(plan.vec_rows):
                 value = jnp.where(at16 == r, sv[r, at : at + 1, :], value)
             gq[j, d // 2, d % 2, R:, :] = value.astype(BF)
-    for offset in range(n_mp):
+    for offset in order:
         RS.to_sibling(offset)
-    RQ.nearer()
     RS.far()
+    RS.free(1)
     RS.free(0)
-    RS.free(1)
-    RU.along()
-    RO.along()
-    for s in range(2):
-        RD.bound(s)
-    RD.nearer()
-    for s in range(2):
-        RS.bound(s)
-    RQ.home()
+    RD.along(order[-1])
+    RS.bound(1)
+    RU.nearer()
+    RU.home()
+    RS.bound(0)
+    RO.end(plan.half)
+    RO.far()
+    for offset in near:
+        RO.end(offset)
+    RO.free(1)
+    RO.free(0)
+    RQ.bound(1)
+    RO.bound(1)
+    RO.bound(0)
+    RD.end(order[-3])
     RS.nearer()
     RS.home()
+    RD.far()
+    RQ.bound(0)
+    RO.nearer()
+    o_o[...] = RO.finish()
+    RS.along()
+    o_s[...] = RS.finish()
+    RD.end(order[-2])
+    RD.free(1)
+    RD.bound(1)
+    RQ.nearer()
+    RQ.home()
+    YX.start()
+    RU.along()
+    RD.end(order[-1])
+    RD.free(0)
+    RD.bound(0)
+    RD.nearer()
+    RQ.along()
+    o_d[...] = RD.finish()
     o_u[...] = RU.finish()
-    o_o[...] = RO.finish()
-    RQ.along()
-    RS.along()
-    o_d[...] = RD.finish()
     o_q[...] = RQ.finish()
-    o_s[...] = RS.finish()
     for r in (RU, RD, RO, RQ, RS):
         r.wait_sent()
     for r in (YO, YF, YX):
@@ -1012,11 +1004,13 @@
             vm((n_z - 1, rows, cols), BF),
         ]
 
-    down_sums = [
-        vm((n_mp, n_z, R, C), BF),
-        vm((2, plan.half, R, C), BF),
-        vm((n_mp, n_z - 1, R, C), BF),
-    ]
+    def ring_last(rows, cols):
+        return [
+            vm((n_mp, n_z, rows, cols), BF),
+            vm((2, plan.half, rows, cols), BF),
+            vm((n_mp, n_z - 1, rows, cols), BF),
+        ]
+
     panel_z = [dma((n_mp, n_z - 1))] * 2
     gather_sems = [dma((n_z - 1,))] * 2 + [dma((2, plan.half))] * 2 + [dma((n_mp,))] * 2
     reduce_sems = [dma((n_mp,))] * 2 + [dma((2, plan.half + 1))] * 2 + [dma((n_z - 1,))] * 2
@@ -1041,7 +1035,7 @@
             panel(R + 16, plan.qw), panel(R // 3, C), panel(R, C), panel(R, C),
             vm(tok.shape, BF), vm(fv.shape, BF), vm(cot.shape, BF),
             vm(tok.shape, BF), vm(tok.shape, BF), vm(fv.shape, BF),
-            *sums(R, plan.qw), *sums(16, plan.qw), *sums(R // 3, C), *sums(R, C), *down_sums,
+            *sums(R, plan.qw), *sums(16, plan.qw), *ring_last(R // 3, C), *sums(R, C), *ring_last(R, C),
             vm((D, QKV), BF), vm((D, D), BF),
             vm((plan.vec_rows, n, plan.qw), F32), vm((16, D), F32), vm((max(8, n_mp), C), F32),
             wide(BF), tall(BF), vm((SEQ, 3 * D), BF), tall(F32), tall(BF),
@@ -1050,12 +1044,10 @@
             wide(F32), wide(F32), vm((SEQ, C), BF), wide(BF),
             vm((SEQ, 128), F32), vm((SEQ, 128), F32), vm((128, SEQ), F32),
             vm((16, D), F32), vm((max(8, n_mp), C), F32),
-            *gather_sems,
+            *(gather_sems * 4),
             *(panel_z + gather_sems[2:]),
-            *gather_sems,
-            *(panel_z + gather_sems[2:]),
-            *(reduce_sems * 4),
-            *(reduce_sems[:4] + panel_z),
+            *(reduce_sems * 3),
+            *((reduce_sems[:4] + panel_z) * 2),
             *([dma((MICRO,))] * 12),
         ],
         compiler_params=pltpu.CompilerParams(

time: 196 us -> 186 us (0.949)
  Pallas kernels: 194 us -> 183 us
    pallas_call x1, Pallas kernels: 190 us -> 179 us  [step(): pl.pallas_call(functools.partial(step_kernel, plan, len(ins)), name='step...]
where the time goes in v5:
time: 186 us; the launch traced here: 184 us
  Pallas kernels  183 us (98%)
    pallas_call x1, Pallas kernels, step(): pl.pallas_call(functools.partial(step_kernel, plan, len(ins)), name='step...  179 us
    pallas_call x1, Pallas kernels, unpack(): pl.pallas_call(functools.partial(unpack_kernel, plan, widths), name='unpa...  3.98 us

profile of v5, /device:TPU:1, one launch (start us, length us, event | category | flops | bytes accessed | tf_op | source)
XLA Modules:
  0.0 183.7 jit_solution(3506382283260382650)
XLA Ops:
  0.7 178.9 %step.1 = (bf16[4,128,768]{2,1,0:T(8,128)(2,1)}, bf16[4,128,768]{2,1,0:T(8,128)(2,1)}, bf16[4,128,384]{2,1,0:T(8,128)(2,1)}, f32[96,512]{1,0:T(8,128)}, f32[16,5...) custom-call(s32[8,768]{1,0:T(8,128)} %constant.4.clone.refs_0_, ...), custom_call_target="tpu_custom_call" | custom-call | tf_op jit(solution)/shard_map/step/pallas_call | solution.py:1019
  179.6 4.0 %unpack.1 = (bf16[4,128,768]{2,1,0:T(8,128)(2,1)}, bf16[4,128,768]{2,1,0:T(8,128)(2,1)}, bf16[4,128,384]{2,1,0:T(8,128)(2,1)}, f32[24]{0:T(128)}, f32[24]{0:T(12...) custom-call(bf16[4,128,768]{2,1,0:T(8,128)(2,1)} %get-tuple-element., ...), custom_call_target="tpu_custom_call" | custom-call | tf_op jit(solution)/shard_map/unpack/pallas_call | solution.py:1084

commit v6 on v5

--- a/solution.py
+++ b/solution.py
@@ -49,7 +49,7 @@
         self.half = self.n_mp // 2
         self.per_seq = SEQ // (SEQ // MICRO)
         self.n_seq = self.n_mp // MICRO
-        assert self.out <= self.group and self.rows % 48 == 0 and self.vec_rows <= 16
+        assert self.out <= self.group and self.rows % 48 == 0 and self.vec_rows <= 8
         self.bits = self.n_z.bit_length() - 1
         assert self.n_seq * MICRO == self.n_mp and self.n_z == 1 << self.bits and self.bits > 0
 
@@ -128,7 +128,7 @@
         partners += [(self.dp, (self.i + k) % plan.n_mp) for k in range(1, plan.n_mp)]
         for partner in partners:
             pl.semaphore_signal(barrier, inc=1, device_id=partner, device_id_type=MESH)
-        pl.semaphore_wait(barrier, len(partners))
+        return lambda: pl.semaphore_wait(barrier, len(partners))
 
     def push(self, src, dst, send, recv, device):
         return pltpu.make_async_remote_copy(
@@ -544,13 +544,14 @@
     (tab, dev, w_qkv, w_out, w_up, w_down, tok, fv, cot), small = refs[:9], refs[9:n_in]
     (o_out, o_dx, o_df, o_q, o_s, o_o, o_u, o_d) = refs[n_in : n_in + 8]
     (
-        gq, go, gu, gd, x3, f3, y3, out3, dx3, df3,
+        gq, go, gu, gd, x3, f3, y3, out3,
         q_other, q_ring, q_last, s_other, s_ring, s_last, o_other, o_ring, o_last, u_other, u_ring, u_last,
         d_other, d_ring, d_last,
-        wq, wo, sv, vec, ub, hl, hlt, qkv, ot, otb, lse, mid, n2, inv2, h2, h2t, yt,
-        big, acc, act, du, dv, dk, dqt, sums, ubg,
-    ) = refs[n_in + 8 : n_in + 8 + 51]
-    sems = refs[n_in + 8 + 51 :]
+        wq, wo, sv, vec, ub, hlt, qkv, otb, lse, mid, h2, h2t, yt,
+        big, acc, act, slope, du, dv, dk, dqt, sums, ubg,
+    ) = refs[n_in + 8 : n_in + 8 + 46]
+    sems = refs[n_in + 8 + 46 :]
+    dx3, df3 = y3, f3
     R, C, n_mp, n_dp, n_z = plan.rows, plan.cols, plan.n_mp, plan.n_dp, plan.n_z
     step = 64
     ex = Exchange(plan)
@@ -561,9 +562,9 @@
     U2 = Gather(ex, gu, sems[18:24], plan.row_half(1, R))
     W = RingFirst(ex, gd, sems[24:30])
     RQ = Reduce(ex, gq, slice(0, R), q_other, q_ring, q_last, sems[30:36])
-    RS = Reduce(ex, gq, slice(R, R + 16), s_other, s_ring, s_last, sems[36:42])
+    RS = Reduce(ex, gq, slice(R, R + 8), s_other, s_ring, s_last, sems[36:42])
     RU = Reduce(ex, gu, slice(0, R), u_other, u_ring, u_last, sems[42:48])
-    RO = RingLast(ex, go, slice(0, R // 3), o_other, o_ring, o_last, sems[48:54])
+    RO = Reduce(ex, go, slice(0, R // 3), o_other, o_ring, o_last, sems[48:54])
     RD = RingLast(ex, gd, slice(0, R), d_other, d_ring, d_last, sems[54:60])
     a2a = sems[60:72]
     XT = Rows(ex, tok, x3, a2a[0], a2a[1], False)
@@ -574,42 +575,42 @@
     YF = Rows(ex, df3, o_df, a2a[10], a2a[11], True)
     near = range(-plan.half + 1, plan.half)
 
+    all_here = ex.greet()
     third = R // 3
     gq[i, z, c, 0:R, 0 : plan.qkv] = w_qkv[...]
-    sv[0, 0:16, :] = jnp.zeros((16, plan.qw), F32)
+    sv[0, 0:8, :] = jnp.zeros((8, plan.qw), F32)
     for r in range(plan.vec_rows):
         pieces = [small[v][...] for v in range(r * plan.spr, min((r + 1) * plan.spr, N_VEC))]
         for k, piece in enumerate(pieces):
             sv[0, r : r + 1, k * 128 : k * 128 + piece.shape[0]] = piece.astype(F32)[None]
-    gq[i, z, c, R:, :] = sv[0, 0:16, :].astype(BF)
+    gq[i, z, c, R:, :] = sv[0, 0:8, :].astype(BF)
     for t in range(3):
         go[i, z, c, :, t * plan.group : t * plan.group + plan.out] = w_out[t * third : (t + 1) * third, :]
     gu[i, z, c] = w_up[...]
     gd[i, z, c] = w_down[...]
-    ex.greet()
+    all_here()
     Q.start()
     XT.start()
     Q.spread()
     Q.column()
+    U1.start()
+    U2.start()
+    W.begin(0)
+    Q.hop(1)
+    U1.spread()
+    XF.start()
+    U2.spread()
     O.start()
     W.circle()
-    W.begin(0)
-    U1.start()
-    U2.start()
+    W.spread(0)
+    O.spread()
+    U1.column()
+    U2.column()
+    O.column()
+    W.column(0)
     W.hop(1)
-    O.spread()
-    for d in range(2, plan.half + 1):
-        W.hop(d)
-    Q.hop(1)
-    XF.start()
-    U1.spread()
-    U2.spread()
-    O.column()
     for d in range(2, plan.half + 1):
         Q.hop(d)
-    XY.start()
-    for d in range(1, plan.half):
-        O.hop(d)
 
     rowdev = dev[:, 0:1]
     row = lambda v: vec[v : v + 1, :]
@@ -650,29 +651,26 @@
     for j in range(n_mp):
         ub[j : j + 1, :] = expand(UP_BIAS, e96, tab[5:6, :C] + j * n_dp)
 
-    W.spread(0)
-    U1.column()
-    U2.column()
     XT.wait_here()
     XT.wait_sent()
 
     def first_norm(at, rows):
         n1, _ = norm_stats(rows_of(x3, at, step)[...].astype(F32))
-        hl[rows, :] = (n1 * row(G1) + row(B1)).astype(BF)
+        rows_of(out3, at, step)[...] = (n1 * row(G1) + row(B1)).astype(BF)
 
     blocks(step, first_norm)
-    hlt[...] = hl[...].T
+    for d in range(2, plan.half + 1):
+        W.hop(d)
+    hl = out3[...].reshape(SEQ, D)
+    hlt[...] = hl.T
     XF.wait_here()
     XF.wait_sent()
 
-    q = dot(hl[...], wq[:, 0:D]) + row(QB)
+    q = dot(hl, wq[:, 0:D]) + row(QB)
     qkv[:, 0:D] = q.astype(BF) * 0.125
-    qkv[:, D : 2 * D] = dot(hl[...], wq[:, D : 2 * D]).astype(BF)
-    v = dot(hl[...], wq[:, 2 * D : QKV]) + row(V_BIAS)[:, :VFRESH]
+    qkv[:, D : 2 * D] = dot(hl, wq[:, D : 2 * D]).astype(BF)
+    v = dot(hl, wq[:, 2 * D : QKV]) + row(V_BIAS)[:, :VFRESH]
     qkv[:, 2 * D : QKV] = v.astype(BF)
-    for offset in near:
-        if offset:
-            W.spread(offset)
     qkv[:, QKV : 3 * D] = f3[...].reshape(SEQ, D // 2)
 
     B = 256
@@ -698,17 +696,31 @@
                 ex_ = jnp.exp(s - top)
                 total = jnp.sum(ex_, axis=0, keepdims=True)
                 o = dot(vt[e * HEAD : (e + 1) * HEAD, 0:kk], ex_.astype(BF)) / total
-                ot[pl.ds(pl.multiple_of(t * 128 + e * HEAD, HEAD), HEAD), span] = o
+                otb[pl.ds(pl.multiple_of(t * 128 + e * HEAD, HEAD), HEAD), span] = o.astype(BF)
                 lse[t, e : e + 1, span] = top + jnp.log(total)
 
         @pl.when(t == 0)
         def _():
+            for d in range(1, plan.half):
+                O.hop(d)
+
+        @pl.when(t == 1)
+        def _():
+            for d in range(1, plan.half):
+                U1.hop(d)
+                U2.hop(d)
+            for offset in near:
+                if offset:
+                    W.spread(offset)
+            XY.start()
+
+        @pl.when(t == 3)
+        def _():
             O.hop(plan.half)
+
+        @pl.when(t == 5)
+        def _():
             W.spread(plan.half)
-
-        @pl.when(t == 4)
-        def _():
-            W.column(0)
 
     for offset in (*near, plan.half):
         O.wait_sib(offset)
@@ -719,7 +731,6 @@
                 wo[rows, j * plan.out : (j + 1) * plan.out] = go[
                     j, d // 2, d % 2, :, t * plan.group : t * plan.group + plan.out
                 ]
-    otb[...] = ot[...].astype(BF)
     du[:, 0:D] = otb[...].T
 
     acc[...] = dot(du[:, 0:D], wo[...]) + row(OB)
@@ -727,84 +738,88 @@
     def second_norm(at, rows):
         m = rows_of(x3, at, step)[...].astype(F32) + acc[rows, :]
         mid[rows, :] = m
-        scaled, inv = norm_stats(m)
-        n2[rows, :] = scaled
-        inv2[rows, :] = jnp.broadcast_to(inv, (step, 128))
+        scaled, _ = norm_stats(m)
         h2[rows, :] = (scaled * row(G2) + row(B2)).astype(BF)
 
     blocks(step, second_norm)
-    W.column(plan.half)
     for offset in near:
         if offset:
             W.column(offset)
-    for d in range(1, plan.half):
-        U1.hop(d)
-        U2.hop(d)
     h2t[...] = h2[...].T
-    XY.wait_here()
-    XY.wait_sent()
-    yt[...] = y3[...].reshape(SEQ, D).T
     acc[...] = jnp.zeros_like(acc)
     big[...] = jnp.zeros_like(big)
 
-    order = [0, plan.half]
-    for d in range(plan.half - 1, 0, -1):
-        order += [-d, d]
-
-    def nth(q):
-        d = plan.half - q // 2
-        return jnp.where(q == 0, 0, jnp.where(q == 1, plan.half, d * (2 * (q % 2) - 1)))
-
-    def ring_turn(r, offset):
-        if offset == plan.half:
-            r.far()
-        elif abs(offset) == plan.half - 1:
-            r.free(0 if offset > 0 else 1)
+    offset_of = lambda q: (q + 1) // 2 * (1 - 2 * (q % 2))
 
     @pl.loop(0, n_mp)
     def _(q):
-        j = ex.at(ex.p + nth(q))
-        for s, offset in enumerate(order):
+        j = ex.at(ex.p + offset_of(q))
+        for s in range(n_mp):
+            offset = plan.half if s == n_mp - 1 else offset_of(s)
 
             @pl.when(q == s)
             def _():
-                if s == 1:
+                if s == n_mp - 2:
+                    W.column(plan.half)
                     U1.hop(plan.half)
                     U2.hop(plan.half)
-                    RD.begin(order[0])
                 U1.wait_sib(offset)
                 U2.wait_sib(offset)
                 W.wait_sib(offset)
 
-        up = gu[j].reshape(D, C)
-        down = gd[j].reshape(D, C)
-        u = dot(h2[...], up) + ub[pl.ds(j, 1), :]
+        u = dot(h2[...], gu[j].reshape(D, C)) + ub[pl.ds(j, 1), :]
         u2 = u * u
         tangent = jnp.tanh(GELU_C * (u + GELU_A * u2 * u))
         half = 0.5 * (1.0 + tangent)
         a = (u * half).astype(BF)
-        slope = half + 0.5 * u * (1.0 - tangent * tangent) * GELU_C * (1.0 + 3.0 * GELU_A * u2)
-        act[...] = a
-        acc[...] += dot_nt(a, down)
-        g = (dot(y3[...].reshape(SEQ, D), down) * slope).astype(BF)
+        act[j] = a
+        slope[j] = (
+            half + 0.5 * u * (1.0 - tangent * tangent) * GELU_C * (1.0 + 3.0 * GELU_A * u2)
+        ).astype(BF)
+        acc[...] += dot_nt(a, gd[j].reshape(D, C))
+
+    def finish_out(at, rows):
+        rows_of(out3, at, step)[...] = (mid[rows, :] + (acc[rows, :] + row(DB))).astype(BF)
+
+    blocks(step, finish_out)
+    YO.start()
+    XY.wait_here()
+    XY.wait_sent()
+    yt[...] = y3[...].reshape(SEQ, D).T
+
+    order = [plan.half]
+    for d in range(plan.half - 1, 0, -1):
+        order += [-d, d]
+    order += [0]
+
+    def nth(q):
+        d = plan.half - (q + 1) // 2
+        return jnp.where(q == 0, plan.half, jnp.where(q == n_mp - 1, 0, d * (1 - 2 * (q % 2))))
+
+    def leave(offset):
+        RD.begin(offset)
+        if offset == plan.half:
+            RU.far()
+        elif abs(offset) == plan.half - 1:
+            RU.free(0 if offset > 0 else 1)
+
+    @pl.loop(0, n_mp)
+    def _(q):
+        j = ex.at(ex.p + nth(q))
+        g = (dot(y3[...].reshape(SEQ, D), gd[j].reshape(D, C)) * slope[j].astype(F32)).astype(BF)
         du[:, 0:C] = g
-        big[...] += dot_nt(g, up)
+        big[...] += dot_nt(g, gu[j].reshape(D, C))
         for s, offset in enumerate(order):
 
             @pl.when(q == s)
             def _():
-                if s == 2:
-                    RD.along(order[0])
                 if s >= 3:
-                    RD.begin(order[s - 1])
-                    ring_turn(RU, order[s - 1])
-                if s >= 4:
-                    RD.along(order[s - 3])
+                    leave(order[s - 1])
                 W.wait_sent(offset)
                 U1.wait_sent(offset)
                 U2.wait_sent(offset)
 
-        gd[j] = dot(yt[...], act[...]).astype(BF).reshape(n_z, 2, R, C)
+        gd[j] = dot(yt[...], act[j]).astype(BF).reshape(n_z, 2, R, C)
         gu[j] = dot(h2t[...], du[:, 0:C]).astype(BF).reshape(n_z, 2, R, C)
         ubg[pl.ds(j, 1), :] = jnp.sum(du[:, 0:C].astype(F32), axis=0, keepdims=True)
         for s, offset in enumerate(order):
@@ -814,17 +829,16 @@
                 RD.to_sibling(offset)
                 RU.to_sibling(offset)
                 if s == 2:
-                    RD.begin(order[1])
-                    ring_turn(RU, order[1])
+                    leave(order[0])
+                    leave(order[1])
 
     sums[...] = jnp.zeros_like(sums)
 
     def second_back(at, rows):
-        rows_of(out3, at, step)[...] = (mid[rows, :] + (acc[rows, :] + row(DB))).astype(BF)
         dh = big[rows, :]
         dy = rows_of(y3, at, step)[...].astype(F32)
-        scaled = n2[rows, :]
-        dr = norm_back(dh, scaled, inv2[rows, 0:1], row(G2))
+        scaled, inv = norm_stats(mid[rows, :])
+        dr = norm_back(dh, scaled, inv, row(G2))
         dmid = dy + dr
         mid[rows, :] = dmid
         low = dmid.astype(BF)
@@ -836,9 +850,9 @@
         sums[DB : DB + 1, :] += total(dy)
 
     blocks(step, second_back)
-    for offset in order[:-3]:
+    for offset in order[:-4]:
+        RD.along(offset)
         RD.end(offset)
-    YO.start()
     for offset in (*near, plan.half):
         O.wait_sent(offset)
         Q.wait_sent(offset)
@@ -848,22 +862,21 @@
             go[j, :, :, :, t * plan.group : t * plan.group + plan.out] = g[:, :, t]
     for offset in order:
         RO.to_sibling(offset)
-    RD.begin(order[-1])
-    ring_turn(RU, order[-1])
-    for side in range(2):
-        RU.bound(side)
-    RD.along(order[-3])
-    for offset in order[1:] + order[:1]:
-        RO.begin(offset)
-    do = hl
+    do = h2
     do[...] = dot_nt(du[:, 0:D], wo[...]).astype(BF)
+    RD.begin(0)
+    RU.bound(0)
+    RO.far()
+    RO.free(0)
+    RO.free(1)
+    RU.bound(1)
 
     @pl.loop(0, HEADS // 2)
     def _(t):
         cols = lambda base: pl.ds(pl.multiple_of(base + t * 128, 128), 128)
         kt = qkv[:, cols(D)].T
         dot_ = do[:, cols(0)].astype(F32).T
-        prod = dot_ * ot[cols(0), :]
+        prod = dot_ * otb[cols(0), :].astype(F32)
         dv[...] = jnp.zeros_like(dv)
         dk[...] = jnp.zeros_like(dk)
         for e in range(2):
@@ -885,18 +898,22 @@
         qkv[:, cols(D)] = dk[...].astype(BF)
         qkv[:, cols(2 * D)] = dv[...].astype(BF)
 
+        @pl.when(t == 3)
+        def _():
+            RD.along(order[-4])
+
     df3[...] = qkv[:, QKV : 3 * D].reshape(df3.shape)
     YF.start()
+    RO.bound(1)
     for j in range(n_mp):
         g = dot(hlt[...], qkv[:, j * plan.qkv : (j + 1) * plan.qkv]).astype(BF)
         gq[j, :, :, 0:R, 0 : plan.qkv] = g.reshape(n_z, 2, R, plan.qkv)
-    for offset in (plan.half, *near):
+    for offset in order:
         RQ.to_sibling(offset)
+    RO.bound(0)
+    RD.along(order[-3])
     acc[...] = dot_nt(qkv[:, 0:QKV], wq[...])
-    RO.along(plan.half)
     RD.along(order[-2])
-    for offset in near:
-        RO.along(offset)
 
     def first_back(at, rows):
         n1, inv = norm_stats(rows_of(x3, at, step)[...].astype(F32))
@@ -924,52 +941,47 @@
     for j in range(1, n_mp):
         got = got + collect(ubg[j : j + 1, :], e96, tab[5:6, :C] + j * n_dp)
     sv[UP_BIAS // plan.spr, :, lanes(UP_BIAS)] = got
-    at16 = lax.broadcasted_iota(jnp.int32, (16, plan.qw), 0)
+    at8 = lax.broadcasted_iota(jnp.int32, (8, plan.qw), 0)
     for j in range(n_mp):
         for d in range(n_dp):
             at = j * n_dp + d
-            value = jnp.zeros((16, plan.qw), F32)
+            value = jnp.zeros((8, plan.qw), F32)
             for r in range(plan.vec_rows):
-                value = jnp.where(at16 == r, sv[r, at : at + 1, :], value)
+                value = jnp.where(at8 == r, sv[r, at : at + 1, :], value)
             gq[j, d // 2, d % 2, R:, :] = value.astype(BF)
     for offset in order:
         RS.to_sibling(offset)
+    RD.along(order[-1])
     RS.far()
+    RS.free(0)
     RS.free(1)
-    RS.free(0)
-    RD.along(order[-1])
-    RS.bound(1)
+    RO.nearer()
+    RO.home()
     RU.nearer()
     RU.home()
+    RS.bound(1)
     RS.bound(0)
-    RO.end(plan.half)
-    RO.far()
-    for offset in near:
-        RO.end(offset)
-    RO.free(1)
-    RO.free(0)
-    RQ.bound(1)
-    RO.bound(1)
-    RO.bound(0)
-    RD.end(order[-3])
     RS.nearer()
     RS.home()
+    RD.end(order[-4])
     RD.far()
+    RQ.bound(1)
+    RS.along()
     RQ.bound(0)
-    RO.nearer()
-    o_o[...] = RO.finish()
-    RS.along()
+    RO.along()
     o_s[...] = RS.finish()
-    RD.end(order[-2])
+    RD.end(order[-3])
     RD.free(1)
     RD.bound(1)
     RQ.nearer()
     RQ.home()
     YX.start()
+    RD.end(order[-2])
+    RD.free(0)
+    RD.bound(0)
+    o_o[...] = RO.finish()
     RU.along()
     RD.end(order[-1])
-    RD.free(0)
-    RD.bound(0)
     RD.nearer()
     RQ.along()
     o_d[...] = RD.finish()
@@ -1024,7 +1036,7 @@
             shape(tok.shape, BF),
             shape(fv.shape, BF),
             shape((R, plan.qw), F32),
-            shape((16, plan.qw), F32),
+            shape((8, plan.qw), F32),
             shape((R // 3, C), F32),
             shape((R, C), F32),
             shape((R, C), F32),
@@ -1032,22 +1044,22 @@
         in_specs=[IN_VMEM] * 6 + [ANY] * 3 + [IN_VMEM] * N_VEC,
         out_specs=(ANY,) * 3 + (IN_VMEM,) * 5,
         scratch_shapes=[
-            panel(R + 16, plan.qw), panel(R // 3, C), panel(R, C), panel(R, C),
+            panel(R + 8, plan.qw), panel(R // 3, C), panel(R, C), panel(R, C),
             vm(tok.shape, BF), vm(fv.shape, BF), vm(cot.shape, BF),
-            vm(tok.shape, BF), vm(tok.shape, BF), vm(fv.shape, BF),
-            *sums(R, plan.qw), *sums(16, plan.qw), *ring_last(R // 3, C), *sums(R, C), *ring_last(R, C),
+            vm(tok.shape, BF),
+            *sums(R, plan.qw), *sums(8, plan.qw), *sums(R // 3, C), *sums(R, C), *ring_last(R, C),
             vm((D, QKV), BF), vm((D, D), BF),
             vm((plan.vec_rows, n, plan.qw), F32), vm((16, D), F32), vm((max(8, n_mp), C), F32),
-            wide(BF), tall(BF), vm((SEQ, 3 * D), BF), tall(F32), tall(BF),
+            tall(BF), vm((SEQ, 3 * D), BF), tall(BF),
             vm((HEADS // 2, 8, SEQ), F32),
-            wide(F32), wide(F32), vm((SEQ, 128), F32), wide(BF), tall(BF), tall(BF),
-            wide(F32), wide(F32), vm((SEQ, C), BF), wide(BF),
+            wide(F32), wide(BF), tall(BF), tall(BF),
+            wide(F32), wide(F32), vm((n_mp, SEQ, C), BF), vm((n_mp, SEQ, C), BF), wide(BF),
             vm((SEQ, 128), F32), vm((SEQ, 128), F32), vm((128, SEQ), F32),
             vm((16, D), F32), vm((max(8, n_mp), C), F32),
             *(gather_sems * 4),
             *(panel_z + gather_sems[2:]),
-            *(reduce_sems * 3),
-            *((reduce_sems[:4] + panel_z) * 2),
+            *(reduce_sems * 4),
+            *(reduce_sems[:4] + panel_z),
             *([dma((MICRO,))] * 12),
         ],
         compiler_params=pltpu.CompilerParams(

time: 186 us -> 170 us (0.914)
  Pallas kernels: 183 us -> 167 us
    pallas_call x1, Pallas kernels: 179 us -> 163 us  [step(): pl.pallas_call(functools.partial(step_kernel, plan, len(ins)), name='step...]
where the time goes in v6:
time: 170 us; the launch traced here: 168 us
  Pallas kernels  167 us (98%)
    pallas_call x1, Pallas kernels, step(): pl.pallas_call(functools.partial(step_kernel, plan, len(ins)), name='step...  163 us
    pallas_call x1, Pallas kernels, unpack(): pl.pallas_call(functools.partial(unpack_kernel, plan, widths), name='unpa...  3.99 us

profile of v6, /device:TPU:1, one launch (start us, length us, event | category | flops | bytes accessed | tf_op | source)
XLA Modules:
  0.0 167.6 jit_solution(12155761678371748669)
XLA Ops:
  0.7 162.8 %step.1 = (bf16[4,128,768]{2,1,0:T(8,128)(2,1)}, bf16[4,128,768]{2,1,0:T(8,128)(2,1)}, bf16[4,128,384]{2,1,0:T(8,128)(2,1)}, f32[96,512]{1,0:T(8,128)}, f32[8,51...) custom-call(s32[8,768]{1,0:T(8,128)} %constant.4.clone.refs_0_, ...), custom_call_target="tpu_custom_call" | custom-call | tf_op jit(solution)/shard_map/step/pallas_call | solution.py:1031
  163.5 4.0 %unpack.1 = (bf16[4,128,768]{2,1,0:T(8,128)(2,1)}, bf16[4,128,768]{2,1,0:T(8,128)(2,1)}, bf16[4,128,384]{2,1,0:T(8,128)(2,1)}, f32[24]{0:T(128)}, f32[24]{0:T(12...) custom-call(bf16[4,128,768]{2,1,0:T(8,128)(2,1)} %get-tuple-element., ...), custom_call_target="tpu_custom_call" | custom-call | tf_op jit(solution)/shard_map/unpack/pallas_call | solution.py:1096

commit v7 on v6

--- a/solution.py
+++ b/solution.py
@@ -43,13 +43,13 @@
         self.qkv = QKV // self.n_mp
         self.out = D // self.n_mp
         self.qw = -(-self.qkv // 128) * 128
-        self.group = self.cols // 3
+        self.parts = self.cols // self.out
         self.spr = self.qw // 128
         self.vec_rows = -(-N_VEC // self.spr)
         self.half = self.n_mp // 2
         self.per_seq = SEQ // (SEQ // MICRO)
         self.n_seq = self.n_mp // MICRO
-        assert self.out <= self.group and self.rows % 48 == 0 and self.vec_rows <= 8
+        assert self.parts * self.out == self.cols and self.rows % (8 * self.parts) == 0 and self.vec_rows <= 8
         self.bits = self.n_z.bit_length() - 1
         assert self.n_seq * MICRO == self.n_mp and self.n_z == 1 << self.bits and self.bits > 0
 
@@ -554,6 +554,7 @@
     dx3, df3 = y3, f3
     R, C, n_mp, n_dp, n_z = plan.rows, plan.cols, plan.n_mp, plan.n_dp, plan.n_z
     step = 64
+    part = R // plan.parts
     ex = Exchange(plan)
     i, z, c = ex.i, ex.z, ex.c
     Q = Gather(ex, gq, sems[0:6])
@@ -564,7 +565,7 @@
     RQ = Reduce(ex, gq, slice(0, R), q_other, q_ring, q_last, sems[30:36])
     RS = Reduce(ex, gq, slice(R, R + 8), s_other, s_ring, s_last, sems[36:42])
     RU = Reduce(ex, gu, slice(0, R), u_other, u_ring, u_last, sems[42:48])
-    RO = Reduce(ex, go, slice(0, R // 3), o_other, o_ring, o_last, sems[48:54])
+    RO = Reduce(ex, go, slice(0, part), o_other, o_ring, o_last, sems[48:54])
     RD = RingLast(ex, gd, slice(0, R), d_other, d_ring, d_last, sems[54:60])
     a2a = sems[60:72]
     XT = Rows(ex, tok, x3, a2a[0], a2a[1], False)
@@ -576,7 +577,6 @@
     near = range(-plan.half + 1, plan.half)
 
     all_here = ex.greet()
-    third = R // 3
     gq[i, z, c, 0:R, 0 : plan.qkv] = w_qkv[...]
     sv[0, 0:8, :] = jnp.zeros((8, plan.qw), F32)
     for r in range(plan.vec_rows):
@@ -584,18 +584,34 @@
         for k, piece in enumerate(pieces):
             sv[0, r : r + 1, k * 128 : k * 128 + piece.shape[0]] = piece.astype(F32)[None]
     gq[i, z, c, R:, :] = sv[0, 0:8, :].astype(BF)
-    for t in range(3):
-        go[i, z, c, :, t * plan.group : t * plan.group + plan.out] = w_out[t * third : (t + 1) * third, :]
-    gu[i, z, c] = w_up[...]
-    gd[i, z, c] = w_down[...]
+    def rows_of(ref3, at, step):
+        part = SEQ // MICRO
+        return ref3.at[at // (part // step), pl.ds(pl.multiple_of((at % (part // step)) * step, step), step)]
+
+    def blocks(step, body):
+        @pl.loop(0, SEQ // step)
+        def _(at):
+            body(at, pl.ds(pl.multiple_of(at * step, step), step))
+
     all_here()
     Q.start()
     XT.start()
+    for t in range(plan.parts):
+        go[i, z, c, :, t * plan.out : (t + 1) * plan.out] = w_out[t * part : (t + 1) * part, :]
+    gu[i, z, c] = w_up[...]
+    gd[i, z, c] = w_down[...]
     Q.spread()
     Q.column()
     U1.start()
     U2.start()
     W.begin(0)
+    XT.wait_here()
+    XT.wait_sent()
+
+    def first_stats(at, rows):
+        acc[rows, :], _ = norm_stats(rows_of(x3, at, step)[...].astype(F32))
+
+    blocks(step, first_stats)
     Q.hop(1)
     U1.spread()
     XF.start()
@@ -619,15 +635,6 @@
     e24 = onehot(0, D)
     e96 = onehot(4, C)
 
-    def rows_of(ref3, at, step):
-        part = SEQ // MICRO
-        return ref3.at[at // (part // step), pl.ds(pl.multiple_of((at % (part // step)) * step, step), step)]
-
-    def blocks(step, body):
-        @pl.loop(0, SEQ // step)
-        def _(at):
-            body(at, pl.ds(pl.multiple_of(at * step, step), step))
-
     for offset in (*near, plan.half):
         Q.wait_sib(offset)
 
@@ -651,12 +658,8 @@
     for j in range(n_mp):
         ub[j : j + 1, :] = expand(UP_BIAS, e96, tab[5:6, :C] + j * n_dp)
 
-    XT.wait_here()
-    XT.wait_sent()
-
     def first_norm(at, rows):
-        n1, _ = norm_stats(rows_of(x3, at, step)[...].astype(F32))
-        rows_of(out3, at, step)[...] = (n1 * row(G1) + row(B1)).astype(BF)
+        rows_of(out3, at, step)[...] = (acc[rows, :] * row(G1) + row(B1)).astype(BF)
 
     blocks(step, first_norm)
     for d in range(2, plan.half + 1):
@@ -726,10 +729,10 @@
         O.wait_sib(offset)
     for j in range(n_mp):
         for d in range(n_dp):
-            for t in range(3):
-                rows = slice(d * R + t * third, d * R + (t + 1) * third)
+            for t in range(plan.parts):
+                rows = slice(d * R + t * part, d * R + (t + 1) * part)
                 wo[rows, j * plan.out : (j + 1) * plan.out] = go[
-                    j, d // 2, d % 2, :, t * plan.group : t * plan.group + plan.out
+                    j, d // 2, d % 2, :, t * plan.out : (t + 1) * plan.out
                 ]
     du[:, 0:D] = otb[...].T
 
@@ -796,8 +799,7 @@
         d = plan.half - (q + 1) // 2
         return jnp.where(q == 0, plan.half, jnp.where(q == n_mp - 1, 0, d * (1 - 2 * (q % 2))))
 
-    def leave(offset):
-        RD.begin(offset)
+    def up_leaves(offset):
         if offset == plan.half:
             RU.far()
         elif abs(offset) == plan.half - 1:
@@ -813,25 +815,30 @@
 
             @pl.when(q == s)
             def _():
-                if s >= 3:
-                    leave(order[s - 1])
+                if s >= 1:
+                    up_leaves(order[s - 1])
+                if s >= 2:
+                    RD.begin(order[s - 2])
                 W.wait_sent(offset)
                 U1.wait_sent(offset)
                 U2.wait_sent(offset)
 
+        gu[j] = dot(h2t[...], du[:, 0:C]).astype(BF).reshape(n_z, 2, R, C)
+        for s, offset in enumerate(order):
+
+            @pl.when(q == s)
+            def _():
+                RU.to_sibling(offset)
+
         gd[j] = dot(yt[...], act[j]).astype(BF).reshape(n_z, 2, R, C)
-        gu[j] = dot(h2t[...], du[:, 0:C]).astype(BF).reshape(n_z, 2, R, C)
         ubg[pl.ds(j, 1), :] = jnp.sum(du[:, 0:C].astype(F32), axis=0, keepdims=True)
         for s, offset in enumerate(order):
 
             @pl.when(q == s)
             def _():
                 RD.to_sibling(offset)
-                RU.to_sibling(offset)
-                if s == 2:
-                    leave(order[0])
-                    leave(order[1])
-
+
+    RD.begin(order[-2])
     sums[...] = jnp.zeros_like(sums)
 
     def second_back(at, rows):
@@ -857,9 +864,9 @@
         O.wait_sent(offset)
         Q.wait_sent(offset)
     for j in range(n_mp):
-        g = dot(otb[...], du[:, j * plan.out : (j + 1) * plan.out]).astype(BF).reshape(n_z, 2, 3, third, plan.out)
-        for t in range(3):
-            go[j, :, :, :, t * plan.group : t * plan.group + plan.out] = g[:, :, t]
+        g = dot(otb[...], du[:, j * plan.out : (j + 1) * plan.out]).reshape(n_z, 2, plan.parts, part, plan.out)
+        for t in range(plan.parts):
+            go[j, :, :, :, t * plan.out : (t + 1) * plan.out] = g[:, :, t].astype(BF)
     for offset in order:
         RO.to_sibling(offset)
     do = h2
@@ -1037,17 +1044,17 @@
             shape(fv.shape, BF),
             shape((R, plan.qw), F32),
             shape((8, plan.qw), F32),
-            shape((R // 3, C), F32),
+            shape((R // plan.parts, C), F32),
             shape((R, C), F32),
             shape((R, C), F32),
         ),
         in_specs=[IN_VMEM] * 6 + [ANY] * 3 + [IN_VMEM] * N_VEC,
         out_specs=(ANY,) * 3 + (IN_VMEM,) * 5,
         scratch_shapes=[
-            panel(R + 8, plan.qw), panel(R // 3, C), panel(R, C), panel(R, C),
+            panel(R + 8, plan.qw), panel(R // plan.parts, C), panel(R, C), panel(R, C),
             vm(tok.shape, BF), vm(fv.shape, BF), vm(cot.shape, BF),
             vm(tok.shape, BF),
-            *sums(R, plan.qw), *sums(8, plan.qw), *sums(R // 3, C), *sums(R, C), *ring_last(R, C),
+            *sums(R, plan.qw), *sums(8, plan.qw), *sums(R // plan.parts, C), *sums(R, C), *ring_last(R, C),
             vm((D, QKV), BF), vm((D, D), BF),
             vm((plan.vec_rows, n, plan.qw), F32), vm((16, D), F32), vm((max(8, n_mp), C), F32),
             tall(BF), vm((SEQ, 3 * D), BF), tall(BF),
@@ -1074,9 +1081,9 @@
     for move in moves:
         move.start()
     outs[5][...] = t_q[:, 0 : plan.qkv]
-    third = plan.rows // 3
-    for t in range(3):
-        outs[8][t * third : (t + 1) * third, :] = t_o[:, t * plan.group : t * plan.group + plan.out]
+    part = plan.rows // plan.parts
+    for t in range(plan.parts):
+        outs[8][t * part : (t + 1) * part, :] = t_o[:, t * plan.out : (t + 1) * plan.out]
     outs[12][...] = t_u[...]
     outs[14][...] = t_d[...]
     for v, at in enumerate((3, 4, 6, 7, 9, 10, 11, 13, 15)):
@@ -1108,19 +1115,486 @@
     ln2_gain, ln2_bias, w_up, up_bias, w_down, down_bias,
 ):
     small = (ln1_gain, ln1_bias, q_bias, v_bias, out_bias, ln2_gain, ln2_bias, up_bias, down_bias)
+    assert tokens.shape[1] * plan.n_mp == SEQ
     summed = step(plan, w_qkv, w_out, w_up, w_down.T, tokens, first_values, out_cot, small)
     outs = unpack(plan, summed, [s.shape[0] for s in small])
     return (*outs[:14], outs[14].T, outs[15])
 
 
+def layer_norm(inputs, gain_vec, shift_vec):
+    average = jnp.mean(inputs, axis=-1, keepdims=True)
+    centred = inputs - average
+    variance = jnp.mean(centred * centred, axis=-1, keepdims=True)
+    inv_std = lax.rsqrt(variance + EPS)
+    scaled = centred * inv_std
+    return (scaled * gain_vec + shift_vec, scaled, inv_std)
+
+
+def norm_back_all(grad_out, scaled, inv_std, gain_vec):
+    grad_scaled = grad_out * gain_vec
+    first_term = jnp.mean(grad_scaled, axis=-1, keepdims=True)
+    second_term = jnp.mean(grad_scaled * scaled, axis=-1, keepdims=True)
+    grad_in = inv_std * (grad_scaled - first_term - scaled * second_term)
+    return (grad_in, jnp.sum(grad_out * scaled, axis=0), jnp.sum(grad_out, axis=0))
+
+
+def gelu_both(inputs):
+    cubic_term = inputs + GELU_A * inputs * inputs * inputs
+    tangent = jnp.tanh(GELU_C * cubic_term)
+    gelu_out = 0.5 * inputs * (1.0 + tangent)
+    gelu_slope = 0.5 * (1.0 + tangent) + 0.5 * inputs * (1.0 - tangent * tangent) * GELU_C * (
+        1.0 + 3.0 * GELU_A * inputs * inputs
+    )
+    return (gelu_out, gelu_slope)
+
+
+def split_heads(matrix):
+    return matrix.reshape(matrix.shape[0], HEADS, HEAD)
+
+
+def block_scores(query_heads, key_block, row_first, key_first):
+    key_heads = split_heads(key_block)
+    scores = jnp.einsum(
+        "qhd,khd->hqk", query_heads, key_heads, preferred_element_type=jnp.float32
+    ) * HEAD ** (-0.5)
+    query_pos = row_first + jnp.arange(query_heads.shape[0], dtype=jnp.int32)
+    key_pos = key_first + jnp.arange(key_block.shape[0], dtype=jnp.int32)
+    allowed = key_pos[None, :] <= query_pos[:, None]
+    return (jnp.where(allowed[None], scores, -BIG), allowed, key_heads)
+
+
+def block_length():
+    return 512
+
+
+def fold_blocks(function, carried, key_block, value_block, key_first):
+    row_count = key_block.shape[0]
+    block_rows = block_length()
+    if block_rows == row_count:
+        return function(carried, key_block, value_block, key_first)
+    key_parts = key_block.reshape(row_count // block_rows, block_rows, key_block.shape[1])
+    value_parts = value_block.reshape(row_count // block_rows, block_rows, value_block.shape[1])
+    offsets = key_first + jnp.arange(row_count // block_rows, dtype=jnp.int32) * block_rows
+
+    def step_once(inner_state, element):
+        return (function(inner_state, element[0], element[1], element[2]), None)
+
+    result, ignored = lax.scan(step_once, carried, (key_parts, value_parts, offsets))
+    return result
+
+
+def map_blocks(function, key_block, value_block, key_first):
+    row_count = key_block.shape[0]
+    block_rows = block_length()
+    if block_rows == row_count:
+        return function(key_block, value_block, key_first)
+    key_parts = key_block.reshape(row_count // block_rows, block_rows, key_block.shape[1])
+    value_parts = value_block.reshape(row_count // block_rows, block_rows, value_block.shape[1])
+    offsets = key_first + jnp.arange(row_count // block_rows, dtype=jnp.int32) * block_rows
+
+    def apply_once(element):
+        return function(element[0], element[1], element[2])
+
+    outputs = lax.map(apply_once, (key_parts, value_parts, offsets))
+    return outputs.reshape(row_count, outputs.shape[-1])
+
+
+def attention_forward(queries, keys_low, values_low, row_first):
+    query_heads = split_heads(queries)
+    row_total = queries.shape[0]
+
+    def online_step(fold_state, key_block, value_block, key_first):
+        running_top, running_sum, running_acc = fold_state
+        masked, allowed, ignored = block_scores(query_heads, key_block, row_first, key_first)
+        new_top = jnp.maximum(running_top, jnp.max(masked, axis=-1))
+        weights = jnp.exp(masked - new_top[:, :, None]) * allowed[None]
+        shrink = jnp.exp(running_top - new_top)
+        running_sum = running_sum * shrink + jnp.sum(weights, axis=-1)
+        running_acc = running_acc * shrink[:, :, None] + jnp.einsum(
+            "hqk,khd->hqd",
+            weights.astype(jnp.bfloat16),
+            split_heads(value_block),
+            preferred_element_type=jnp.float32,
+        )
+        return (new_top, running_sum, running_acc)
+
+    start_state = (
+        jnp.full((HEADS, row_total), -BIG, jnp.float32),
+        jnp.zeros((HEADS, row_total), jnp.float32),
+        jnp.zeros((HEADS, row_total, HEAD), jnp.float32),
+    )
+    running_top, running_sum, running_acc = fold_blocks(
+        online_step,
+        start_state,
+        lax.all_gather(keys_low, "mp", axis=0, tiled=True),
+        lax.all_gather(values_low, "mp", axis=0, tiled=True),
+        jnp.int32(0),
+    )
+    attended = (running_acc / running_sum[:, :, None]).transpose(1, 0, 2).reshape(row_total, D)
+    return (attended, running_top + jnp.log(running_sum))
+
+
+def attention_backward(queries, keys_low, values_low, grad_out, attended, log_total, row_first):
+    query_heads = split_heads(queries)
+    grad_heads = split_heads(grad_out)
+    row_total = queries.shape[0]
+    score_scale = HEAD ** (-0.5)
+    row_delta = jnp.sum(grad_heads.astype(jnp.float32) * split_heads(attended), axis=-1).T
+    keys_all, values_all = (
+        lax.all_gather(keys_low, "mp", axis=0, tiled=True),
+        lax.all_gather(values_low, "mp", axis=0, tiled=True),
+    )
+
+    def soft_grads(key_block, value_block, key_first):
+        masked, allowed, key_heads = block_scores(query_heads, key_block, row_first, key_first)
+        probabilities = jnp.exp(masked - log_total[:, :, None])
+        grad_probs = jnp.einsum(
+            "qhd,khd->hqk", grad_heads, split_heads(value_block), preferred_element_type=jnp.float32
+        )
+        grad_scores = (probabilities * (grad_probs - row_delta[:, :, None])).astype(jnp.bfloat16)
+        return (probabilities, grad_scores, key_heads)
+
+    def query_step(accum, key_block, value_block, key_first):
+        probabilities, grad_scores, key_heads = soft_grads(key_block, value_block, key_first)
+        return (
+            accum
+            + jnp.einsum("hqk,khd->qhd", grad_scores, key_heads, preferred_element_type=jnp.float32)
+            * score_scale
+        )
+
+    grad_query = fold_blocks(
+        query_step, jnp.zeros((row_total, HEADS, HEAD), jnp.float32), keys_all, values_all, 0
+    )
+
+    def key_step(key_block, value_block, key_first):
+        probabilities, grad_scores, key_heads = soft_grads(key_block, value_block, key_first)
+        grad_value = jnp.einsum(
+            "hqk,qhd->khd",
+            probabilities.astype(jnp.bfloat16),
+            grad_heads,
+            preferred_element_type=jnp.float32,
+        )
+        grad_key = (
+            jnp.einsum("hqk,qhd->khd", grad_scores, query_heads, preferred_element_type=jnp.float32)
+            * score_scale
+        )
+        return jnp.concatenate(
+            [grad_key.reshape(key_block.shape[0], D), grad_value.reshape(key_block.shape[0], D)],
+            axis=1,
+        )
+
+    key_block = keys_all
+    value_block = values_all
+    grad_kv = lax.psum_scatter(
+        map_blocks(key_step, key_block, value_block, jnp.int32(0)).astype(jnp.bfloat16),
+        "mp",
+        scatter_dimension=0,
+        tiled=True,
+    ).astype(jnp.float32)
+    return (grad_query.reshape(row_total, D), grad_kv)
+
+
+def reduce_grads(local_grads):
+    row_parts = (
+        lax.psum_scatter(
+            local_grads[0].astype(jnp.bfloat16), "dp", scatter_dimension=0, tiled=True
+        ).astype(jnp.float32),
+        lax.psum_scatter(
+            local_grads[1].astype(jnp.bfloat16), "dp", scatter_dimension=0, tiled=True
+        ).astype(jnp.float32),
+        lax.psum_scatter(
+            local_grads[2].astype(jnp.bfloat16), "dp", scatter_dimension=0, tiled=True
+        ).astype(jnp.float32),
+        lax.psum_scatter(
+            local_grads[3].astype(jnp.bfloat16), "dp", scatter_dimension=0, tiled=True
+        ).astype(jnp.float32),
+        lax.psum_scatter(
+            local_grads[4].astype(jnp.bfloat16), "dp", scatter_dimension=0, tiled=True
+        ).astype(jnp.float32),
+        lax.psum_scatter(
+            local_grads[5].astype(jnp.bfloat16), "dp", scatter_dimension=0, tiled=True
+        ).astype(jnp.float32),
+        lax.psum_scatter(
+            local_grads[6].astype(jnp.bfloat16), "dp", scatter_dimension=0, tiled=True
+        ).astype(jnp.float32),
+        lax.psum_scatter(
+            local_grads[7].astype(jnp.bfloat16), "dp", scatter_dimension=0, tiled=True
+        ).astype(jnp.float32),
+        lax.psum_scatter(
+            local_grads[8].astype(jnp.bfloat16), "dp", scatter_dimension=0, tiled=True
+        ).astype(jnp.float32),
+        lax.psum_scatter(
+            local_grads[9].astype(jnp.bfloat16), "dp", scatter_dimension=0, tiled=True
+        ).astype(jnp.float32),
+        lax.psum_scatter(
+            local_grads[10].astype(jnp.bfloat16), "dp", scatter_dimension=0, tiled=True
+        ).astype(jnp.float32),
+        lax.psum_scatter(
+            local_grads[11].astype(jnp.bfloat16), "dp", scatter_dimension=1, tiled=True
+        ).astype(jnp.float32),
+        lax.psum_scatter(
+            local_grads[12].astype(jnp.bfloat16), "dp", scatter_dimension=0, tiled=True
+        ).astype(jnp.float32),
+    )
+    row_parts = tuple(row_parts)
+    col_parts = tuple(
+        (
+            lax.psum_scatter(
+                row_parts[0].astype(jnp.bfloat16), "mp", scatter_dimension=0, tiled=True
+            ).astype(jnp.float32),
+            lax.psum_scatter(
+                row_parts[1].astype(jnp.bfloat16), "mp", scatter_dimension=0, tiled=True
+            ).astype(jnp.float32),
+            lax.psum_scatter(
+                row_parts[2].astype(jnp.bfloat16), "mp", scatter_dimension=1, tiled=True
+            ).astype(jnp.float32),
+            lax.psum_scatter(
+                row_parts[3].astype(jnp.bfloat16), "mp", scatter_dimension=0, tiled=True
+            ).astype(jnp.float32),
+            lax.psum_scatter(
+                row_parts[4].astype(jnp.bfloat16), "mp", scatter_dimension=0, tiled=True
+            ).astype(jnp.float32),
+            lax.psum_scatter(
+                row_parts[5].astype(jnp.bfloat16), "mp", scatter_dimension=1, tiled=True
+            ).astype(jnp.float32),
+            lax.psum_scatter(
+                row_parts[6].astype(jnp.bfloat16), "mp", scatter_dimension=0, tiled=True
+            ).astype(jnp.float32),
+            lax.psum_scatter(
+                row_parts[7].astype(jnp.bfloat16), "mp", scatter_dimension=0, tiled=True
+            ).astype(jnp.float32),
+            lax.psum_scatter(
+                row_parts[8].astype(jnp.bfloat16), "mp", scatter_dimension=0, tiled=True
+            ).astype(jnp.float32),
+            lax.psum_scatter(
+                row_parts[10].astype(jnp.bfloat16), "mp", scatter_dimension=0, tiled=True
+            ).astype(jnp.float32),
+            lax.psum_scatter(
+                row_parts[12].astype(jnp.bfloat16), "mp", scatter_dimension=0, tiled=True
+            ).astype(jnp.float32),
+        )
+    )
+    return col_parts[:9] + (row_parts[9], col_parts[9], row_parts[11], col_parts[10])
+
+
+def general_shards(
+    tokens,
+    first_values,
+    out_cot,
+    ln1_gain,
+    ln1_bias,
+    w_qkv,
+    q_bias,
+    v_bias,
+    w_out,
+    out_bias,
+    ln2_gain,
+    ln2_bias,
+    w_up,
+    up_bias,
+    w_down,
+    down_bias,
+):
+    near_blocks = tuple(
+        (
+            lax.all_gather(ln1_gain, "mp", axis=0, tiled=True),
+            lax.all_gather(ln1_bias, "mp", axis=0, tiled=True),
+            lax.all_gather(w_qkv, "mp", axis=1, tiled=True),
+            lax.all_gather(q_bias, "mp", axis=0, tiled=True),
+            lax.all_gather(v_bias, "mp", axis=0, tiled=True),
+            lax.all_gather(w_out, "mp", axis=1, tiled=True),
+            lax.all_gather(out_bias, "mp", axis=0, tiled=True),
+            lax.all_gather(ln2_gain, "mp", axis=0, tiled=True),
+            lax.all_gather(ln2_bias, "mp", axis=0, tiled=True),
+            lax.all_gather(up_bias, "mp", axis=0, tiled=True),
+            lax.all_gather(down_bias, "mp", axis=0, tiled=True),
+        )
+    )
+    near_blocks = near_blocks[:9] + (w_up, near_blocks[9], w_down, near_blocks[10])
+    params = tuple(
+        (
+            lax.all_gather(near_blocks[0], "dp", axis=0, tiled=True),
+            lax.all_gather(near_blocks[1], "dp", axis=0, tiled=True),
+            lax.all_gather(near_blocks[2], "dp", axis=0, tiled=True),
+            lax.all_gather(near_blocks[3], "dp", axis=0, tiled=True),
+            lax.all_gather(near_blocks[4], "dp", axis=0, tiled=True),
+            lax.all_gather(near_blocks[5], "dp", axis=0, tiled=True),
+            lax.all_gather(near_blocks[6], "dp", axis=0, tiled=True),
+            lax.all_gather(near_blocks[7], "dp", axis=0, tiled=True),
+            lax.all_gather(near_blocks[8], "dp", axis=0, tiled=True),
+            lax.all_gather(near_blocks[9], "dp", axis=0, tiled=True),
+            lax.all_gather(near_blocks[10], "dp", axis=0, tiled=True),
+            lax.all_gather(near_blocks[11], "dp", axis=1, tiled=True),
+            lax.all_gather(near_blocks[12], "dp", axis=0, tiled=True),
+        )
+    )
+    gain_one = params[0].astype(jnp.float32)
+    shift_one = params[1].astype(jnp.float32)
+    qkv_full = params[2]
+    query_shift = params[3].astype(jnp.float32)
+    value_shift = params[4].astype(jnp.float32)
+    out_full = params[5]
+    out_shift = params[6].astype(jnp.float32)
+    gain_two = params[7].astype(jnp.float32)
+    shift_two = params[8].astype(jnp.float32)
+    up_full = params[9]
+    up_shift_all = params[10].astype(jnp.float32)
+    down_full = params[11]
+    down_shift = params[12].astype(jnp.float32)
+    up_cols = up_full.shape[1]
+    up_start = 0
+    up_start = lax.axis_index("mp") * up_cols
+    up_used = lax.dynamic_slice_in_dim(up_shift_all, up_start, up_cols, 0)
+    row_total = tokens.shape[1]
+    row_first = lax.axis_index("mp") * row_total
+    fresh_cols = value_shift.shape[0]
+    outputs = []
+    grad_inputs = []
+    grad_firsts = []
+    summed = None
+    for micro_index in range(MICRO):
+        cot_low = out_cot[micro_index]
+        inputs = tokens[micro_index].astype(jnp.float32)
+        normed, scaled_one, inv_one = layer_norm(inputs, gain_one, shift_one)
+        normed_low = normed.astype(jnp.bfloat16)
+        mixed_proj = jnp.dot(normed_low, qkv_full, preferred_element_type=jnp.float32)
+        queries = (mixed_proj[:, :D] + query_shift).astype(jnp.bfloat16)
+        keys_low = mixed_proj[:, D : 2 * D].astype(jnp.bfloat16)
+        values_low = jnp.concatenate(
+            [
+                (mixed_proj[:, 2 * D :] + value_shift).astype(jnp.bfloat16),
+                first_values[micro_index],
+            ],
+            axis=1,
+        )
+        attended, log_total = attention_forward(queries, keys_low, values_low, row_first)
+        attended_low = attended.astype(jnp.bfloat16)
+        middle = inputs + (
+            jnp.dot(attended_low, out_full, preferred_element_type=jnp.float32) + out_shift
+        )
+        normed_two, scaled_two, inv_two = layer_norm(middle, gain_two, shift_two)
+        normed_two_low = normed_two.astype(jnp.bfloat16)
+        cot_float = cot_low.astype(jnp.float32)
+        row_piece = lax.all_gather(normed_two_low, "mp", axis=0, tiled=True)
+        hidden = jnp.dot(row_piece, up_full, preferred_element_type=jnp.float32) + up_used
+        gelu_out, gelu_slope = gelu_both(hidden)
+        active_all = gelu_out.astype(jnp.bfloat16)
+        down_part = lax.psum_scatter(
+            jnp.dot(active_all, down_full, preferred_element_type=jnp.float32).astype(jnp.bfloat16),
+            "mp",
+            scatter_dimension=0,
+            tiled=True,
+        ).astype(jnp.float32)
+        result = middle + (down_part + down_shift)
+        back_row_piece = lax.all_gather(cot_low, "mp", axis=0, tiled=True)
+        grad_active = jnp.einsum(
+            "rd,fd->rf", back_row_piece, down_full, preferred_element_type=jnp.float32
+        )
+        back_gelu_out, back_gelu_slope = gelu_both(hidden)
+        grad_hidden = (grad_active * back_gelu_slope).astype(jnp.bfloat16)
+        grad_normed_two = lax.psum_scatter(
+            jnp.einsum(
+                "rf,df->rd", grad_hidden, up_full, preferred_element_type=jnp.float32
+            ).astype(jnp.bfloat16),
+            "mp",
+            scatter_dimension=0,
+            tiled=True,
+        ).astype(jnp.float32)
+        grad_down = jnp.einsum(
+            "rf,rd->fd", active_all, back_row_piece, preferred_element_type=jnp.float32
+        )
+        grad_up = jnp.einsum(
+            "rd,rf->df", row_piece, grad_hidden, preferred_element_type=jnp.float32
+        )
+        up_piece = jnp.sum(grad_hidden.astype(jnp.float32), axis=0)
+        grad_up_shift = lax.dynamic_update_slice_in_dim(
+            jnp.zeros((FF,), jnp.float32), up_piece, up_start, 0
+        )
+        grad_norm_two, grad_gain_two, grad_shift_two = norm_back_all(
+            grad_normed_two, scaled_two, inv_two, gain_two
+        )
+        grad_middle = cot_float + grad_norm_two
+        grad_branch = grad_middle.astype(jnp.bfloat16)
+        grad_out_shift = jnp.sum(grad_branch.astype(jnp.float32), axis=0)
+        grad_out_proj = jnp.einsum(
+            "rd,re->de", attended_low, grad_branch, preferred_element_type=jnp.float32
+        )
+        grad_attended = jnp.einsum(
+            "re,de->rd", grad_branch, out_full, preferred_element_type=jnp.float32
+        ).astype(jnp.bfloat16)
+        grad_query, grad_kv = attention_backward(
+            queries, keys_low, values_low, grad_attended, attended, log_total, row_first
+        )
+        grad_query_low = grad_query.astype(jnp.bfloat16)
+        grad_kv_low = grad_kv.astype(jnp.bfloat16)
+        grad_mixed = jnp.concatenate([grad_query_low, grad_kv_low[:, : D + fresh_cols]], axis=1)
+        grad_query_shift = jnp.sum(grad_query_low.astype(jnp.float32), axis=0)
+        grad_value_shift = jnp.sum(grad_kv_low[:, D : D + fresh_cols].astype(jnp.float32), axis=0)
+        grad_qkv = jnp.einsum(
+            "rd,rc->dc", normed_low, grad_mixed, preferred_element_type=jnp.float32
+        )
+        grad_normed = jnp.einsum(
+            "rc,dc->rd", grad_mixed, qkv_full, preferred_element_type=jnp.float32
+        )
+        grad_norm_one, grad_gain_one, grad_shift_one = norm_back_all(
+            grad_normed, scaled_one, inv_one, gain_one
+        )
+        grad_input = grad_middle + grad_norm_one
+        local_grads = (
+            grad_gain_one,
+            grad_shift_one,
+            grad_qkv,
+            grad_query_shift,
+            grad_value_shift,
+            grad_out_proj,
+            grad_out_shift,
+            grad_gain_two,
+            grad_shift_two,
+            grad_up,
+            grad_up_shift,
+            grad_down,
+            jnp.sum(cot_float, axis=0),
+        )
+        result, grad_input, grad_first, local_grads = (
+            result.astype(jnp.bfloat16),
+            grad_input.astype(jnp.bfloat16),
+            grad_kv_low[:, D + fresh_cols :],
+            local_grads,
+        )
+        outputs.append(result)
+        grad_inputs.append(grad_input)
+        grad_firsts.append(grad_first)
+        local_grads = reduce_grads(local_grads)
+        summed = local_grads if summed is None else jax.tree.map(jnp.add, summed, local_grads)
+    return (
+        jnp.stack(outputs),
+        jnp.stack(grad_inputs),
+        jnp.stack(grad_firsts),
+        summed[0],
+        summed[1],
+        summed[2],
+        summed[3],
+        summed[4],
+        summed[5],
+        summed[6],
+        summed[7],
+        summed[8],
+        summed[9],
+        summed[10],
+        summed[11],
+        summed[12],
+    )
+
+
 def solution(mesh):
-    plan = Plan(mesh)
+    whole_sequences = mesh.shape["mp"] == MICRO
+    body = functools.partial(shards, Plan(mesh)) if whole_sequences else general_shards
     line = P(("dp", "mp"))
     rows = P(None, ("dp", "mp"), None)
     block = P("dp", "mp")
     grads = (line, line, block, line, line, block, line, line, line, block, line, P("mp", "dp"), line)
     return jax.shard_map(
-        functools.partial(shards, plan),
+        body,
         mesh=mesh,
         in_specs=(rows, rows, rows) + grads,
         out_specs=(rows, rows, rows) + grads,

time: 170 us -> 168 us (0.988); the launches traced: 168 us -> 167 us
  no operation moved by 1% of the time
where the time goes in v7:
time: 168 us; the launch traced here: 167 us
  Pallas kernels  167 us (99%)
    pallas_call x1, Pallas kernels, step(): pl.pallas_call(functools.partial(step_kernel, plan, len(ins)), name='step...  163 us
    pallas_call x1, Pallas kernels, unpack(): pl.pallas_call(functools.partial(unpack_kernel, plan, widths), name='unpa...  3.98 us

profile of v7, /device:TPU:1, one launch (start us, length us, event | category | flops | bytes accessed | tf_op | source)
XLA Modules:
  0.0 167.4 jit_solution(3915768411228826584)
XLA Ops:
  0.7 162.6 %step.1 = (bf16[4,128,768]{2,1,0:T(8,128)(2,1)}, bf16[4,128,768]{2,1,0:T(8,128)(2,1)}, bf16[4,128,384]{2,1,0:T(8,128)(2,1)}, f32[96,512]{1,0:T(8,128)}, f32[8,51...) custom-call(s32[8,768]{1,0:T(8,128)} %constant.4.clone.refs_0_, ...), custom_call_target="tpu_custom_call" | custom-call | tf_op jit(solution)/shard_map/step/pallas_call | solution.py:1038
  163.2 4.0 %unpack.1 = (bf16[4,128,768]{2,1,0:T(8,128)(2,1)}, bf16[4,128,768]{2,1,0:T(8,128)(2,1)}, bf16[4,128,384]{2,1,0:T(8,128)(2,1)}, f32[24]{0:T(128)}, f32[24]{0:T(12...) custom-call(bf16[4,128,768]{2,1,0:T(8,128)(2,1)} %get-tuple-element., ...), custom_call_target="tpu_custom_call" | custom-call | tf_op jit(solution)/shard_map/unpack/pallas_call | solution.py:1103

commit v8 on v7

--- a/solution.py
+++ b/solution.py
@@ -30,6 +30,8 @@
 V_BIAS, UP_BIAS = 3, 7
 G1, B1, QB, OB, G2, B2, DB = WIDE
 N_VEC = 9
+LANES = 32
+UP_ROWS = (UP_BIAS, N_VEC, N_VEC + 1)
 
 
 class Plan:
@@ -49,6 +51,7 @@
         self.half = self.n_mp // 2
         self.per_seq = SEQ // (SEQ // MICRO)
         self.n_seq = self.n_mp // MICRO
+        assert self.qkv + LANES <= self.qw and D // self.n <= LANES and FF // self.n <= 3 * LANES
         assert self.parts * self.out == self.cols and self.rows % (8 * self.parts) == 0 and self.vec_rows <= 8
         self.bits = self.n_z.bit_length() - 1
         assert self.n_seq * MICRO == self.n_mp and self.n_z == 1 << self.bits and self.bits > 0
@@ -547,17 +550,17 @@
         gq, go, gu, gd, x3, f3, y3, out3,
         q_other, q_ring, q_last, s_other, s_ring, s_last, o_other, o_ring, o_last, u_other, u_ring, u_last,
         d_other, d_ring, d_last,
-        wq, wo, sv, vec, ub, hlt, qkv, otb, lse, mid, h2, h2t, yt,
+        wq, wo, sv, tail, vec, ub, hlt, qkv, otb, lse, mid, h2, h2t, yt,
         big, acc, act, slope, du, dv, dk, dqt, sums, ubg,
-    ) = refs[n_in + 8 : n_in + 8 + 46]
-    sems = refs[n_in + 8 + 46 :]
+    ) = refs[n_in + 8 : n_in + 8 + 47]
+    sems = refs[n_in + 8 + 47 :]
     dx3, df3 = y3, f3
     R, C, n_mp, n_dp, n_z = plan.rows, plan.cols, plan.n_mp, plan.n_dp, plan.n_z
     step = 64
     part = R // plan.parts
     ex = Exchange(plan)
     i, z, c = ex.i, ex.z, ex.c
-    Q = Gather(ex, gq, sems[0:6])
+    Q = Gather(ex, gq, sems[0:6], slice(0, R))
     O = Gather(ex, go, sems[6:12])
     U1 = Gather(ex, gu, sems[12:18], plan.row_half(0, R))
     U2 = Gather(ex, gu, sems[18:24], plan.row_half(1, R))
@@ -578,12 +581,15 @@
 
     all_here = ex.greet()
     gq[i, z, c, 0:R, 0 : plan.qkv] = w_qkv[...]
-    sv[0, 0:8, :] = jnp.zeros((8, plan.qw), F32)
-    for r in range(plan.vec_rows):
-        pieces = [small[v][...] for v in range(r * plan.spr, min((r + 1) * plan.spr, N_VEC))]
-        for k, piece in enumerate(pieces):
-            sv[0, r : r + 1, k * 128 : k * 128 + piece.shape[0]] = piece.astype(F32)[None]
-    gq[i, z, c, R:, :] = sv[0, 0:8, :].astype(BF)
+    sv[0, 0:16, 0:128] = jnp.zeros((16, 128), F32)
+    sv[1, 0:1, 0 : 3 * LANES] = jnp.zeros((1, 3 * LANES), F32)
+    sv[1, 0:1, 0 : small[UP_BIAS].shape[0]] = small[UP_BIAS][...].astype(F32)[None]
+    for v in range(N_VEC):
+        if v != UP_BIAS:
+            sv[0, v : v + 1, 0 : small[v].shape[0]] = small[v][...].astype(F32)[None]
+    for k, r in enumerate(UP_ROWS):
+        sv[0, r : r + 1, 0:LANES] = sv[1, 0:1, k * LANES : (k + 1) * LANES]
+    gq[i, z, c, 0:16, plan.qw - LANES :] = sv[0, 0:16, 0:LANES].astype(BF)
     def rows_of(ref3, at, step):
         part = SEQ // MICRO
         return ref3.at[at // (part // step), pl.ds(pl.multiple_of((at % (part // step)) * step, step), step)]
@@ -602,6 +608,7 @@
     gd[i, z, c] = w_down[...]
     Q.spread()
     Q.column()
+    W.circle()
     U1.start()
     U2.start()
     W.begin(0)
@@ -617,7 +624,6 @@
     XF.start()
     U2.spread()
     O.start()
-    W.circle()
     W.spread(0)
     O.spread()
     U1.column()
@@ -642,21 +648,24 @@
         for d in range(n_dp):
             rows = slice(d * R, (d + 1) * R)
             wq[rows, j * plan.qkv : (j + 1) * plan.qkv] = gq[j, d // 2, d % 2, 0:R, 0 : plan.qkv]
-    for r in range(plan.vec_rows):
-        for j in range(n_mp):
-            for d in range(n_dp):
-                at = j * n_dp + d
-                sv[r, at : at + 1, :] = gq[j, d // 2, d % 2, R + r : R + r + 1, :].astype(F32)
-
-    def expand(v, e, owner):
-        got = dot(sv[v // plan.spr, :, lanes(v)].astype(BF), e)
+    for j in range(n_mp):
+        for d in range(n_dp):
+            tail[j * n_dp + d] = gq[j, d // 2, d % 2, 0:16, plan.qw - 128 :].astype(F32)
+    skip = 128 - LANES
+    shifted = lambda t, width, back: (
+        lax.broadcasted_iota(jnp.int32, (128, width), 0) - skip == tab[t : t + 1, :width] - back
+    ) & (lax.broadcasted_iota(jnp.int32, (128, width), 0) >= skip)
+
+    def expand(r, e, owner):
+        got = dot(tail[:, r, :].astype(BF), e.astype(BF))
         return jnp.sum(jnp.where(owner == rowdev, got, 0.0), axis=0, keepdims=True)
 
     for v in WIDE:
-        vec[v : v + 1, :] = expand(v, e24, tab[1:2, :])
-    vec[V_BIAS : V_BIAS + 1, :] = expand(V_BIAS, onehot(2, D), tab[3:4, :])
+        vec[v : v + 1, :] = expand(v, shifted(0, D, 0), tab[1:2, :])
+    vec[V_BIAS : V_BIAS + 1, :] = expand(V_BIAS, shifted(2, D, 0), tab[3:4, :])
     for j in range(n_mp):
-        ub[j : j + 1, :] = expand(UP_BIAS, e96, tab[5:6, :C] + j * n_dp)
+        owner = tab[5:6, :C] + j * n_dp
+        ub[j : j + 1, :] = sum(expand(r, shifted(4, C, k * LANES), owner) for k, r in enumerate(UP_ROWS))
 
     def first_norm(at, rows):
         rows_of(out3, at, step)[...] = (acc[rows, :] * row(G1) + row(B1)).astype(BF)
@@ -1056,7 +1065,7 @@
             vm(tok.shape, BF),
             *sums(R, plan.qw), *sums(8, plan.qw), *sums(R // plan.parts, C), *sums(R, C), *ring_last(R, C),
             vm((D, QKV), BF), vm((D, D), BF),
-            vm((plan.vec_rows, n, plan.qw), F32), vm((16, D), F32), vm((max(8, n_mp), C), F32),
+            vm((plan.vec_rows, n, plan.qw), F32), vm((n, 16, 128), F32), vm((16, D), F32), vm((max(8, n_mp), C), F32),
             tall(BF), vm((SEQ, 3 * D), BF), tall(BF),
             vm((HEADS // 2, 8, SEQ), F32),
             wide(F32), wide(BF), tall(BF), tall(BF),

time: 168 us -> 164 us (0.976)
  Pallas kernels: 167 us -> 162 us
    pallas_call x1, Pallas kernels: 163 us -> 158 us  [step(): pl.pallas_call(functools.partial(step_kernel, plan, len(ins)), name='step...]
where the time goes in v8:
time: 164 us; the launch traced here: 163 us
  Pallas kernels  162 us (99%)
    pallas_call x1, Pallas kernels, step(): pl.pallas_call(functools.partial(step_kernel, plan, len(ins)), name='step...  158 us
    pallas_call x1, Pallas kernels, unpack(): pl.pallas_call(functools.partial(unpack_kernel, plan, widths), name='unpa...  3.98 us

profile of v8, /device:TPU:1, one launch (start us, length us, event | category | flops | bytes accessed | tf_op | source)
XLA Modules:
  0.0 163.1 jit_solution(12487369694904840291)
XLA Ops:
  0.7 158.3 %step.1 = (bf16[4,128,768]{2,1,0:T(8,128)(2,1)}, bf16[4,128,768]{2,1,0:T(8,128)(2,1)}, bf16[4,128,384]{2,1,0:T(8,128)(2,1)}, f32[96,512]{1,0:T(8,128)}, f32[8,51...) custom-call(s32[8,768]{1,0:T(8,128)} %constant.4.clone.refs_0_, ...), custom_call_target="tpu_custom_call" | custom-call | tf_op jit(solution)/shard_map/step/pallas_call | solution.py:1047
  159.0 4.0 %unpack.1 = (bf16[4,128,768]{2,1,0:T(8,128)(2,1)}, bf16[4,128,768]{2,1,0:T(8,128)(2,1)}, bf16[4,128,384]{2,1,0:T(8,128)(2,1)}, f32[24]{0:T(128)}, f32[24]{0:T(12...) custom-call(bf16[4,128,768]{2,1,0:T(8,128)(2,1)} %get-tuple-element., ...), custom_call_target="tpu_custom_call" | custom-call | tf_op jit(solution)/shard_map/unpack/pallas_call | solution.py:1112

commit v9 on v8

--- a/solution.py
+++ b/solution.py
@@ -771,7 +771,7 @@
 
             @pl.when(q == s)
             def _():
-                if s == n_mp - 2:
+                if s == 1:
                     W.column(plan.half)
                     U1.hop(plan.half)
                     U2.hop(plan.half)

time: 164 us -> 163 us (level)
  no operation moved by 1% of the time
where the time goes in v9:
time: 163 us; the launch traced here: 162 us
  Pallas kernels  161 us (99%)
    pallas_call x1, Pallas kernels, step(): pl.pallas_call(functools.partial(step_kernel, plan, len(ins)), name='step...  157 us
    pallas_call x1, Pallas kernels, unpack(): pl.pallas_call(functools.partial(unpack_kernel, plan, widths), name='unpa...  3.98 us

profile of v9, /device:TPU:1, one launch (start us, length us, event | category | flops | bytes accessed | tf_op | source)
XLA Modules:
  0.0 162.1 jit_solution(6369035625402827852)
XLA Ops:
  0.7 157.3 %step.1 = (bf16[4,128,768]{2,1,0:T(8,128)(2,1)}, bf16[4,128,768]{2,1,0:T(8,128)(2,1)}, bf16[4,128,384]{2,1,0:T(8,128)(2,1)}, f32[96,512]{1,0:T(8,128)}, f32[8,51...) custom-call(s32[8,768]{1,0:T(8,128)} %constant.4.clone.refs_0_, ...), custom_call_target="tpu_custom_call" | custom-call | tf_op jit(solution)/shard_map/step/pallas_call | solution.py:1047
  157.9 4.0 %unpack.1 = (bf16[4,128,768]{2,1,0:T(8,128)(2,1)}, bf16[4,128,768]{2,1,0:T(8,128)(2,1)}, bf16[4,128,384]{2,1,0:T(8,128)(2,1)}, f32[24]{0:T(128)}, f32[24]{0:T(12...) custom-call(bf16[4,128,768]{2,1,0:T(8,128)(2,1)} %get-tuple-element., ...), custom_call_target="tpu_custom_call" | custom-call | tf_op jit(solution)/shard_map/unpack/pallas_call | solution.py:1112

commit v10 on v9

--- a/solution.py
+++ b/solution.py
@@ -609,6 +609,7 @@
     Q.spread()
     Q.column()
     W.circle()
+    O.start()
     U1.start()
     U2.start()
     W.begin(0)
@@ -623,7 +624,6 @@
     U1.spread()
     XF.start()
     U2.spread()
-    O.start()
     W.spread(0)
     O.spread()
     U1.column()
@@ -721,10 +721,10 @@
             for d in range(1, plan.half):
                 U1.hop(d)
                 U2.hop(d)
+            XY.start()
             for offset in near:
                 if offset:
                     W.spread(offset)
-            XY.start()
 
         @pl.when(t == 3)
         def _():
@@ -930,6 +930,9 @@
     RD.along(order[-3])
     acc[...] = dot_nt(qkv[:, 0:QKV], wq[...])
     RD.along(order[-2])
+    RQ.far()
+    RQ.free(0)
+    RQ.free(1)
 
     def first_back(at, rows):
         n1, inv = norm_stats(rows_of(x3, at, step)[...].astype(F32))
@@ -943,9 +946,6 @@
         sums[V_BIAS : V_BIAS + 1, 0:VFRESH] += total(qkv[rows, 2 * D : QKV].astype(F32))
 
     blocks(step, first_back)
-    RQ.far()
-    RQ.free(0)
-    RQ.free(1)
 
     def collect(g, e, owner):
         return dot_nt(jnp.where(owner == rowdev, g, 0.0).astype(BF), e)

time: 163 us -> 163 us (level)
  no operation moved by 1% of the time
where the time goes in v10:
time: 163 us; the launch traced here: 162 us
  Pallas kernels  162 us (99%)
    pallas_call x1, Pallas kernels, step(): pl.pallas_call(functools.partial(step_kernel, plan, len(ins)), name='step...  158 us
    pallas_call x1, Pallas kernels, unpack(): pl.pallas_call(functools.partial(unpack_kernel, plan, widths), name='unpa...  3.98 us

profile of v10, /device:TPU:1, one launch (start us, length us, event | category | flops | bytes accessed | tf_op | source)
XLA Modules:
  0.0 162.3 jit_solution(12940576304551569377)
XLA Ops:
  0.7 157.5 %step.1 = (bf16[4,128,768]{2,1,0:T(8,128)(2,1)}, bf16[4,128,768]{2,1,0:T(8,128)(2,1)}, bf16[4,128,384]{2,1,0:T(8,128)(2,1)}, f32[96,512]{1,0:T(8,128)}, f32[8,51...) custom-call(s32[8,768]{1,0:T(8,128)} %constant.4.clone.refs_0_, ...), custom_call_target="tpu_custom_call" | custom-call | tf_op jit(solution)/shard_map/step/pallas_call | solution.py:1047
  158.2 4.0 %unpack.1 = (bf16[4,128,768]{2,1,0:T(8,128)(2,1)}, bf16[4,128,768]{2,1,0:T(8,128)(2,1)}, bf16[4,128,384]{2,1,0:T(8,128)(2,1)}, f32[24]{0:T(128)}, f32[24]{0:T(12...) custom-call(bf16[4,128,768]{2,1,0:T(8,128)(2,1)} %get-tuple-element., ...), custom_call_target="tpu_custom_call" | custom-call | tf_op jit(solution)/shard_map/unpack/pallas_call | solution.py:1112
